TPU v7x, 32 devices: a whole 2x2x4 slice. The times are simulated.
32 devices in a mesh: kgrp: 4 (over x, core), row: 4 (over z), col: 2 (over y).
Axes of the slice: x: 2, y: 2, z: 4, core: 2. Of those that a mesh axis runs over, the one named last changes fastest.
Arguments:
- occ_orbitals: bfloat16 [8, 1024, 2, 512], P('kgrp', ('row', 'col')), may hold values from -5 to 5
- emp_orbitals: bfloat16 [8, 1024, 2, 512], P('kgrp', ('row', 'col')), may hold values from -5 to 5
- energies: float32 [2, 8, 512], replicated, may hold values from 0.05 to 1.5
- band_order: int32 [2, 8, 512], replicated, may hold values from 0 to 511, each once within a row
- imag_times: float32 [2], replicated, may hold values from 0.3 to 3
- kq_map: int32 [2, 8], replicated, may hold values from 0 to 7, each once within a row
- slot_kpoint: int32 [8], replicated, may hold values from 0 to 7, each once
Outputs:
- suscept: float32 [2, 2, 2, 512, 2, 1024], P(None, None, 'col', 'kgrp', None, 'row')
Inputs may be any that keep to these rules, and one draw needn't show every extreme that they name: `kq_map`: each row is a permutation of the k-point ids. `slot_kpoint`: a permutation of the k-point ids. `band_order`: each row over the last dimension is a permutation of the ranks.
All inputs are finite; a program needn't handle non-finite values.
Results may differ from a plain program's by a relative error of at most 0.0003.
Values may be sent and summed in bfloat16 or wider, within the bound.
No kernel may reach another device: no remote copies, remote signals or barrier semaphores. Data moves between devices by JAX's collectives and lax.ppermute only.
A program may use at most 64 MiB of HBM per device.

v0:
```python
import functools

import jax
import jax.numpy as jnp
from jax import lax
from jax.experimental import pallas as pl
from jax.experimental.pallas import tpu as pltpu
from jax.sharding import PartitionSpec as P


def table_row(lookup_table, wanted):
    positions = jnp.arange(lookup_table.shape[0], dtype=jnp.int32)
    chosen = positions[:, None] == wanted
    return jnp.sum(jnp.where(chosen, lookup_table, jnp.zeros_like(lookup_table)), axis=0)


def band_weights(levels, band_rank, imag_times):
    picked = jnp.take(levels, band_rank, axis=0)
    return jnp.exp(-picked[None, :] * imag_times[:, None])


def green_tile(row_panel, col_panel, weights):
    times_count = weights.shape[0]
    scaled = (row_panel[None] * weights[:, None, None, :]).astype(jnp.bfloat16)
    scaled = scaled.reshape(times_count, row_panel.shape[0], -1)
    turned = jnp.concatenate([-col_panel[:, 1], col_panel[:, 0]], axis=1)
    stacked = jnp.concatenate([col_panel.reshape(col_panel.shape[0], -1), turned], axis=0)
    result = lax.dot_general(
        stacked, scaled, (((1,), (2,)), ((), ())), preferred_element_type=jnp.float32
    )
    return result.reshape(2, col_panel.shape[0], times_count, row_panel.shape[0])


def pair_term(held_tile, moved_tile, factor):
    real_part = held_tile[0] * moved_tile[0] + held_tile[1] * moved_tile[1]
    imag_part = held_tile[1] * moved_tile[0] - held_tile[0] * moved_tile[1]
    return factor * jnp.stack([real_part, imag_part])


def source_slots(kq_map, slot_kpoint, own_slots):
    positions = jnp.arange(slot_kpoint.shape[0], dtype=jnp.int32)
    own_kpoint = jnp.sum(
        jnp.where(own_slots[:, None] == positions[None, :], slot_kpoint[None, :], 0), axis=1
    )
    target = jnp.sum(
        jnp.where(own_kpoint[None, :, None] == positions[None, None, :], kq_map[:, None, :], 0),
        axis=2,
    )
    return jnp.sum(
        jnp.where(target[:, :, None] == slot_kpoint[None, None, :], positions[None, None, :], 0),
        axis=2,
    )


def summed_over_groups(occ_orbitals, emp_orbitals, energies, band_order, imag_times, kq_map, slot_kpoint):
    groups = lax.axis_size("kgrp")
    per_group = occ_orbitals.shape[0]
    kpoints = groups * per_group
    transfers = kq_map.shape[0]
    factor = -1.0 / kpoints
    own_slots = lax.axis_index("kgrp") * per_group + jnp.arange(per_group, dtype=jnp.int32)
    sources = source_slots(kq_map, slot_kpoint, own_slots)
    flat_sources = sources.reshape(-1)
    initial = jnp.zeros((flat_sources.shape[0],) + emp_orbitals.shape[1:], jnp.float32)
    block_part = lax.all_gather(emp_orbitals, "kgrp", axis=0, tiled=True)
    numbered = block_part.shape[0]
    matches = (flat_sources[:, None] == jnp.arange(numbered, dtype=jnp.int32)[None, :]).astype(
        jnp.bfloat16
    )
    update = jnp.dot(matches, block_part.reshape(numbered, -1), preferred_element_type=jnp.float32)
    fetched = update.reshape(initial.shape).astype(jnp.bfloat16)
    occ_rows, emp_rows = (
        lax.all_gather(occ_orbitals, "col", axis=1, tiled=True),
        lax.all_gather(fetched, "col", axis=1, tiled=True),
    )
    occ_cols, emp_cols = (
        lax.all_gather(occ_orbitals, "row", axis=1, tiled=True),
        lax.all_gather(fetched, "row", axis=1, tiled=True),
    )
    tiles = []
    for position in range(per_group):
        weights = band_weights(
            table_row(energies[0], own_slots[position]),
            table_row(band_order[0], own_slots[position]),
            imag_times,
        )
        tiles.append(green_tile(occ_rows[position], occ_cols[position], weights))

    def transfer_terms(transfer):
        partial_value = None
        for position in range(per_group):
            source = sources[transfer, position]
            weights = band_weights(
                table_row(energies[1], source), table_row(band_order[1], source), imag_times
            )
            moved_index = transfer * per_group + position
            moved_tile = green_tile(emp_rows[moved_index], emp_cols[moved_index], weights)
            addition = pair_term(tiles[position], moved_tile, factor)
            partial_value = addition if partial_value is None else partial_value + addition
        return partial_value

    terms_all = jnp.stack([transfer_terms(transfer) for transfer in range(transfers)], axis=1)
    summed = lax.psum_scatter(terms_all, "kgrp", scatter_dimension=2, tiled=True)
    return summed[:, :, None]


LANES = 128
HBM = pl.BlockSpec(memory_space=pltpu.HBM)
VMEM = pl.BlockSpec(memory_space=pltpu.VMEM)
SMEM = pl.BlockSpec(memory_space=pltpu.SMEM)
LIMIT = pltpu.CompilerParams(vmem_limit_bytes=24 * 2**20)
AXES = ("kgrp", "row", "col")


def place():
    group = lax.axis_index("kgrp")
    return lax.div(group, 2), lax.rem(group, 2), lax.axis_index("row"), lax.axis_index("col")


def prep_kernel(levels_ref, rank_ref, times_ref, map_ref, kpoint_ref, weight_ref, pair_ref, slot_of):
    bands = levels_ref.shape[2]
    times = weight_ref.shape[1]
    for kind in range(2):
        for start in range(0, bands, LANES):
            rank = rank_ref[kind, :, start : start + LANES]
            low, high = rank & (LANES - 1), rank // LANES
            picked = jnp.zeros(rank.shape, jnp.float32)
            for piece in range(bands // LANES):
                table = levels_ref[kind, :, piece * LANES : (piece + 1) * LANES]
                found = jnp.take_along_axis(table, low, axis=1)
                picked = jnp.where(high == piece, found, picked)
            for t in range(times):
                value = jnp.exp(-picked * times_ref[t])
                weight_ref[kind, t, :, start : start + LANES] = value
                weight_ref[kind, t, :, bands + start : bands + start + LANES] = value
    transfers, kpoints = map_ref.shape
    per_group = kpoints // lax.axis_size("kgrp")
    group = lax.axis_index("kgrp")

    def relative(slot):
        return (lax.div(slot, per_group) ^ group) * per_group + lax.rem(slot, per_group)

    for slot in range(kpoints):
        slot_of[kpoint_ref[slot]] = slot
    for transfer in range(transfers):
        for slot in range(kpoints):
            source = slot_of[map_ref[transfer, kpoint_ref[slot]]]
            pair_ref[transfer, relative(source)] = relative(jnp.int32(slot))


def flatten_occ_kernel(occ_ref, occ_out):
    for slot in range(occ_out.shape[0]):
        occ_out[slot] = occ_ref[slot].reshape(occ_out.shape[1:])


def flatten_emp_kernel(emp_ref, occ_flat_ref, emp_out, both_out):
    slots = emp_out.shape[0]
    for slot in range(slots):
        panel = emp_ref[slot].reshape(emp_out.shape[1:])
        emp_out[slot] = panel
        both_out[slot] = occ_flat_ref[slot]
        both_out[slots + slot] = panel


def choose():
    x, h, z, _ = place()
    half = lax.axis_size("row") // 2
    near = x == lax.div(z, half)
    inner = (z == half - 1) | (z == half)
    owns = h == lax.rem(z, 2)
    first = h == lax.div(z, half)
    swapped = jnp.where(inner, 1, 2)
    far1 = jnp.where(inner, 3, 5)
    far2 = jnp.where(inner, 4, 6)
    keep = jnp.where(near, jnp.where(owns, 0, swapped), jnp.where(first, far1, far2))
    send = jnp.where(near, jnp.where(owns, swapped, 0), jnp.where(first, far2, far1))
    return keep, send


def part(ref, kind, slots):
    return ref if ref.shape[0] == slots else ref.at[pl.ds(kind * slots, slots)]


def pack_kernel(kind, cases, *refs):
    direct, crossed = refs[:cases], refs[cases : 2 * cases]
    send_ref, sems = refs[2 * cases :]
    _, send = choose()
    slots = send_ref.shape[1]
    for case in range(cases):

        @pl.when(send == case)
        def _():
            for side, source in enumerate((direct[case], crossed[case])):
                pltpu.make_async_copy(part(source, kind, slots), send_ref.at[side], sems.at[side]).start()

    for side in range(2):
        pltpu.make_async_copy(send_ref.at[side], send_ref.at[side], sems.at[side]).wait()


def pack(kind, direct, crossed, shape):
    return pl.pallas_call(
        functools.partial(pack_kernel, kind, len(direct)),
        out_shape=jax.ShapeDtypeStruct((2,) + shape, jnp.bfloat16),
        in_specs=[HBM] * (2 * len(direct)),
        out_specs=VMEM,
        scratch_shapes=[pltpu.SemaphoreType.DMA((2,))],
        compiler_params=LIMIT,
    )(*direct, *crossed)


def load_panels(kind, groups, rows, direct, crossed, recv, last, row_buf, col_buf, sems):
    slots = col_buf.shape[1]
    keep, _ = choose()

    def fetch(source, k):
        pltpu.make_async_copy(part(source, kind, slots), col_buf.at[k], sems.at[k, 0]).start()

    for k in groups:
        if k & 1:
            inside = recv.at[k >> 1]
            if last is None or k == 1:
                fetch(inside, k)
            else:
                pl.when(keep == 6)(functools.partial(fetch, last, k))
                pl.when(keep != 6)(functools.partial(fetch, inside, k))
        else:
            for case, source in enumerate((direct, crossed)[k >> 1]):
                pl.when(keep == case)(functools.partial(fetch, source, k))
        for half in range(2):
            panel = part(rows[half * 4 + k], kind, slots)
            pltpu.make_async_copy(panel, row_buf.at[half, k], sems.at[k, 1 + half]).start()

    def wait(k):
        for index, target in enumerate((col_buf.at[k], row_buf.at[0, k], row_buf.at[1, k])):
            pltpu.make_async_copy(target, target, sems.at[k, index]).wait()

    return wait


def tile(kind, k, i, half, stacked, row_buf, weight_ref):
    per_group = row_buf.shape[2]
    slot = (lax.axis_index("kgrp") ^ k) * per_group + i
    panel = row_buf[half, k, i].astype(jnp.float32)
    scaled = [
        (panel * weight_ref[kind, t, pl.ds(slot, 1), :]).astype(jnp.bfloat16)
        for t in range(weight_ref.shape[1])
    ]
    return lax.dot_general(
        stacked,
        jnp.concatenate(scaled, axis=0),
        (((1,), (1,)), ((), ())),
        preferred_element_type=jnp.float32,
    )


def stack_columns(columns):
    width = columns.shape[1] // 2
    turned = jnp.concatenate([-columns[:, width:], columns[:, :width]], axis=1)
    return jnp.concatenate([columns, turned], axis=0)


def occ_kernel(cases, *refs):
    rows, direct, crossed = refs[:8], refs[8 : 8 + cases], refs[8 + cases : 8 + 2 * cases]
    recv, weight_ref, out_ref, row_buf, col_buf, sems = refs[8 + 2 * cases :]
    wait = load_panels(0, range(4), rows, direct, crossed, recv, None, row_buf, col_buf, sems)
    per_group = col_buf.shape[1]
    for k in range(4):
        wait(k)
        for i in range(per_group):
            stacked = stack_columns(col_buf[k, i])
            for half in range(2):
                out_ref[k * per_group + i, half] = tile(0, k, i, half, stacked, row_buf, weight_ref)


def emp_direct_kernel(cases, *refs):
    rows, direct = refs[:8], refs[8 : 8 + cases]
    recv, weight_ref, out_ref, row_buf, col_buf, sems = refs[8 + cases :]
    wait = load_panels(1, (0, 1), rows, direct, None, recv, None, row_buf, col_buf, sems)
    per_group = col_buf.shape[1]
    for k in (0, 1):
        wait(k)
        for i in range(per_group):
            stacked = stack_columns(col_buf[k, i])
            for half in range(2):
                out_ref[k * per_group + i, half] = tile(1, k, i, half, stacked, row_buf, weight_ref)


STRIP = 16


def closing_kernel(factor, cases, *refs):
    rows, crossed = refs[:8], refs[8 : 8 + cases]
    recv, last, weight_ref, pair_ref, occ_ref, direct_ref, out_ref, row_buf, col_buf, moved, sems = refs[8 + cases :]
    wait = load_panels(1, (2, 3), rows, None, crossed, recv, last, row_buf, col_buf, sems)
    per_group, block = col_buf.shape[1], col_buf.shape[2]
    split = 2 * per_group
    transfers = pair_ref.shape[0]
    times = weight_ref.shape[1]
    y = lax.axis_index("col")
    for k in (2, 3):
        wait(k)
        for i in range(per_group):
            stacked = stack_columns(col_buf[k, i])
            for half in range(2):
                moved[k * per_group + i - split, half] = tile(1, k, i, half, stacked, row_buf, weight_ref)
    held = [[pair_ref[q, a] for a in range(2 * split)] for q in range(transfers)]
    for half in range(2):
        start = pl.multiple_of((y ^ half) * block, LANES)

        def strip(index, carry):
            real_rows = pl.ds(pl.multiple_of(index * STRIP, STRIP), STRIP)
            imag_rows = pl.ds(pl.multiple_of(index * STRIP + block, STRIP), STRIP)
            sums = [[None, None] for _ in range(transfers)]
            for a in range(2 * split):
                source = direct_ref if a < split else moved
                re = source[a % split, half, real_rows, :]
                im = source[a % split, half, imag_rows, :]
                for q in range(transfers):
                    ro = occ_ref[held[q][a], half, real_rows, :]
                    io = occ_ref[held[q][a], half, imag_rows, :]
                    for comp, piece in enumerate((ro * re + io * im, io * re - ro * im)):
                        sums[q][comp] = piece if a == 0 else sums[q][comp] + piece
            for q in range(transfers):
                for comp in range(2):
                    total = sums[q][comp] * factor
                    for t in range(times):
                        out_ref[comp, q, real_rows, t, pl.ds(start, block)] = total[:, t * block : (t + 1) * block]
            return carry

        lax.fori_loop(0, block // STRIP, strip, 0)


def output_stationary(occ_orbitals, emp_orbitals, energies, band_order, imag_times, kq_map, slot_kpoint):
    groups, rows, cols = (lax.axis_size(name) for name in AXES)
    slots, block = occ_orbitals.shape[:2]
    width = occ_orbitals.shape[2] * occ_orbitals.shape[3]
    transfers, times = kq_map.shape[0], imag_times.shape[0]
    kpoints = groups * slots
    half = rows // 2
    top = rows - 1

    def send(array, route):
        pairs = []
        for g in range(groups):
            for z in range(rows):
                for y in range(cols):
                    target = route(g // 2, g % 2, z, y)
                    if target is not None:
                        x2, h2, z2, y2 = target
                        pairs.append(((g * rows + z) * cols + y, ((2 * x2 + h2) * rows + z2) * cols + y2))
        return lax.ppermute(array, AXES, pairs)

    def inner(z):
        return z in (half - 1, half)

    def near(x, z):
        return x == z // half

    def swap(x, h, z, y):
        return x, h, z ^ 1, y

    def swap_main(x, h, z, y):
        return None if inner(z) and near(x, z) else (x, h, z ^ 1, y)

    def swap_late(x, h, z, y):
        return (x, h, z ^ 1, y) if inner(z) and near(x, z) else None

    def middle(x, h, z, y):
        return (x, h, top - z, y) if inner(z) else None

    def outward_near(x, h, z, y):
        return (x, h, z ^ 1, y) if inner(z) and near(x, z) else None

    def outward_far(x, h, z, y):
        return (x, h, z ^ 1, y) if inner(z) and not near(x, z) else None

    def flip_x(x, h, z, y):
        return 1 - x, h, z, y

    def middle_or_to_near(x, h, z, y):
        if inner(z):
            return x, h, top - z, y
        return None if near(x, z) else (1 - x, h, z, y)

    def from_near(x, h, z, y):
        if not near(x, z):
            return None
        return (x, h, top - z, y) if inner(z) else (x, h, z ^ 1, y)

    def to_far_or_outward(x, h, z, y):
        if not inner(z):
            return None
        return (1 - x, h, z, y) if near(x, z) else (x, h, z ^ 1, y)

    def to_far_outer(x, h, z, y):
        return (1 - x, h, z, y) if near(x, z) and not inner(z) else None

    def flip_y(x, h, z, y):
        return x, h, z, 1 - y

    def flip_core(x, h, z, y):
        return x, 1 - h, z, y

    flat = jax.ShapeDtypeStruct((slots, block, width), jnp.bfloat16)
    occ_flat = pl.pallas_call(
        flatten_occ_kernel,
        out_shape=flat,
        in_specs=[VMEM],
        out_specs=VMEM,
        compiler_params=LIMIT,
        name="flatten_occ",
    )(occ_orbitals)
    emp_flat, both = pl.pallas_call(
        flatten_emp_kernel,
        out_shape=[flat, jax.ShapeDtypeStruct((2 * slots, block, width), jnp.bfloat16)],
        in_specs=[VMEM] * 2,
        out_specs=[VMEM] * 2,
        compiler_params=LIMIT,
        name="flatten_emp",
    )(emp_orbitals, occ_flat)
    kinds = [occ_flat, emp_flat]

    prepare = pl.pallas_call(
        prep_kernel,
        out_shape=[
            jax.ShapeDtypeStruct((2, times, kpoints, width), jnp.float32),
            jax.ShapeDtypeStruct((transfers, kpoints), jnp.int32),
        ],
        in_specs=[VMEM, VMEM, SMEM, SMEM, SMEM],
        out_specs=[VMEM, SMEM],
        scratch_shapes=[pltpu.SMEM((kpoints,), jnp.int32)],
        compiler_params=LIMIT,
        name="prep",
    )
    weights, pairs = prepare(energies, band_order, imag_times, kq_map, slot_kpoint)

    s1 = [send(kinds[0], swap), send(kinds[1], swap_main)]
    late = send(kinds[1], swap_late)
    b = [send(kinds[i], middle) for i in range(2)]
    crossed = send(both, flip_x)
    turned = send(both, flip_y)
    sibling = send(both, flip_core)
    d = [send(s1[i], middle_or_to_near) for i in range(2)]
    en = [send(b[i], outward_near) for i in range(2)]
    e = [send(b[i], outward_far) for i in range(2)]
    bx = send(crossed, from_near)
    turned_crossed = send(crossed, flip_y)
    crossed_sibling = send(crossed, flip_core)
    turned_sibling = send(turned, flip_core)
    turned_crossed_sibling = send(turned_crossed, flip_core)
    ex = [send(en[i], to_far_outer) for i in range(2)]
    fn = [send(d[i], outward_near) for i in range(2)]
    f = [send(d[i], to_far_or_outward) for i in range(2)]
    fx = [send(fn[i], to_far_outer) for i in range(2)]
    last = send(fx[1], flip_core)
    row_panels, direct, across, given = [], [], [], []
    for kind in range(2):
        row_panels.append([
            kinds[kind], sibling, crossed, crossed_sibling,
            turned, turned_sibling, turned_crossed, turned_crossed_sibling,
        ])
        swapped = late if kind else s1[0]
        direct.append([kinds[kind], s1[kind], swapped, b[kind], d[kind], e[kind], f[kind]])
        across.append([crossed, bx, d[kind], bx, f[kind], ex[kind], fx[kind]])
        ready = across[kind][:-1] + [ex[1] if kind else fx[0]]
        give = pack(kind, direct[kind], ready, (slots, block, width))
        given.append(send(give, flip_core))

    panel_scratch = [
        pltpu.VMEM((2, 4, slots, block, width), jnp.bfloat16),
        pltpu.VMEM((4, slots, block, width), jnp.bfloat16),
    ]
    cases = len(direct[0])
    occ_tiles = pl.pallas_call(
        functools.partial(occ_kernel, cases),
        out_shape=jax.ShapeDtypeStruct((kpoints, 2, 2 * block, times * block), jnp.float32),
        in_specs=[HBM] * (9 + 2 * cases) + [VMEM],
        out_specs=VMEM,
        scratch_shapes=panel_scratch + [pltpu.SemaphoreType.DMA((4, 3))],
        compiler_params=LIMIT,
        name="occ_tiles",
    )
    tiles = occ_tiles(*row_panels[0], *direct[0], *across[0], given[0], weights)
    half_tiles = (kpoints // 2, 2, 2 * block, times * block)
    emp_direct = pl.pallas_call(
        functools.partial(emp_direct_kernel, cases),
        out_shape=jax.ShapeDtypeStruct(half_tiles, jnp.float32),
        in_specs=[HBM] * (9 + cases) + [VMEM],
        out_specs=VMEM,
        scratch_shapes=panel_scratch + [pltpu.SemaphoreType.DMA((4, 3))],
        compiler_params=LIMIT,
        name="emp_direct",
    )
    direct_tiles = emp_direct(*row_panels[1], *direct[1], given[1], weights)
    result = pl.pallas_call(
        functools.partial(closing_kernel, -1.0 / kpoints, cases),
        out_shape=jax.ShapeDtypeStruct((2, transfers, block, times, cols * block), jnp.float32),
        in_specs=[HBM] * (10 + cases) + [VMEM, SMEM, VMEM, VMEM],
        out_specs=VMEM,
        scratch_shapes=panel_scratch + [pltpu.VMEM(half_tiles, jnp.float32), pltpu.SemaphoreType.DMA((4, 3))],
        compiler_params=LIMIT,
        name="closing",
    )(*row_panels[1], *across[1], given[1], last, weights, pairs, tiles, direct_tiles)
    return result[:, :, None]


def staged(*arguments):
    return output_stationary(*arguments)


def solution(mesh):
    in_specs = (
        P("kgrp", ("row", "col"), None, None),
        P("kgrp", ("row", "col"), None, None),
        P(),
        P(),
        P(),
        P(),
        P(),
    )
    out_specs = P(None, None, "col", "kgrp", None, "row")
    groups, rows, cols = (mesh.shape[name] for name in AXES)
    line = groups == rows == 2 * cols == 4
    body = staged if line else summed_over_groups
    return jax.shard_map(body, mesh=mesh, in_specs=in_specs, out_specs=out_specs, check_vma=False)
```

profile of v0, /device:TPU:0, one launch (start us, length us, event | category | flops | bytes accessed | tf_op | source)
XLA Modules:
  0.0 131.8 jit_solution(11306496268377370493)
XLA Ops:
  0.0 1.0 copy-done
  1.0 0.2 flatten_occ.1.occ_flat_ref.refs_0_.refs_8_
  1.2 0.0 copy-start.1
  1.2 1.0 copy-done.1
  2.2 0.2 flatten_emp.1
  2.4 5.0 %collective-permute-start.8 = (bf16[2,128,1024]{2,1,0:T(8,128)(2,1)S(1)}, bf16[2,128,1024]{2,1,0:T(8,128)(2,1)S(1)}, u32[]{:S(2)}, u32[]{:S(2)}) collective-permute-start(bf16[2,128,1024]{2,1,0:T(8,128)(2,1)S(1)} %get-tuple-element.9.refs_0_.refs_8_), channel_id=1, source_target_pairs={{0,2},{1,3},{4,6},{5,7},{6,4},{7,5},{8,10},{9,11},{12,14},{13,15},... | collective-permute-start | bytes 1572872 | tf_op jit(solution)/shard_map/ppermute | solution.py:351
  7.4 0.7 collective-permute-start.11
  8.1 1.3 collective-permute-start.16
  9.4 0.9 collective-permute-start.1
  10.3 3.6 %collective-permute-start.20 = (bf16[2,128,1024]{2,1,0:T(8,128)(2,1)S(1)}, bf16[2,128,1024]{2,1,0:T(8,128)(2,1)S(1)}, u32[]{:S(2)}, u32[]{:S(2)}) collective-permute-start(bf16[2,128,1024]{2,1,0:T(8,128)(2,1)S(1)} %flatten_occ.1.occ_flat_ref.refs_0_.refs_8_), channel_id=1, source_target_pairs={{0,2},{1,3},{2,0},{3,1},{4,6},{5,7},{6,4},{7,5},{8,10},{9,11},{10,... | collective-permute-start | bytes 1572872 | tf_op jit(solution)/shard_map/ppermute | solution.py:351
  13.9 5.7 %collective-permute-done.8.refs_1_.refs_9_ = bf16[2,128,1024]{2,1,0:T(8,128)(2,1)S(1)} collective-permute-done((bf16[2,128,1024]{2,1,0:T(8,128)(2,1)S(1)}, bf16[2,128,1024]{2,1,0:T(8,128)(2,1)S(1)}, u32[]{:S(2)}, u32[]{:S(2)}) %collective-permute-start.8) | collective-permute-done | bytes 524320 | tf_op jit(solution)/shard_map/ppermute | solution.py:351
  19.7 0.7 collective-permute-start.21
  20.4 0.0 collective-permute-done.11.refs_3_.refs_11_
  20.4 1.6 %collective-permute-start.3 = (bf16[4,128,1024]{2,1,0:T(8,128)(2,1)S(1)}, bf16[4,128,1024]{2,1,0:T(8,128)(2,1)S(1)}, u32[]{:S(2)}, u32[]{:S(2)}) collective-permute-start(bf16[4,128,1024]{2,1,0:T(8,128)(2,1)S(1)} %get-tuple-element.10), channel_id=1, source_target_pairs={{0,1},{1,0},{2,3},{3,2},{4,5},{5,4},{6,7},{7,6},{8,9},{9,8},{10,11... | collective-permute-start | bytes 3145736 | tf_op jit(solution)/shard_map/ppermute | solution.py:351
  22.0 4.5 %collective-permute-done.16.refs_2_.refs_10_ = bf16[2,128,1024]{2,1,0:T(8,128)(2,1)S(1)} collective-permute-done((bf16[2,128,1024]{2,1,0:T(8,128)(2,1)S(1)}, bf16[2,128,1024]{2,1,0:T(8,128)(2,1)S(1)}, u32[]{:S(2)}, u32[]{:S(2)}) %collective-permute-start.16) | collective-permute-done | bytes 524320 | tf_op jit(solution)/shard_map/ppermute | solution.py:351
  26.5 1.3 collective-permute-start.9
  27.8 8.5 %collective-permute-done.20.refs_1_.refs_2_.refs_9_.refs_10_ = bf16[2,128,1024]{2,1,0:T(8,128)(2,1)S(1)} collective-permute-done((bf16[2,128,1024]{2,1,0:T(8,128)(2,1)S(1)}, bf16[2,128,1024]{2,1,0:T(8,128)(2,1)S(1)}, u32[]{:S(2)}, u32[]{:S(2)}) %collective-permute-start.20) | collective-permute-done | bytes 524320 | tf_op jit(solution)/shard_map/ppermute | solution.py:351
  36.3 1.3 collective-permute-start.12
  37.6 0.0 collective-permute-done.21.refs_3_.refs_11_
  37.6 0.7 collective-permute-start.17
  38.3 7.0 %collective-permute-done.9.refs_4_.refs_9_.refs_12_.refs_10_ = bf16[2,128,1024]{2,1,0:T(8,128)(2,1)S(1)} collective-permute-done((bf16[2,128,1024]{2,1,0:T(8,128)(2,1)S(1)}, bf16[2,128,1024]{2,1,0:T(8,128)(2,1)S(1)}, u32[]{:S(2)}, u32[]{:S(2)}) %collective-permute-start.9) | collective-permute-done | bytes 524320 | tf_op jit(solution)/shard_map/ppermute | solution.py:351
  45.3 1.3 collective-permute-start.22
  46.6 0.0 collective-permute-done.1.refs_7_.refs_2_.refs_15_.refs_8_
  46.6 1.3 collective-permute-start.25
  47.9 3.7 %collective-permute-done.12 = bf16[2,128,1024]{2,1,0:T(8,128)(2,1)S(1)} collective-permute-done((bf16[2,128,1024]{2,1,0:T(8,128)(2,1)S(1)}, bf16[2,128,1024]{2,1,0:T(8,128)(2,1)S(1)}, u32[]{:S(2)}, u32[]{:S(2)}) %collective-permute-start.12) | collective-permute-done | bytes 524320 | tf_op jit(solution)/shard_map/ppermute | solution.py:351
  51.7 0.7 collective-permute-start.23
  52.4 0.7 collective-permute-start.10
  53.1 0.0 collective-permute-done.3.refs_4_
  53.1 1.5 %collective-permute-start.13 = (bf16[2,128,1024]{2,1,0:T(8,128)(2,1)S(1)}, bf16[2,128,1024]{2,1,0:T(8,128)(2,1)S(1)}, u32[]{:S(2)}, u32[]{:S(2)}) collective-permute-start(bf16[2,128,1024]{2,1,0:T(8,128)(2,1)S(1)} %collective-permute-done.12), channel_id=1, source_target_pairs={{0,16},{1,17},{8,24},{9,25},{22,6},{23,7},{30,14},{31,15}} | collective-permute-start | bytes 1572872 | tf_op jit(solution)/shard_map/ppermute | solution.py:351
  54.6 5.2 %collective-permute-done.22.refs_4_.refs_9_.refs_12_.refs_17_ = bf16[2,128,1024]{2,1,0:T(8,128)(2,1)S(1)} collective-permute-done((bf16[2,128,1024]{2,1,0:T(8,128)(2,1)S(1)}, bf16[2,128,1024]{2,1,0:T(8,128)(2,1)S(1)}, u32[]{:S(2)}, u32[]{:S(2)}) %collective-permute-start.22) | collective-permute-done | bytes 524320 | tf_op jit(solution)/shard_map/ppermute | solution.py:351
  59.7 1.3 collective-permute-start.27
  61.0 0.9 collective-permute-done.25
  62.0 3.7 %collective-permute-start.7 = (bf16[4,128,1024]{2,1,0:T(8,128)(2,1)S(1)}, bf16[4,128,1024]{2,1,0:T(8,128)(2,1)S(1)}, u32[]{:S(2)}, u32[]{:S(2)}) collective-permute-start(bf16[4,128,1024]{2,1,0:T(8,128)(2,1)S(1)} %collective-permute-done.1.refs_7_.refs_2_.refs_15_.refs_8_), channel_id=1, source_target_pairs={{0,2},{1,3},{2,4},{3,5},{8,10},{9,11},{10,12},{11,13},{20,18},{21,... | collective-permute-start | bytes 3145736 | tf_op jit(solution)/shard_map/ppermute | solution.py:351
  65.7 0.7 collective-permute-start.24
  66.4 0.0 collective-permute-done.10.refs_6_.refs_11_.refs_14_.refs_12_
  66.4 13.4 %collective-permute-start.26 = (bf16[2,128,1024]{2,1,0:T(8,128)(2,1)S(1)}, bf16[2,128,1024]{2,1,0:T(8,128)(2,1)S(1)}, u32[]{:S(2)}, u32[]{:S(2)}) collective-permute-start(bf16[2,128,1024]{2,1,0:T(8,128)(2,1)S(1)} %collective-permute-done.25), channel_id=1, source_target_pairs={{0,16},{1,17},{8,24},{9,25},{22,6},{23,7},{30,14},{31,15}} | collective-permute-start | bytes 1572872 | tf_op jit(solution)/shard_map/ppermute | solution.py:351
  79.9 0.0 collective-permute-done.13.refs_12_.refs_13_
  79.9 0.1 collective-permute-start
  80.0 0.0 collective-permute-done.27
  80.0 1.6 %collective-permute-start.5 = (bf16[4,128,1024]{2,1,0:T(8,128)(2,1)S(1)}, bf16[4,128,1024]{2,1,0:T(8,128)(2,1)S(1)}, u32[]{:S(2)}, u32[]{:S(2)}) collective-permute-start(bf16[4,128,1024]{2,1,0:T(8,128)(2,1)S(1)} %collective-permute-done.1.refs_7_.refs_2_.refs_15_.refs_8_), channel_id=1, source_target_pairs={{0,1},{1,0},{2,3},{3,2},{4,5},{5,4},{6,7},{7,6},{8,9},{9,8},{10,11... | collective-permute-start | bytes 3145736 | tf_op jit(solution)/shard_map/ppermute | solution.py:351
  81.6 0.1 collective-permute-start.2
  81.7 4.8 %collective-permute-done.26.refs_12_.refs_20_ = bf16[2,128,1024]{2,1,0:T(8,128)(2,1)S(1)} collective-permute-done((bf16[2,128,1024]{2,1,0:T(8,128)(2,1)S(1)}, bf16[2,128,1024]{2,1,0:T(8,128)(2,1)S(1)}, u32[]{:S(2)}, u32[]{:S(2)}) %collective-permute-start.26) | collective-permute-done | bytes 524320 | tf_op jit(solution)/shard_map/ppermute | solution.py:351
  86.5 4.4 %collective-permute-start.28 = (bf16[2,128,1024]{2,1,0:T(8,128)(2,1)S(1)}, bf16[2,128,1024]{2,1,0:T(8,128)(2,1)S(1)}, u32[]{:S(2)}, u32[]{:S(2)}) collective-permute-start(bf16[2,128,1024]{2,1,0:T(8,128)(2,1)S(1)} %collective-permute-done.27), channel_id=1, source_target_pairs={{0,16},{1,17},{8,24},{9,25},{22,6},{23,7},{30,14},{31,15}} | collective-permute-start | bytes 1572872 | tf_op jit(solution)/shard_map/ppermute | solution.py:351
  90.9 1.3 collective-permute-start.14
  92.2 0.2 shard_map.73
  92.4 0.0 copy-start.2
  92.4 0.0 copy-start.3
  92.4 0.0 copy-start.4
  92.4 0.0 copy-start.5
  92.5 0.0 copy-start.6
  92.5 7.9 %collective-permute-done.28.refs_13_.refs_21_ = bf16[2,128,1024]{2,1,0:T(8,128)(2,1)S(1)} collective-permute-done((bf16[2,128,1024]{2,1,0:T(8,128)(2,1)S(1)}, bf16[2,128,1024]{2,1,0:T(8,128)(2,1)S(1)}, u32[]{:S(2)}, u32[]{:S(2)}) %collective-permute-start.28) | collective-permute-done | bytes 524320 | tf_op jit(solution)/shard_map/ppermute | solution.py:351
  100.4 0.0 collective-permute-start.4
  100.4 0.1 shard_map.74
  100.5 0.6 collective-permute-start.18
  101.1 4.4 %collective-permute-done.5.refs_6_ = bf16[4,128,1024]{2,1,0:T(8,128)(2,1)S(1)} collective-permute-done((bf16[4,128,1024]{2,1,0:T(8,128)(2,1)S(1)}, bf16[4,128,1024]{2,1,0:T(8,128)(2,1)S(1)}, u32[]{:S(2)}, u32[]{:S(2)}) %collective-permute-start.5) | collective-permute-done | bytes 1048608 | tf_op jit(solution)/shard_map/ppermute | solution.py:351
  105.5 0.0 collective-permute-start.6
  105.5 0.0 collective-permute-done.14
  105.5 0.5 collective-permute-start.29
  106.0 1.3 collective-permute-start.15
  107.4 11.6 %collective-permute-done.15.refs_14_ = bf16[2,128,1024]{2,1,0:T(8,128)(2,1)S(1)} collective-permute-done((bf16[2,128,1024]{2,1,0:T(8,128)(2,1)S(1)}, bf16[2,128,1024]{2,1,0:T(8,128)(2,1)S(1)}, u32[]{:S(2)}, u32[]{:S(2)}) %collective-permute-start.15) | collective-permute-done | bytes 524320 | tf_op jit(solution)/shard_map/ppermute | solution.py:351
  119.0 1.3 %prep.1 = (f32[2,2,8,1024]{3,2,1,0:T(8,128)S(1)}, s32[2,8]{1,0:T(2,128)S(1)}) custom-call(f32[2,8,512]{2,1,0:T(8,128)S(1)} %copy-done.2, s32[2,8,512]{2,1,0:T(8,128)S(1)} %copy-done.3, f32[2]{0:T(128)S(1)} %copy-done.5, s32[2,8]{1,0:T(2,128)S(1)} %copy-done.4, s32[8]{0:T(128)S(1)} %copy-done.6), custom_call_target="tpu_custom_call" | custom-call | tf_op jit(solution)/shard_map/prep/pallas_call | solution.py:435
  120.4 1.9 %emp_direct.1.refs_20_ = f32[4,2,256,256]{3,2,1,0:T(8,128)S(1)} custom-call(bf16[2,128,1024]{2,1,0:T(8,128)(2,1)S(1)} %get-tuple-element.9.refs_0_.refs_8_, bf16[4,128,1024]{2,1,0:T(8,128)(2,1)S(1)} %collective-permute-done.refs_1_, bf16[4,128,1024]{2,1,0:T(8,128)(2,1)S(1)} %collective-permute-done.1.refs_7_.refs_2_.refs_15_.refs_8_, ...), custom_call_target="tpu_custom_call" | custom-call | tf_op jit(solution)/shard_map/emp_direct/pallas_call | solution.py:494
  122.3 3.7 %occ_tiles.1.refs_19_ = f32[8,2,256,256]{3,2,1,0:T(8,128)S(1)} custom-call(bf16[2,128,1024]{2,1,0:T(8,128)(2,1)S(1)} %flatten_occ.1.occ_flat_ref.refs_0_.refs_8_, bf16[4,128,1024]{2,1,0:T(8,128)(2,1)S(1)} %collective-permute-done.refs_1_, bf16[4,128,1024]{2,1,0:T(8,128)(2,1)S(1)} %collective-permute-done.1.refs_7_.refs_2_.refs_15_.refs_8_, ...), custom_call_target="tpu_custom_call" | custom-call | tf_op jit(solution)/shard_map/occ_tiles/pallas_call | solution.py:483
  126.0 5.8 %closing.1 = f32[2,2,128,2,256]{4,3,2,1,0:T(2,128)} custom-call(bf16[2,128,1024]{2,1,0:T(8,128)(2,1)S(1)} %get-tuple-element.9.refs_0_.refs_8_, bf16[4,128,1024]{2,1,0:T(8,128)(2,1)S(1)} %collective-permute-done.refs_1_, bf16[4,128,1024]{2,1,0:T(8,128)(2,1)S(1)} %collective-permute-done.1.refs_7_.refs_2_.refs_15_.refs_8_, ...), custom_call_target="tpu_custom_call" | custom-call | tf_op jit(solution)/shard_map/closing/pallas_call | solution.py:495
  (18 shorter events, 0.0 us)
Async XLA Ops:
  0.0 1.0 copy-start
  1.2 1.0 copy-start.1
  2.4 17.3 %collective-permute-start.8 = (bf16[2,128,1024]{2,1,0:T(8,128)(2,1)S(1)}, bf16[2,128,1024]{2,1,0:T(8,128)(2,1)S(1)}, u32[]{:S(2)}, u32[]{:S(2)}) collective-permute-start(bf16[2,128,1024]{2,1,0:T(8,128)(2,1)S(1)} %get-tuple-element.9.refs_0_.refs_8_), channel_id=1, source_target_pairs={{0,2},{1,3},{4,6},{5,7},{6,4},{7,5},{8,10},{9,11},{12,14},{13,15},... | collective-permute-start | bytes 1572872 | tf_op jit(solution)/shard_map/ppermute | solution.py:351
  7.4 13.0 %collective-permute-start.11 = (bf16[2,128,1024]{2,1,0:T(8,128)(2,1)S(1)}, bf16[2,128,1024]{2,1,0:T(8,128)(2,1)S(1)}, u32[]{:S(2)}, u32[]{:S(2)}) collective-permute-start(bf16[2,128,1024]{2,1,0:T(8,128)(2,1)S(1)} %get-tuple-element.9.refs_0_.refs_8_), channel_id=1, source_target_pairs={{2,4},{3,5},{4,2},{5,3},{10,12},{11,13},{12,10},{13,11},{18,20},{1... | collective-permute-start | bytes 1572872 | tf_op jit(solution)/shard_map/ppermute | solution.py:351
  8.1 18.4 %collective-permute-start.16 = (bf16[2,128,1024]{2,1,0:T(8,128)(2,1)S(1)}, bf16[2,128,1024]{2,1,0:T(8,128)(2,1)S(1)}, u32[]{:S(2)}, u32[]{:S(2)}) collective-permute-start(bf16[2,128,1024]{2,1,0:T(8,128)(2,1)S(1)} %get-tuple-element.9.refs_0_.refs_8_), channel_id=1, source_target_pairs={{2,0},{3,1},{10,8},{11,9},{20,22},{21,23},{28,30},{29,31}} | collective-permute-start | bytes 1572872 | tf_op jit(solution)/shard_map/ppermute | solution.py:351
  9.4 37.2 %collective-permute-start.1 = (bf16[4,128,1024]{2,1,0:T(8,128)(2,1)S(1)}, bf16[4,128,1024]{2,1,0:T(8,128)(2,1)S(1)}, u32[]{:S(2)}, u32[]{:S(2)}) collective-permute-start(bf16[4,128,1024]{2,1,0:T(8,128)(2,1)S(1)} %get-tuple-element.10), channel_id=1, source_target_pairs={{0,16},{1,17},{2,18},{3,19},{4,20},{5,21},{6,22},{7,23},{8,24},{9,... | collective-permute-start | bytes 3145736 | tf_op jit(solution)/shard_map/ppermute | solution.py:351
  10.3 26.0 %collective-permute-start.20 = (bf16[2,128,1024]{2,1,0:T(8,128)(2,1)S(1)}, bf16[2,128,1024]{2,1,0:T(8,128)(2,1)S(1)}, u32[]{:S(2)}, u32[]{:S(2)}) collective-permute-start(bf16[2,128,1024]{2,1,0:T(8,128)(2,1)S(1)} %flatten_occ.1.occ_flat_ref.refs_0_.refs_8_), channel_id=1, source_target_pairs={{0,2},{1,3},{2,0},{3,1},{4,6},{5,7},{6,4},{7,5},{8,10},{9,11},{10,... | collective-permute-start | bytes 1572872 | tf_op jit(solution)/shard_map/ppermute | solution.py:351
  19.7 17.9 %collective-permute-start.21 = (bf16[2,128,1024]{2,1,0:T(8,128)(2,1)S(1)}, bf16[2,128,1024]{2,1,0:T(8,128)(2,1)S(1)}, u32[]{:S(2)}, u32[]{:S(2)}) collective-permute-start(bf16[2,128,1024]{2,1,0:T(8,128)(2,1)S(1)} %flatten_occ.1.occ_flat_ref.refs_0_.refs_8_), channel_id=1, source_target_pairs={{2,4},{3,5},{4,2},{5,3},{10,12},{11,13},{12,10},{13,11},{18,20},{1... | collective-permute-start | bytes 1572872 | tf_op jit(solution)/shard_map/ppermute | solution.py:351
  20.4 32.7 %collective-permute-start.3 = (bf16[4,128,1024]{2,1,0:T(8,128)(2,1)S(1)}, bf16[4,128,1024]{2,1,0:T(8,128)(2,1)S(1)}, u32[]{:S(2)}, u32[]{:S(2)}) collective-permute-start(bf16[4,128,1024]{2,1,0:T(8,128)(2,1)S(1)} %get-tuple-element.10), channel_id=1, source_target_pairs={{0,1},{1,0},{2,3},{3,2},{4,5},{5,4},{6,7},{7,6},{8,9},{9,8},{10,11... | collective-permute-start | bytes 3145736 | tf_op jit(solution)/shard_map/ppermute | solution.py:351
  26.5 18.8 %collective-permute-start.9 = (bf16[2,128,1024]{2,1,0:T(8,128)(2,1)S(1)}, bf16[2,128,1024]{2,1,0:T(8,128)(2,1)S(1)}, u32[]{:S(2)}, u32[]{:S(2)}) collective-permute-start(bf16[2,128,1024]{2,1,0:T(8,128)(2,1)S(1)} %collective-permute-done.8.refs_1_.refs_9_), channel_id=1, source_target_pairs={{2,4},{3,5},{4,2},{5,3},{6,22},{7,23},{10,12},{11,13},{12,10},{13,... | collective-permute-start | bytes 1572872 | tf_op jit(solution)/shard_map/ppermute | solution.py:351
  36.3 15.3 %collective-permute-start.12 = (bf16[2,128,1024]{2,1,0:T(8,128)(2,1)S(1)}, bf16[2,128,1024]{2,1,0:T(8,128)(2,1)S(1)}, u32[]{:S(2)}, u32[]{:S(2)}) collective-permute-start(bf16[2,128,1024]{2,1,0:T(8,128)(2,1)S(1)} %collective-permute-done.11.refs_3_.refs_11_), channel_id=1, source_target_pairs={{2,0},{3,1},{10,8},{11,9},{20,22},{21,23},{28,30},{29,31}} | collective-permute-start | bytes 1572872 | tf_op jit(solution)/shard_map/ppermute | solution.py:351
  37.6 14.7 %collective-permute-start.17 = (bf16[2,128,1024]{2,1,0:T(8,128)(2,1)S(1)}, bf16[2,128,1024]{2,1,0:T(8,128)(2,1)S(1)}, u32[]{:S(2)}, u32[]{:S(2)}) collective-permute-start(bf16[2,128,1024]{2,1,0:T(8,128)(2,1)S(1)} %collective-permute-done.11.refs_3_.refs_11_), channel_id=1, source_target_pairs={{4,6},{5,7},{12,14},{13,15},{18,16},{19,17},{26,24},{27,25}} | collective-permute-start | bytes 1572872 | tf_op jit(solution)/shard_map/ppermute | solution.py:351
  45.3 14.4 %collective-permute-start.22 = (bf16[2,128,1024]{2,1,0:T(8,128)(2,1)S(1)}, bf16[2,128,1024]{2,1,0:T(8,128)(2,1)S(1)}, u32[]{:S(2)}, u32[]{:S(2)}) collective-permute-start(bf16[2,128,1024]{2,1,0:T(8,128)(2,1)S(1)} %collective-permute-done.20.refs_1_.refs_2_.refs_9_.refs_10_), channel_id=1, source_target_pairs={{2,4},{3,5},{4,2},{5,3},{6,22},{7,23},{10,12},{11,13},{12,10},{13,... | collective-permute-start | bytes 1572872 | tf_op jit(solution)/shard_map/ppermute | solution.py:351
  46.6 15.3 %collective-permute-start.25 = (bf16[2,128,1024]{2,1,0:T(8,128)(2,1)S(1)}, bf16[2,128,1024]{2,1,0:T(8,128)(2,1)S(1)}, u32[]{:S(2)}, u32[]{:S(2)}) collective-permute-start(bf16[2,128,1024]{2,1,0:T(8,128)(2,1)S(1)} %collective-permute-done.21.refs_3_.refs_11_), channel_id=1, source_target_pairs={{2,0},{3,1},{10,8},{11,9},{20,22},{21,23},{28,30},{29,31}} | collective-permute-start | bytes 1572872 | tf_op jit(solution)/shard_map/ppermute | solution.py:351
  51.7 14.0 %collective-permute-start.23 = (bf16[2,128,1024]{2,1,0:T(8,128)(2,1)S(1)}, bf16[2,128,1024]{2,1,0:T(8,128)(2,1)S(1)}, u32[]{:S(2)}, u32[]{:S(2)}) collective-permute-start(bf16[2,128,1024]{2,1,0:T(8,128)(2,1)S(1)} %collective-permute-done.21.refs_3_.refs_11_), channel_id=1, source_target_pairs={{4,6},{5,7},{12,14},{13,15},{18,16},{19,17},{26,24},{27,25}} | collective-permute-start | bytes 1572872 | tf_op jit(solution)/shard_map/ppermute | solution.py:351
  52.4 14.1 %collective-permute-start.10 = (bf16[2,128,1024]{2,1,0:T(8,128)(2,1)S(1)}, bf16[2,128,1024]{2,1,0:T(8,128)(2,1)S(1)}, u32[]{:S(2)}, u32[]{:S(2)}) collective-permute-start(bf16[2,128,1024]{2,1,0:T(8,128)(2,1)S(1)} %collective-permute-done.9.refs_4_.refs_9_.refs_12_.refs_10_), channel_id=1, source_target_pairs={{2,18},{3,19},{4,6},{5,7},{10,26},{11,27},{12,14},{13,15},{18,16},... | collective-permute-start | bytes 1572872 | tf_op jit(solution)/shard_map/ppermute | solution.py:351
  53.1 26.8 %collective-permute-start.13 = (bf16[2,128,1024]{2,1,0:T(8,128)(2,1)S(1)}, bf16[2,128,1024]{2,1,0:T(8,128)(2,1)S(1)}, u32[]{:S(2)}, u32[]{:S(2)}) collective-permute-start(bf16[2,128,1024]{2,1,0:T(8,128)(2,1)S(1)} %collective-permute-done.12), channel_id=1, source_target_pairs={{0,16},{1,17},{8,24},{9,25},{22,6},{23,7},{30,14},{31,15}} | collective-permute-start | bytes 1572872 | tf_op jit(solution)/shard_map/ppermute | solution.py:351
  59.7 20.2 %collective-permute-start.27 = (bf16[2,128,1024]{2,1,0:T(8,128)(2,1)S(1)}, bf16[2,128,1024]{2,1,0:T(8,128)(2,1)S(1)}, u32[]{:S(2)}, u32[]{:S(2)}) collective-permute-start(bf16[2,128,1024]{2,1,0:T(8,128)(2,1)S(1)} %collective-permute-done.22.refs_4_.refs_9_.refs_12_.refs_17_), channel_id=1, source_target_pairs={{2,0},{3,1},{10,8},{11,9},{20,22},{21,23},{28,30},{29,31}} | collective-permute-start | bytes 1572872 | tf_op jit(solution)/shard_map/ppermute | solution.py:351
  62.0 29.0 %collective-permute-start.7 = (bf16[4,128,1024]{2,1,0:T(8,128)(2,1)S(1)}, bf16[4,128,1024]{2,1,0:T(8,128)(2,1)S(1)}, u32[]{:S(2)}, u32[]{:S(2)}) collective-permute-start(bf16[4,128,1024]{2,1,0:T(8,128)(2,1)S(1)} %collective-permute-done.1.refs_7_.refs_2_.refs_15_.refs_8_), channel_id=1, source_target_pairs={{0,2},{1,3},{2,4},{3,5},{8,10},{9,11},{10,12},{11,13},{20,18},{21,... | collective-permute-start | bytes 3145736 | tf_op jit(solution)/shard_map/ppermute | solution.py:351
  65.7 15.9 %collective-permute-start.24 = (bf16[2,128,1024]{2,1,0:T(8,128)(2,1)S(1)}, bf16[2,128,1024]{2,1,0:T(8,128)(2,1)S(1)}, u32[]{:S(2)}, u32[]{:S(2)}) collective-permute-start(bf16[2,128,1024]{2,1,0:T(8,128)(2,1)S(1)} %collective-permute-done.22.refs_4_.refs_9_.refs_12_.refs_17_), channel_id=1, source_target_pairs={{2,18},{3,19},{4,6},{5,7},{10,26},{11,27},{12,14},{13,15},{18,16},... | collective-permute-start | bytes 1572872 | tf_op jit(solution)/shard_map/ppermute | solution.py:351
  66.4 20.1 %collective-permute-start.26 = (bf16[2,128,1024]{2,1,0:T(8,128)(2,1)S(1)}, bf16[2,128,1024]{2,1,0:T(8,128)(2,1)S(1)}, u32[]{:S(2)}, u32[]{:S(2)}) collective-permute-start(bf16[2,128,1024]{2,1,0:T(8,128)(2,1)S(1)} %collective-permute-done.25), channel_id=1, source_target_pairs={{0,16},{1,17},{8,24},{9,25},{22,6},{23,7},{30,14},{31,15}} | collective-permute-start | bytes 1572872 | tf_op jit(solution)/shard_map/ppermute | solution.py:351
  79.9 20.6 %collective-permute-start = (bf16[4,128,1024]{2,1,0:T(8,128)(2,1)S(1)}, bf16[4,128,1024]{2,1,0:T(8,128)(2,1)S(1)}, u32[]{:S(2)}, u32[]{:S(2)}) collective-permute-start(bf16[4,128,1024]{2,1,0:T(8,128)(2,1)S(1)} %get-tuple-element.10), channel_id=1, source_target_pairs={{0,8},{1,9},{2,10},{3,11},{4,12},{5,13},{6,14},{7,15},{8,0},{9,1},... | collective-permute-start | bytes 3145736 | tf_op jit(solution)/shard_map/ppermute | solution.py:351
  80.0 25.6 %collective-permute-start.5 = (bf16[4,128,1024]{2,1,0:T(8,128)(2,1)S(1)}, bf16[4,128,1024]{2,1,0:T(8,128)(2,1)S(1)}, u32[]{:S(2)}, u32[]{:S(2)}) collective-permute-start(bf16[4,128,1024]{2,1,0:T(8,128)(2,1)S(1)} %collective-permute-done.1.refs_7_.refs_2_.refs_15_.refs_8_), channel_id=1, source_target_pairs={{0,1},{1,0},{2,3},{3,2},{4,5},{5,4},{6,7},{7,6},{8,9},{9,8},{10,11... | collective-permute-start | bytes 3145736 | tf_op jit(solution)/shard_map/ppermute | solution.py:351
  81.6 24.5 %collective-permute-start.2 = (bf16[4,128,1024]{2,1,0:T(8,128)(2,1)S(1)}, bf16[4,128,1024]{2,1,0:T(8,128)(2,1)S(1)}, u32[]{:S(2)}, u32[]{:S(2)}) collective-permute-start(bf16[4,128,1024]{2,1,0:T(8,128)(2,1)S(1)} %collective-permute-done.1.refs_7_.refs_2_.refs_15_.refs_8_), channel_id=1, source_target_pairs={{0,8},{1,9},{2,10},{3,11},{4,12},{5,13},{6,14},{7,15},{8,0},{9,1},... | collective-permute-start | bytes 3145736 | tf_op jit(solution)/shard_map/ppermute | solution.py:351
  86.5 13.9 %collective-permute-start.28 = (bf16[2,128,1024]{2,1,0:T(8,128)(2,1)S(1)}, bf16[2,128,1024]{2,1,0:T(8,128)(2,1)S(1)}, u32[]{:S(2)}, u32[]{:S(2)}) collective-permute-start(bf16[2,128,1024]{2,1,0:T(8,128)(2,1)S(1)} %collective-permute-done.27), channel_id=1, source_target_pairs={{0,16},{1,17},{8,24},{9,25},{22,6},{23,7},{30,14},{31,15}} | collective-permute-start | bytes 1572872 | tf_op jit(solution)/shard_map/ppermute | solution.py:351
  90.9 14.6 %collective-permute-start.14 = (bf16[2,128,1024]{2,1,0:T(8,128)(2,1)S(1)}, bf16[2,128,1024]{2,1,0:T(8,128)(2,1)S(1)}, u32[]{:S(2)}, u32[]{:S(2)}) collective-permute-start(bf16[2,128,1024]{2,1,0:T(8,128)(2,1)S(1)} %collective-permute-done.9.refs_4_.refs_9_.refs_12_.refs_10_), channel_id=1, source_target_pairs={{2,0},{3,1},{10,8},{11,9},{20,22},{21,23},{28,30},{29,31}} | collective-permute-start | bytes 1572872 | tf_op jit(solution)/shard_map/ppermute | solution.py:351
  92.4 26.6 %copy-start.2 = (f32[2,8,512]{2,1,0:T(8,128)S(1)}, f32[2,8,512]{2,1,0:T(8,128)}, u32[]{:S(2)}) copy-start(f32[2,8,512]{2,1,0:T(8,128)} %levels_ref.1) | copy-start | bytes 98308
  92.4 26.5 %copy-start.3 = (s32[2,8,512]{2,1,0:T(8,128)S(1)}, s32[2,8,512]{2,1,0:T(8,128)}, u32[]{:S(2)}) copy-start(s32[2,8,512]{2,1,0:T(8,128)} %rank_ref.1) | copy-start | bytes 98308
  92.4 26.5 %copy-start.4 = (s32[2,8]{1,0:T(2,128)S(1)}, s32[2,8]{1,0:T(2,128)}, u32[]{:S(2)}) copy-start(s32[2,8]{1,0:T(2,128)} %map_ref.1) | copy-start | bytes 196
  92.4 26.5 %copy-start.5 = (f32[2]{0:T(128)S(1)}, f32[2]{0:T(128)}, u32[]{:S(2)}) copy-start(f32[2]{0:T(128)} %times_ref.1) | copy-start | bytes 28
  92.5 26.5 %copy-start.6 = (s32[8]{0:T(128)S(1)}, s32[8]{0:T(128)}, u32[]{:S(2)}) copy-start(s32[8]{0:T(128)} %kpoint_ref.1) | copy-start | bytes 100
  100.4 20.0 %collective-permute-start.4 = (bf16[4,128,1024]{2,1,0:T(8,128)(2,1)S(1)}, bf16[4,128,1024]{2,1,0:T(8,128)(2,1)S(1)}, u32[]{:S(2)}, u32[]{:S(2)}) collective-permute-start(bf16[4,128,1024]{2,1,0:T(8,128)(2,1)S(1)} %collective-permute-done.3.refs_4_), channel_id=1, source_target_pairs={{0,8},{1,9},{2,10},{3,11},{4,12},{5,13},{6,14},{7,15},{8,0},{9,1},... | collective-permute-start | bytes 3145736 | tf_op jit(solution)/shard_map/ppermute | solution.py:351
  100.5 19.8 %collective-permute-start.18 = (bf16[2,2,128,1024]{3,2,1,0:T(8,128)(2,1)S(1)}, bf16[2,2,128,1024]{3,2,1,0:T(8,128)(2,1)S(1)}, u32[]{:S(2)}, u32[]{:S(2)}) collective-permute-start(bf16[2,2,128,1024]{3,2,1,0:T(8,128)(2,1)S(1)} %shard_map.73), channel_id=1, source_target_pairs={{0,8},{1,9},{2,10},{3,11},{4,12},{5,13},{6,14},{7,15},{8,0},{9,1},... | collective-permute-start | bytes 3145736 | tf_op jit(solution)/shard_map/ppermute | solution.py:351
  105.5 14.8 %collective-permute-start.6 = (bf16[4,128,1024]{2,1,0:T(8,128)(2,1)S(1)}, bf16[4,128,1024]{2,1,0:T(8,128)(2,1)S(1)}, u32[]{:S(2)}, u32[]{:S(2)}) collective-permute-start(bf16[4,128,1024]{2,1,0:T(8,128)(2,1)S(1)} %collective-permute-done.5.refs_6_), channel_id=1, source_target_pairs={{0,8},{1,9},{2,10},{3,11},{4,12},{5,13},{6,14},{7,15},{8,0},{9,1},... | collective-permute-start | bytes 3145736 | tf_op jit(solution)/shard_map/ppermute | solution.py:351
  105.5 16.8 %collective-permute-start.29 = (bf16[2,2,128,1024]{3,2,1,0:T(8,128)(2,1)S(1)}, bf16[2,2,128,1024]{3,2,1,0:T(8,128)(2,1)S(1)}, u32[]{:S(2)}, u32[]{:S(2)}) collective-permute-start(bf16[2,2,128,1024]{3,2,1,0:T(8,128)(2,1)S(1)} %shard_map.74), channel_id=1, source_target_pairs={{0,8},{1,9},{2,10},{3,11},{4,12},{5,13},{6,14},{7,15},{8,0},{9,1},... | collective-permute-start | bytes 3145736 | tf_op jit(solution)/shard_map/ppermute | solution.py:351
  106.0 12.9 %collective-permute-start.15 = (bf16[2,128,1024]{2,1,0:T(8,128)(2,1)S(1)}, bf16[2,128,1024]{2,1,0:T(8,128)(2,1)S(1)}, u32[]{:S(2)}, u32[]{:S(2)}) collective-permute-start(bf16[2,128,1024]{2,1,0:T(8,128)(2,1)S(1)} %collective-permute-done.14), channel_id=1, source_target_pairs={{0,16},{1,17},{8,24},{9,25},{22,6},{23,7},{30,14},{31,15}} | collective-permute-start | bytes 1572872 | tf_op jit(solution)/shard_map/ppermute | solution.py:351
  119.0 7.0 %collective-permute-start.19 = (bf16[2,128,1024]{2,1,0:T(8,128)(2,1)S(1)}, bf16[2,128,1024]{2,1,0:T(8,128)(2,1)S(1)}, u32[]{:S(2)}, u32[]{:S(2)}) collective-permute-start(bf16[2,128,1024]{2,1,0:T(8,128)(2,1)S(1)} %collective-permute-done.15.refs_14_), channel_id=1, source_target_pairs={{0,8},{1,9},{2,10},{3,11},{4,12},{5,13},{6,14},{7,15},{8,0},{9,1},... | collective-permute-start | bytes 1572872 | tf_op jit(solution)/shard_map/ppermute | solution.py:351
where the time goes:
time: 133 us; the launch traced here: 132 us
  waiting for transfers between devices  64.5 us (48%)
  starting transfers between devices  51.5 us (39%)
  Pallas kernels  13.4 us (10%)
  local copies, waits for them, and re-layouts  2.11 us (2%)
    ppermute x30, waiting for transfers between devices, send(): return lax.ppermute(array, AXES, pairs)  64.5 us
    ppermute x30, starting transfers between devices, send(): return lax.ppermute(array, AXES, pairs)  51.5 us
    pallas_call x1, Pallas kernels, output_stationary(): pl.pallas_call(functools.partial(closing_kernel, -1.0 / kpoints, cases),...  5.83 us
    pallas_call x1, Pallas kernels, output_stationary(): tiles = occ_tiles(*row_panels[0], *direct[0], *across[0], given[0], weights)  3.7 us
  transfers between devices with their start and end apart: 30, of which 11 were waited for; matrix products, arithmetic and copies ran while one was open for 0% of the time, Pallas kernels for 5%

commit v1 on v0

--- a/solution.py
+++ b/solution.py
@@ -153,11 +153,12 @@
         occ_out[slot] = occ_ref[slot].reshape(occ_out.shape[1:])
 
 
-def flatten_emp_kernel(emp_ref, occ_flat_ref, emp_out, both_out):
+def flatten_emp_kernel(emp_ref, occ_flat_ref, emp_out, both_out, *part_outs):
     slots = emp_out.shape[0]
     for slot in range(slots):
         panel = emp_ref[slot].reshape(emp_out.shape[1:])
         emp_out[slot] = panel
+        part_outs[slot][0] = panel
         both_out[slot] = occ_flat_ref[slot]
         both_out[slots + slot] = panel
 
@@ -181,17 +182,32 @@
     return ref if ref.shape[0] == slots else ref.at[pl.ds(kind * slots, slots)]
 
 
+def start_copy(source, kind, target, sem):
+    slots = target.shape[0]
+    if isinstance(source, tuple):
+        for slot, piece in enumerate(source):
+            pltpu.make_async_copy(piece, target.at[pl.ds(slot, 1)], sem).start()
+    else:
+        pltpu.make_async_copy(part(source, kind, slots), target, sem).start()
+
+
+def grouped(refs, cases):
+    extra = len(refs) - cases
+    if not extra:
+        return list(refs)
+    return list(refs[:2]) + [tuple(refs[2 : 3 + extra])] + list(refs[3 + extra :])
+
+
 def pack_kernel(kind, cases, *refs):
-    direct, crossed = refs[:cases], refs[cases : 2 * cases]
-    send_ref, sems = refs[2 * cases :]
+    direct, crossed = grouped(refs[: -2 - cases], cases), refs[-2 - cases : -2]
+    send_ref, sems = refs[-2:]
     _, send = choose()
-    slots = send_ref.shape[1]
     for case in range(cases):
 
         @pl.when(send == case)
         def _():
             for side, source in enumerate((direct[case], crossed[case])):
-                pltpu.make_async_copy(part(source, kind, slots), send_ref.at[side], sems.at[side]).start()
+                start_copy(source, kind, send_ref.at[side], sems.at[side])
 
     for side in range(2):
         pltpu.make_async_copy(send_ref.at[side], send_ref.at[side], sems.at[side]).wait()
@@ -199,26 +215,25 @@
 
 def pack(kind, direct, crossed, shape):
     return pl.pallas_call(
-        functools.partial(pack_kernel, kind, len(direct)),
+        functools.partial(pack_kernel, kind, len(crossed)),
         out_shape=jax.ShapeDtypeStruct((2,) + shape, jnp.bfloat16),
-        in_specs=[HBM] * (2 * len(direct)),
+        in_specs=[HBM] * (len(direct) + len(crossed)),
         out_specs=VMEM,
         scratch_shapes=[pltpu.SemaphoreType.DMA((2,))],
         compiler_params=LIMIT,
     )(*direct, *crossed)
 
 
-def load_panels(kind, groups, rows, direct, crossed, recv, last, row_buf, col_buf, sems):
-    slots = col_buf.shape[1]
+def load_columns(kind, groups, direct, crossed, recv, last, col_buf, sems):
     keep, _ = choose()
 
     def fetch(source, k):
-        pltpu.make_async_copy(part(source, kind, slots), col_buf.at[k], sems.at[k, 0]).start()
+        start_copy(source, kind, col_buf.at[k], sems.at[k, 0])
 
     for k in groups:
         if k & 1:
             inside = recv.at[k >> 1]
-            if last is None or k == 1:
+            if last is None:
                 fetch(inside, k)
             else:
                 pl.when(keep == 6)(functools.partial(fetch, last, k))
@@ -226,31 +241,37 @@
         else:
             for case, source in enumerate((direct, crossed)[k >> 1]):
                 pl.when(keep == case)(functools.partial(fetch, source, k))
+
+
+def load_rows(kind, groups, rows, row_buf, sems):
+    slots = row_buf.shape[2]
+    for k in groups:
         for half in range(2):
             panel = part(rows[half * 4 + k], kind, slots)
             pltpu.make_async_copy(panel, row_buf.at[half, k], sems.at[k, 1 + half]).start()
 
-    def wait(k):
-        for index, target in enumerate((col_buf.at[k], row_buf.at[0, k], row_buf.at[1, k])):
-            pltpu.make_async_copy(target, target, sems.at[k, index]).wait()
-
-    return wait
-
-
-def tile(kind, k, i, half, stacked, row_buf, weight_ref):
-    per_group = row_buf.shape[2]
-    slot = (lax.axis_index("kgrp") ^ k) * per_group + i
+
+def wait_columns(k, col_buf, sems):
+    pltpu.make_async_copy(col_buf.at[k], col_buf.at[k], sems.at[k, 0]).wait()
+
+
+def wait_rows(k, row_buf, sems):
+    for half in range(2):
+        pltpu.make_async_copy(row_buf.at[half, k], row_buf.at[half, k], sems.at[k, 1 + half]).wait()
+
+
+def scale_rows(kind, k, i, half, row_buf, weight_ref):
+    slot = (lax.axis_index("kgrp") ^ k) * row_buf.shape[2] + i
     panel = row_buf[half, k, i].astype(jnp.float32)
     scaled = [
         (panel * weight_ref[kind, t, pl.ds(slot, 1), :]).astype(jnp.bfloat16)
         for t in range(weight_ref.shape[1])
     ]
-    return lax.dot_general(
-        stacked,
-        jnp.concatenate(scaled, axis=0),
-        (((1,), (1,)), ((), ())),
-        preferred_element_type=jnp.float32,
-    )
+    return jnp.concatenate(scaled, axis=0)
+
+
+def tile(stacked, scaled):
+    return lax.dot_general(stacked, scaled, (((1,), (1,)), ((), ())), preferred_element_type=jnp.float32)
 
 
 def stack_columns(columns):
@@ -262,72 +283,99 @@
 def occ_kernel(cases, *refs):
     rows, direct, crossed = refs[:8], refs[8 : 8 + cases], refs[8 + cases : 8 + 2 * cases]
     recv, weight_ref, out_ref, row_buf, col_buf, sems = refs[8 + 2 * cases :]
-    wait = load_panels(0, range(4), rows, direct, crossed, recv, None, row_buf, col_buf, sems)
+    load_columns(0, range(4), direct, crossed, recv, None, col_buf, sems)
+    load_rows(0, range(4), rows, row_buf, sems)
     per_group = col_buf.shape[1]
     for k in range(4):
-        wait(k)
+        wait_columns(k, col_buf, sems)
+        wait_rows(k, row_buf, sems)
         for i in range(per_group):
             stacked = stack_columns(col_buf[k, i])
             for half in range(2):
-                out_ref[k * per_group + i, half] = tile(0, k, i, half, stacked, row_buf, weight_ref)
-
-
-def emp_direct_kernel(cases, *refs):
-    rows, direct = refs[:8], refs[8 : 8 + cases]
-    recv, weight_ref, out_ref, row_buf, col_buf, sems = refs[8 + cases :]
-    wait = load_panels(1, (0, 1), rows, direct, None, recv, None, row_buf, col_buf, sems)
-    per_group = col_buf.shape[1]
-    for k in (0, 1):
-        wait(k)
-        for i in range(per_group):
-            stacked = stack_columns(col_buf[k, i])
-            for half in range(2):
-                out_ref[k * per_group + i, half] = tile(1, k, i, half, stacked, row_buf, weight_ref)
+                scaled = scale_rows(0, k, i, half, row_buf, weight_ref)
+                out_ref[k * per_group + i, half] = tile(stacked, scaled)
 
 
 STRIP = 16
 
 
-def closing_kernel(factor, cases, *refs):
-    rows, crossed = refs[:8], refs[8 : 8 + cases]
-    recv, last, weight_ref, pair_ref, occ_ref, direct_ref, out_ref, row_buf, col_buf, moved, sems = refs[8 + cases :]
-    wait = load_panels(1, (2, 3), rows, None, crossed, recv, last, row_buf, col_buf, sems)
-    per_group, block = col_buf.shape[1], col_buf.shape[2]
-    split = 2 * per_group
+def pair_sums(moved, occ_ref, pair_ref, first, before, store):
+    count, halves = moved.shape[:2]
+    block = moved.shape[2] // 2
     transfers = pair_ref.shape[0]
-    times = weight_ref.shape[1]
-    y = lax.axis_index("col")
-    for k in (2, 3):
-        wait(k)
-        for i in range(per_group):
-            stacked = stack_columns(col_buf[k, i])
-            for half in range(2):
-                moved[k * per_group + i - split, half] = tile(1, k, i, half, stacked, row_buf, weight_ref)
-    held = [[pair_ref[q, a] for a in range(2 * split)] for q in range(transfers)]
-    for half in range(2):
-        start = pl.multiple_of((y ^ half) * block, LANES)
+    held = [[pair_ref[q, first + a] for a in range(count)] for q in range(transfers)]
+    for half in range(halves):
 
         def strip(index, carry):
             real_rows = pl.ds(pl.multiple_of(index * STRIP, STRIP), STRIP)
             imag_rows = pl.ds(pl.multiple_of(index * STRIP + block, STRIP), STRIP)
             sums = [[None, None] for _ in range(transfers)]
-            for a in range(2 * split):
-                source = direct_ref if a < split else moved
-                re = source[a % split, half, real_rows, :]
-                im = source[a % split, half, imag_rows, :]
+            if before is not None:
+                sums = [[before[q, half, comp, real_rows, :] for comp in range(2)] for q in range(transfers)]
+            for a in range(count):
+                re, im = moved[a, half, real_rows, :], moved[a, half, imag_rows, :]
                 for q in range(transfers):
                     ro = occ_ref[held[q][a], half, real_rows, :]
                     io = occ_ref[held[q][a], half, imag_rows, :]
                     for comp, piece in enumerate((ro * re + io * im, io * re - ro * im)):
-                        sums[q][comp] = piece if a == 0 else sums[q][comp] + piece
+                        sums[q][comp] = piece if sums[q][comp] is None else sums[q][comp] + piece
             for q in range(transfers):
                 for comp in range(2):
-                    total = sums[q][comp] * factor
-                    for t in range(times):
-                        out_ref[comp, q, real_rows, t, pl.ds(start, block)] = total[:, t * block : (t + 1) * block]
+                    store(half, real_rows, q, comp, sums[q][comp])
             return carry
 
         lax.fori_loop(0, block // STRIP, strip, 0)
+
+
+def scale_kernel(*refs):
+    rows, weight_ref, scaled_ref, row_buf, sems = refs[:8], *refs[8:]
+    load_rows(1, range(4), rows, row_buf, sems)
+    for k in range(4):
+        wait_rows(k, row_buf, sems)
+        for i in range(row_buf.shape[2]):
+            for half in range(2):
+                scaled_ref[half, k, i] = scale_rows(1, k, i, half, row_buf, weight_ref)
+
+
+def emp_direct_kernel(cases, *refs):
+    direct = grouped(refs[:-8], cases)
+    recv, scaled_ref, pair_ref, occ_ref, sum_ref, col_buf, moved, sems = refs[-8:]
+    load_columns(1, (0, 1), direct, None, recv, None, col_buf, sems)
+    per_group = col_buf.shape[1]
+    for k in (0, 1):
+        wait_columns(k, col_buf, sems)
+        for i in range(per_group):
+            stacked = stack_columns(col_buf[k, i])
+            for half in range(2):
+                moved[k * per_group + i, half] = tile(stacked, scaled_ref[half, k, i])
+
+    def store(half, rows_at, q, comp, value):
+        sum_ref[q, half, comp, rows_at, :] = value
+
+    pair_sums(moved, occ_ref, pair_ref, 0, None, store)
+
+
+def closing_kernel(factor, cases, *refs):
+    crossed = refs[:cases]
+    recv, last, scaled_ref, pair_ref, occ_ref, sum_ref, out_ref, col_buf, moved, sems = refs[cases:]
+    load_columns(1, (2, 3), None, crossed, recv, last, col_buf, sems)
+    per_group, block = col_buf.shape[1:3]
+    times = out_ref.shape[3]
+    y = lax.axis_index("col")
+    for k in (2, 3):
+        wait_columns(k, col_buf, sems)
+        for i in range(per_group):
+            stacked = stack_columns(col_buf[k, i])
+            for half in range(2):
+                moved[(k - 2) * per_group + i, half] = tile(stacked, scaled_ref[half, k, i])
+
+    def store(half, rows_at, q, comp, value):
+        start = pl.multiple_of((y ^ half) * block, LANES)
+        value = value * factor
+        for t in range(times):
+            out_ref[comp, q, rows_at, t, pl.ds(start, block)] = value[:, t * block : (t + 1) * block]
+
+    pair_sums(moved, occ_ref, pair_ref, 2 * per_group, sum_ref, store)
 
 
 def output_stationary(occ_orbitals, emp_orbitals, energies, band_order, imag_times, kq_map, slot_kpoint):
@@ -395,6 +443,14 @@
     def to_far_outer(x, h, z, y):
         return (1 - x, h, z, y) if near(x, z) and not inner(z) else None
 
+    def to_owner(x, h, z, y):
+        owner = h != z // half
+        return (1 - x, h, z, y) if near(x, z) and not inner(z) and owner else None
+
+    def to_other_owner(x, h, z, y):
+        owner = h != z // half
+        return None if owner or inner(z) or not near(x, z) else (1 - x, 1 - h, z, y)
+
     def flip_y(x, h, z, y):
         return x, h, z, 1 - y
 
@@ -410,11 +466,12 @@
         compiler_params=LIMIT,
         name="flatten_occ",
     )(occ_orbitals)
-    emp_flat, both = pl.pallas_call(
+    single = jax.ShapeDtypeStruct((1, block, width), jnp.bfloat16)
+    emp_flat, both, *emp_parts = pl.pallas_call(
         flatten_emp_kernel,
-        out_shape=[flat, jax.ShapeDtypeStruct((2 * slots, block, width), jnp.bfloat16)],
+        out_shape=[flat, jax.ShapeDtypeStruct((2 * slots, block, width), jnp.bfloat16)] + [single] * slots,
         in_specs=[VMEM] * 2,
-        out_specs=[VMEM] * 2,
+        out_specs=[VMEM] * (2 + slots),
         compiler_params=LIMIT,
         name="flatten_emp",
     )(emp_orbitals, occ_flat)
@@ -435,7 +492,7 @@
     weights, pairs = prepare(energies, band_order, imag_times, kq_map, slot_kpoint)
 
     s1 = [send(kinds[0], swap), send(kinds[1], swap_main)]
-    late = send(kinds[1], swap_late)
+    late = [send(emp_parts[slot], swap_late) for slot in range(slots)]
     b = [send(kinds[i], middle) for i in range(2)]
     crossed = send(both, flip_x)
     turned = send(both, flip_y)
@@ -451,16 +508,16 @@
     ex = [send(en[i], to_far_outer) for i in range(2)]
     fn = [send(d[i], outward_near) for i in range(2)]
     f = [send(d[i], to_far_or_outward) for i in range(2)]
-    fx = [send(fn[i], to_far_outer) for i in range(2)]
-    last = send(fx[1], flip_core)
+    fx = [send(fn[0], to_far_outer), send(fn[1], to_owner)]
+    last = send(fn[1], to_other_owner)
     row_panels, direct, across, given = [], [], [], []
     for kind in range(2):
         row_panels.append([
             kinds[kind], sibling, crossed, crossed_sibling,
             turned, turned_sibling, turned_crossed, turned_crossed_sibling,
         ])
-        swapped = late if kind else s1[0]
-        direct.append([kinds[kind], s1[kind], swapped, b[kind], d[kind], e[kind], f[kind]])
+        swapped = late if kind else s1[:1]
+        direct.append([kinds[kind], s1[kind], *swapped, b[kind], d[kind], e[kind], f[kind]])
         across.append([crossed, bx, d[kind], bx, f[kind], ex[kind], fx[kind]])
         ready = across[kind][:-1] + [ex[1] if kind else fx[0]]
         give = pack(kind, direct[kind], ready, (slots, block, width))
@@ -470,7 +527,7 @@
         pltpu.VMEM((2, 4, slots, block, width), jnp.bfloat16),
         pltpu.VMEM((4, slots, block, width), jnp.bfloat16),
     ]
-    cases = len(direct[0])
+    cases = len(across[0])
     occ_tiles = pl.pallas_call(
         functools.partial(occ_kernel, cases),
         out_shape=jax.ShapeDtypeStruct((kpoints, 2, 2 * block, times * block), jnp.float32),
@@ -482,25 +539,35 @@
     )
     tiles = occ_tiles(*row_panels[0], *direct[0], *across[0], given[0], weights)
     half_tiles = (kpoints // 2, 2, 2 * block, times * block)
+    scale = pl.pallas_call(
+        scale_kernel,
+        out_shape=jax.ShapeDtypeStruct((2, 4, slots, times * block, width), jnp.bfloat16),
+        in_specs=[HBM] * 8 + [VMEM],
+        out_specs=VMEM,
+        scratch_shapes=panel_scratch[:1] + [pltpu.SemaphoreType.DMA((4, 3))],
+        compiler_params=LIMIT,
+        name="scale",
+    )
+    scaled = scale(*row_panels[1], weights)
     emp_direct = pl.pallas_call(
         functools.partial(emp_direct_kernel, cases),
-        out_shape=jax.ShapeDtypeStruct(half_tiles, jnp.float32),
-        in_specs=[HBM] * (9 + cases) + [VMEM],
+        out_shape=jax.ShapeDtypeStruct((transfers, 2, 2, block, times * block), jnp.float32),
+        in_specs=[HBM] * (1 + len(direct[1])) + [VMEM, SMEM, VMEM],
         out_specs=VMEM,
-        scratch_shapes=panel_scratch + [pltpu.SemaphoreType.DMA((4, 3))],
+        scratch_shapes=panel_scratch[1:] + [pltpu.VMEM(half_tiles, jnp.float32), pltpu.SemaphoreType.DMA((4, 3))],
         compiler_params=LIMIT,
         name="emp_direct",
     )
-    direct_tiles = emp_direct(*row_panels[1], *direct[1], given[1], weights)
+    sums = emp_direct(*direct[1], given[1], scaled, pairs, tiles)
     result = pl.pallas_call(
         functools.partial(closing_kernel, -1.0 / kpoints, cases),
         out_shape=jax.ShapeDtypeStruct((2, transfers, block, times, cols * block), jnp.float32),
-        in_specs=[HBM] * (10 + cases) + [VMEM, SMEM, VMEM, VMEM],
+        in_specs=[HBM] * (2 + cases) + [VMEM, SMEM, VMEM, VMEM],
         out_specs=VMEM,
-        scratch_shapes=panel_scratch + [pltpu.VMEM(half_tiles, jnp.float32), pltpu.SemaphoreType.DMA((4, 3))],
+        scratch_shapes=panel_scratch[1:] + [pltpu.VMEM(half_tiles, jnp.float32), pltpu.SemaphoreType.DMA((4, 3))],
         compiler_params=LIMIT,
         name="closing",
-    )(*row_panels[1], *across[1], given[1], last, weights, pairs, tiles, direct_tiles)
+    )(*across[1], given[1], last, scaled, pairs, tiles, sums)
     return result[:, :, None]
 
 

time: 133 us -> 134 us (level)
  waiting for transfers between devices: 64.5 us -> 61.2 us
  starting transfers between devices: 51.5 us -> 54.1 us
  Pallas kernels: 13.4 us -> 15 us
    ppermute x30 -> x31, waiting for transfers between devices: 64.5 us -> 61.2 us  [send(): return lax.ppermute(array, AXES, pairs)]
    pallas_call x3 -> x4, Pallas kernels: 2.18 us -> 5.07 us  [the longest x1 3.02 us: output_stationary(): sums = emp_direct(*direct[1], given[1], scaled, pairs, tiles)]
    ppermute x30 -> x31, starting transfers between devices: 51.5 us -> 54.1 us  [send(): return lax.ppermute(array, AXES, pairs)]
  transfers between devices with their start and end apart: 30 -> 31, of which waited for: 11 -> 10; matrix products, arithmetic and copies ran while one was open for 0% -> 0% of each run, Pallas kernels for 5% -> 8%
where the time goes in v1:
time: 134 us; the launch traced here: 133 us
  waiting for transfers between devices  61.2 us (46%)
  starting transfers between devices  54.1 us (40%)
  Pallas kernels  15 us (11%)
  local copies, waits for them, and re-layouts  2.11 us (2%)
    ppermute x31, waiting for transfers between devices, send(): return lax.ppermute(array, AXES, pairs)  61.2 us
    ppermute x31, starting transfers between devices, send(): return lax.ppermute(array, AXES, pairs)  54.1 us
    pallas_call x1, Pallas kernels, output_stationary(): pl.pallas_call(functools.partial(closing_kernel, -1.0 / kpoints, cases),...  4.61 us
    pallas_call x1, Pallas kernels, output_stationary(): tiles = occ_tiles(*row_panels[0], *direct[0], *across[0], given[0], weights)  3.69 us
    pallas_call x1, Pallas kernels, output_stationary(): sums = emp_direct(*direct[1], given[1], scaled, pairs, tiles)  3.02 us
  transfers between devices with their start and end apart: 31, of which 10 were waited for; matrix products, arithmetic and copies ran while one was open for 0% of the time, Pallas kernels for 8%

profile of v1, /device:TPU:0, one launch (start us, length us, event | category | flops | bytes accessed | tf_op | source)
XLA Modules:
  0.0 132.9 jit_solution(11811334620513752041)
XLA Ops:
  0.0 1.0 copy-done
  1.0 0.2 flatten_occ.1.occ_flat_ref.refs_0_.refs_8_
  1.2 0.0 copy-start.1
  1.2 1.0 copy-done.1
  2.2 0.2 flatten_emp.1
  2.4 1.3 collective-permute-start.10
  3.7 3.1 %collective-permute-start.21 = (bf16[2,128,1024]{2,1,0:T(8,128)(2,1)S(1)}, bf16[2,128,1024]{2,1,0:T(8,128)(2,1)S(1)}, u32[]{:S(2)}, u32[]{:S(2)}) collective-permute-start(bf16[2,128,1024]{2,1,0:T(8,128)(2,1)S(1)} %flatten_occ.1.occ_flat_ref.refs_0_.refs_8_), channel_id=1, source_target_pairs={{0,2},{1,3},{2,0},{3,1},{4,6},{5,7},{6,4},{7,5},{8,10},{9,11},{10,... | collective-permute-start | bytes 1572872 | tf_op jit(solution)/shard_map/ppermute | solution.py:399
  6.9 0.9 collective-permute-start
  7.7 0.7 collective-permute-start.22
  8.4 7.6 %collective-permute-start.2 = (bf16[2,128,1024]{2,1,0:T(8,128)(2,1)S(1)}, bf16[2,128,1024]{2,1,0:T(8,128)(2,1)S(1)}, u32[]{:S(2)}, u32[]{:S(2)}) collective-permute-start(bf16[2,128,1024]{2,1,0:T(8,128)(2,1)S(1)} %get-tuple-element.12.refs_0_), channel_id=1, source_target_pairs={{0,2},{1,3},{4,6},{5,7},{6,4},{7,5},{8,10},{9,11},{12,14},{13,15},... | collective-permute-start | bytes 1572872 | tf_op jit(solution)/shard_map/ppermute | solution.py:399
  16.0 0.0 copy-start.2
  16.1 0.0 copy-start.3
  16.1 0.0 copy-start.4
  16.1 0.0 copy-start.5
  16.1 0.0 copy-start.6
  16.1 1.4 %collective-permute-start.11 = (bf16[1,128,1024]{2,1,0:T(8,128)(2,1)S(1)}, bf16[1,128,1024]{2,1,0:T(8,128)(2,1)S(1)}, u32[]{:S(2)}, u32[]{:S(2)}) collective-permute-start(bf16[1,128,1024]{2,1,0:T(8,128)(2,1)S(1)} %get-tuple-element.14), channel_id=1, source_target_pairs={{2,0},{3,1},{10,8},{11,9},{20,22},{21,23},{28,30},{29,31}} | collective-permute-start | bytes 786440 | tf_op jit(solution)/shard_map/ppermute | solution.py:399
  17.5 12.4 %collective-permute-done.11.refs_3_ = bf16[1,128,1024]{2,1,0:T(8,128)(2,1)S(1)} collective-permute-done((bf16[1,128,1024]{2,1,0:T(8,128)(2,1)S(1)}, bf16[1,128,1024]{2,1,0:T(8,128)(2,1)S(1)}, u32[]{:S(2)}, u32[]{:S(2)}) %collective-permute-start.11) | collective-permute-done | bytes 262176 | tf_op jit(solution)/shard_map/ppermute | solution.py:399
  29.9 0.7 collective-permute-start.5
  30.6 2.4 %collective-permute-start.17 = (bf16[4,128,1024]{2,1,0:T(8,128)(2,1)S(1)}, bf16[4,128,1024]{2,1,0:T(8,128)(2,1)S(1)}, u32[]{:S(2)}, u32[]{:S(2)}) collective-permute-start(bf16[4,128,1024]{2,1,0:T(8,128)(2,1)S(1)} %get-tuple-element.11), channel_id=1, source_target_pairs={{0,1},{1,0},{2,3},{3,2},{4,5},{5,4},{6,7},{7,6},{8,9},{9,8},{10,11... | collective-permute-start | bytes 3145736 | tf_op jit(solution)/shard_map/ppermute | solution.py:399
  33.0 0.0 collective-permute-done.22.refs_3_.refs_11_
  33.0 1.3 collective-permute-start.23
  34.3 1.3 collective-permute-start.26
  35.6 0.7 collective-permute-start.24
  36.3 0.0 collective-permute-done.refs_8_.refs_2_.refs_7_.refs_15_.refs_0_
  36.3 1.3 collective-permute-start.3
  37.6 12.1 %collective-permute-done.23.refs_4_.refs_9_.refs_12_.refs_17_ = bf16[2,128,1024]{2,1,0:T(8,128)(2,1)S(1)} collective-permute-done((bf16[2,128,1024]{2,1,0:T(8,128)(2,1)S(1)}, bf16[2,128,1024]{2,1,0:T(8,128)(2,1)S(1)}, u32[]{:S(2)}, u32[]{:S(2)}) %collective-permute-start.23) | collective-permute-done | bytes 524320 | tf_op jit(solution)/shard_map/ppermute | solution.py:399
  49.7 1.3 collective-permute-start.6
  51.0 0.7 collective-permute-start.12
  51.7 0.0 collective-permute-done.24.refs_5_.refs_13_
  51.7 1.3 collective-permute-start.28
  53.0 2.3 %collective-permute-done.17.refs_4_ = bf16[4,128,1024]{2,1,0:T(8,128)(2,1)S(1)} collective-permute-done((bf16[4,128,1024]{2,1,0:T(8,128)(2,1)S(1)}, bf16[4,128,1024]{2,1,0:T(8,128)(2,1)S(1)}, u32[]{:S(2)}, u32[]{:S(2)}) %collective-permute-start.17) | collective-permute-done | bytes 1048608 | tf_op jit(solution)/shard_map/ppermute | solution.py:399
  55.3 0.7 collective-permute-start.25
  56.0 2.7 %collective-permute-done.3.refs_5_.refs_10_.refs_2_ = bf16[2,128,1024]{2,1,0:T(8,128)(2,1)S(1)} collective-permute-done((bf16[2,128,1024]{2,1,0:T(8,128)(2,1)S(1)}, bf16[2,128,1024]{2,1,0:T(8,128)(2,1)S(1)}, u32[]{:S(2)}, u32[]{:S(2)}) %collective-permute-start.3) | collective-permute-done | bytes 524320 | tf_op jit(solution)/shard_map/ppermute | solution.py:399
  58.6 4.5 %collective-permute-start.27 = (bf16[2,128,1024]{2,1,0:T(8,128)(2,1)S(1)}, bf16[2,128,1024]{2,1,0:T(8,128)(2,1)S(1)}, u32[]{:S(2)}, u32[]{:S(2)}) collective-permute-start(bf16[2,128,1024]{2,1,0:T(8,128)(2,1)S(1)} %collective-permute-done.26), channel_id=1, source_target_pairs={{0,16},{1,17},{8,24},{9,25},{22,6},{23,7},{30,14},{31,15}} | collective-permute-start | bytes 1572872 | tf_op jit(solution)/shard_map/ppermute | solution.py:399
  63.1 8.3 %collective-permute-done.6 = bf16[2,128,1024]{2,1,0:T(8,128)(2,1)S(1)} collective-permute-done((bf16[2,128,1024]{2,1,0:T(8,128)(2,1)S(1)}, bf16[2,128,1024]{2,1,0:T(8,128)(2,1)S(1)}, u32[]{:S(2)}, u32[]{:S(2)}) %collective-permute-start.6) | collective-permute-done | bytes 524320 | tf_op jit(solution)/shard_map/ppermute | solution.py:399
  71.4 1.5 %collective-permute-start.1 = (bf16[4,128,1024]{2,1,0:T(8,128)(2,1)S(1)}, bf16[4,128,1024]{2,1,0:T(8,128)(2,1)S(1)}, u32[]{:S(2)}, u32[]{:S(2)}) collective-permute-start(bf16[4,128,1024]{2,1,0:T(8,128)(2,1)S(1)} %collective-permute-done.refs_8_.refs_2_.refs_7_.refs_15_.refs_0_), channel_id=1, source_target_pairs={{0,2},{1,3},{2,4},{3,5},{8,10},{9,11},{10,12},{11,13},{20,18},{21,... | collective-permute-start | bytes 3145736 | tf_op jit(solution)/shard_map/ppermute | solution.py:399
  72.9 0.0 collective-permute-done.12.refs_6_
  72.9 0.7 collective-permute-start.4
  73.6 5.0 %collective-permute-done.28 = bf16[2,128,1024]{2,1,0:T(8,128)(2,1)S(1)} collective-permute-done((bf16[2,128,1024]{2,1,0:T(8,128)(2,1)S(1)}, bf16[2,128,1024]{2,1,0:T(8,128)(2,1)S(1)}, u32[]{:S(2)}, u32[]{:S(2)}) %collective-permute-start.28) | collective-permute-done | bytes 524320 | tf_op jit(solution)/shard_map/ppermute | solution.py:399
  78.6 1.7 %collective-permute-start.19 = (bf16[4,128,1024]{2,1,0:T(8,128)(2,1)S(1)}, bf16[4,128,1024]{2,1,0:T(8,128)(2,1)S(1)}, u32[]{:S(2)}, u32[]{:S(2)}) collective-permute-start(bf16[4,128,1024]{2,1,0:T(8,128)(2,1)S(1)} %collective-permute-done.refs_8_.refs_2_.refs_7_.refs_15_.refs_0_), channel_id=1, source_target_pairs={{0,1},{1,0},{2,3},{3,2},{4,5},{5,4},{6,7},{7,6},{8,9},{9,8},{10,11... | collective-permute-start | bytes 3145736 | tf_op jit(solution)/shard_map/ppermute | solution.py:399
  80.4 7.8 %collective-permute-start.7 = (bf16[2,128,1024]{2,1,0:T(8,128)(2,1)S(1)}, bf16[2,128,1024]{2,1,0:T(8,128)(2,1)S(1)}, u32[]{:S(2)}, u32[]{:S(2)}) collective-permute-start(bf16[2,128,1024]{2,1,0:T(8,128)(2,1)S(1)} %collective-permute-done.6), channel_id=1, source_target_pairs={{0,16},{1,17},{8,24},{9,25},{22,6},{23,7},{30,14},{31,15}} | collective-permute-start | bytes 1572872 | tf_op jit(solution)/shard_map/ppermute | solution.py:399
  88.3 0.0 collective-permute-done.4.refs_7_.refs_12_.refs_4_
  88.3 7.2 %collective-permute-start.29 = (bf16[2,128,1024]{2,1,0:T(8,128)(2,1)S(1)}, bf16[2,128,1024]{2,1,0:T(8,128)(2,1)S(1)}, u32[]{:S(2)}, u32[]{:S(2)}) collective-permute-start(bf16[2,128,1024]{2,1,0:T(8,128)(2,1)S(1)} %collective-permute-done.28), channel_id=1, source_target_pairs={{0,16},{1,17},{8,24},{9,25},{22,6},{23,7},{30,14},{31,15}} | collective-permute-start | bytes 1572872 | tf_op jit(solution)/shard_map/ppermute | solution.py:399
  95.5 5.0 %collective-permute-done.7.refs_13_.refs_14_.refs_5_ = bf16[2,128,1024]{2,1,0:T(8,128)(2,1)S(1)} collective-permute-done((bf16[2,128,1024]{2,1,0:T(8,128)(2,1)S(1)}, bf16[2,128,1024]{2,1,0:T(8,128)(2,1)S(1)}, u32[]{:S(2)}, u32[]{:S(2)}) %collective-permute-start.7) | collective-permute-done | bytes 524320 | tf_op jit(solution)/shard_map/ppermute | solution.py:399
  100.5 1.3 collective-permute-start.8
  101.8 0.1 collective-permute-start.16
  101.9 9.4 %collective-permute-done.29.refs_13_.refs_21_ = bf16[2,128,1024]{2,1,0:T(8,128)(2,1)S(1)} collective-permute-done((bf16[2,128,1024]{2,1,0:T(8,128)(2,1)S(1)}, bf16[2,128,1024]{2,1,0:T(8,128)(2,1)S(1)}, u32[]{:S(2)}, u32[]{:S(2)}) %collective-permute-start.29) | collective-permute-done | bytes 524320 | tf_op jit(solution)/shard_map/ppermute | solution.py:399
  111.3 0.1 shard_map.74
  111.4 0.0 collective-permute-done.19.refs_6_
  111.4 0.6 collective-permute-start.20
  112.0 0.1 shard_map.73
  112.1 0.0 collective-permute-done.15.refs_1_
  112.1 0.1 collective-permute-start.30
  112.3 3.2 %collective-permute-done.8 = bf16[2,128,1024]{2,1,0:T(8,128)(2,1)S(1)} collective-permute-done((bf16[2,128,1024]{2,1,0:T(8,128)(2,1)S(1)}, bf16[2,128,1024]{2,1,0:T(8,128)(2,1)S(1)}, u32[]{:S(2)}, u32[]{:S(2)}) %collective-permute-start.8) | collective-permute-done | bytes 524320 | tf_op jit(solution)/shard_map/ppermute | solution.py:399
  115.4 0.0 collective-permute-start.13
  115.4 0.0 collective-permute-done.16.refs_3_
  115.4 1.3 %collective-permute-start.14 = (bf16[2,128,1024]{2,1,0:T(8,128)(2,1)S(1)}, bf16[2,128,1024]{2,1,0:T(8,128)(2,1)S(1)}, u32[]{:S(2)}, u32[]{:S(2)}) collective-permute-start(bf16[2,128,1024]{2,1,0:T(8,128)(2,1)S(1)} %collective-permute-done.8), channel_id=1, source_target_pairs={{0,24},{1,25},{30,6},{31,7}} | collective-permute-start | bytes 1572872 | tf_op jit(solution)/shard_map/ppermute | solution.py:399
  116.8 0.7 collective-permute-start.9
  117.5 1.3 prep.1
  118.9 1.8 %scale.1.refs_9_ = bf16[2,4,2,256,1024]{4,3,2,1,0:T(8,128)(2,1)S(1)} custom-call(bf16[2,128,1024]{2,1,0:T(8,128)(2,1)S(1)} %get-tuple-element.12.refs_0_, bf16[4,128,1024]{2,1,0:T(8,128)(2,1)S(1)} %collective-permute-done.15.refs_1_, bf16[4,128,1024]{2,1,0:T(8,128)(2,1)S(1)} %collective-permute-done.refs_8_.refs_2_.refs_7_.refs_15_.refs_0_, ...), custom_call_target="tpu_custom_call" | custom-call | tf_op jit(solution)/shard_map/scale/pallas_call | solution.py:551
  120.7 3.7 %occ_tiles.1.refs_11_ = f32[8,2,256,256]{3,2,1,0:T(8,128)S(1)} custom-call(bf16[2,128,1024]{2,1,0:T(8,128)(2,1)S(1)} %flatten_occ.1.occ_flat_ref.refs_0_.refs_8_, bf16[4,128,1024]{2,1,0:T(8,128)(2,1)S(1)} %collective-permute-done.15.refs_1_, bf16[4,128,1024]{2,1,0:T(8,128)(2,1)S(1)} %collective-permute-done.refs_8_.refs_2_.refs_7_.refs_15_.refs_0_, ...), custom_call_target="tpu_custom_call" | custom-call | tf_op jit(solution)/shard_map/occ_tiles/pallas_call | solution.py:540
  124.4 3.0 %emp_direct.1.refs_12_ = f32[2,2,2,128,256]{4,3,2,1,0:T(8,128)S(1)} custom-call(bf16[2,128,1024]{2,1,0:T(8,128)(2,1)S(1)} %get-tuple-element.12.refs_0_, bf16[2,128,1024]{2,1,0:T(8,128)(2,1)S(1)} %collective-permute-done.2.refs_1_, bf16[1,128,1024]{2,1,0:T(8,128)(2,1)S(1)} %collective-permute-done.10.refs_2_, ...), custom_call_target="tpu_custom_call" | custom-call | tf_op jit(solution)/shard_map/emp_direct/pallas_call | solution.py:561
  127.5 0.8 collective-permute-done.14.refs_8_
  128.3 4.6 %closing.1 = f32[2,2,128,2,256]{4,3,2,1,0:T(2,128)} custom-call(bf16[4,128,1024]{2,1,0:T(8,128)(2,1)S(1)} %collective-permute-done.refs_8_.refs_2_.refs_7_.refs_15_.refs_0_, bf16[4,128,1024]{2,1,0:T(8,128)(2,1)S(1)} %collective-permute-done.1.refs_9_.refs_11_.refs_8_.refs_10_.refs_16_.refs_18_.refs_1_.refs_3_, ...), custom_call_target="tpu_custom_call" | custom-call | tf_op jit(solution)/shard_map/closing/pallas_call | solution.py:562
  (21 shorter events, 0.1 us)
Async XLA Ops:
  0.0 1.0 copy-start
  1.2 1.0 copy-start.1
  2.4 13.6 %collective-permute-start.10 = (bf16[1,128,1024]{2,1,0:T(8,128)(2,1)S(1)}, bf16[1,128,1024]{2,1,0:T(8,128)(2,1)S(1)}, u32[]{:S(2)}, u32[]{:S(2)}) collective-permute-start(bf16[1,128,1024]{2,1,0:T(8,128)(2,1)S(1)} %get-tuple-element.13), channel_id=1, source_target_pairs={{2,0},{3,1},{10,8},{11,9},{20,22},{21,23},{28,30},{29,31}} | collective-permute-start | bytes 786440 | tf_op jit(solution)/shard_map/ppermute | solution.py:399
  3.7 26.9 %collective-permute-start.21 = (bf16[2,128,1024]{2,1,0:T(8,128)(2,1)S(1)}, bf16[2,128,1024]{2,1,0:T(8,128)(2,1)S(1)}, u32[]{:S(2)}, u32[]{:S(2)}) collective-permute-start(bf16[2,128,1024]{2,1,0:T(8,128)(2,1)S(1)} %flatten_occ.1.occ_flat_ref.refs_0_.refs_8_), channel_id=1, source_target_pairs={{0,2},{1,3},{2,0},{3,1},{4,6},{5,7},{6,4},{7,5},{8,10},{9,11},{10,... | collective-permute-start | bytes 1572872 | tf_op jit(solution)/shard_map/ppermute | solution.py:399
  6.9 29.4 %collective-permute-start = (bf16[4,128,1024]{2,1,0:T(8,128)(2,1)S(1)}, bf16[4,128,1024]{2,1,0:T(8,128)(2,1)S(1)}, u32[]{:S(2)}, u32[]{:S(2)}) collective-permute-start(bf16[4,128,1024]{2,1,0:T(8,128)(2,1)S(1)} %get-tuple-element.11), channel_id=1, source_target_pairs={{0,16},{1,17},{2,18},{3,19},{4,20},{5,21},{6,22},{7,23},{8,24},{9,... | collective-permute-start | bytes 3145736 | tf_op jit(solution)/shard_map/ppermute | solution.py:399
  7.7 25.3 %collective-permute-start.22 = (bf16[2,128,1024]{2,1,0:T(8,128)(2,1)S(1)}, bf16[2,128,1024]{2,1,0:T(8,128)(2,1)S(1)}, u32[]{:S(2)}, u32[]{:S(2)}) collective-permute-start(bf16[2,128,1024]{2,1,0:T(8,128)(2,1)S(1)} %flatten_occ.1.occ_flat_ref.refs_0_.refs_8_), channel_id=1, source_target_pairs={{2,4},{3,5},{4,2},{5,3},{10,12},{11,13},{12,10},{13,11},{18,20},{1... | collective-permute-start | bytes 1572872 | tf_op jit(solution)/shard_map/ppermute | solution.py:399
  8.4 25.9 %collective-permute-start.2 = (bf16[2,128,1024]{2,1,0:T(8,128)(2,1)S(1)}, bf16[2,128,1024]{2,1,0:T(8,128)(2,1)S(1)}, u32[]{:S(2)}, u32[]{:S(2)}) collective-permute-start(bf16[2,128,1024]{2,1,0:T(8,128)(2,1)S(1)} %get-tuple-element.12.refs_0_), channel_id=1, source_target_pairs={{0,2},{1,3},{4,6},{5,7},{6,4},{7,5},{8,10},{9,11},{12,14},{13,15},... | collective-permute-start | bytes 1572872 | tf_op jit(solution)/shard_map/ppermute | solution.py:399
  16.0 101.4 %copy-start.2 = (f32[2,8,512]{2,1,0:T(8,128)S(1)}, f32[2,8,512]{2,1,0:T(8,128)}, u32[]{:S(2)}) copy-start(f32[2,8,512]{2,1,0:T(8,128)} %levels_ref.1) | copy-start | bytes 98308
  16.1 101.4 %copy-start.3 = (s32[2,8,512]{2,1,0:T(8,128)S(1)}, s32[2,8,512]{2,1,0:T(8,128)}, u32[]{:S(2)}) copy-start(s32[2,8,512]{2,1,0:T(8,128)} %rank_ref.1) | copy-start | bytes 98308
  16.1 101.4 %copy-start.4 = (s32[2,8]{1,0:T(2,128)S(1)}, s32[2,8]{1,0:T(2,128)}, u32[]{:S(2)}) copy-start(s32[2,8]{1,0:T(2,128)} %map_ref.1) | copy-start | bytes 196
  16.1 101.4 %copy-start.5 = (f32[2]{0:T(128)S(1)}, f32[2]{0:T(128)}, u32[]{:S(2)}) copy-start(f32[2]{0:T(128)} %times_ref.1) | copy-start | bytes 28
  16.1 101.4 %copy-start.6 = (s32[8]{0:T(128)S(1)}, s32[8]{0:T(128)}, u32[]{:S(2)}) copy-start(s32[8]{0:T(128)} %kpoint_ref.1) | copy-start | bytes 100
  16.1 13.8 %collective-permute-start.11 = (bf16[1,128,1024]{2,1,0:T(8,128)(2,1)S(1)}, bf16[1,128,1024]{2,1,0:T(8,128)(2,1)S(1)}, u32[]{:S(2)}, u32[]{:S(2)}) collective-permute-start(bf16[1,128,1024]{2,1,0:T(8,128)(2,1)S(1)} %get-tuple-element.14), channel_id=1, source_target_pairs={{2,0},{3,1},{10,8},{11,9},{20,22},{21,23},{28,30},{29,31}} | collective-permute-start | bytes 786440 | tf_op jit(solution)/shard_map/ppermute | solution.py:399
  29.9 5.7 %collective-permute-start.5 = (bf16[2,128,1024]{2,1,0:T(8,128)(2,1)S(1)}, bf16[2,128,1024]{2,1,0:T(8,128)(2,1)S(1)}, u32[]{:S(2)}, u32[]{:S(2)}) collective-permute-start(bf16[2,128,1024]{2,1,0:T(8,128)(2,1)S(1)} %get-tuple-element.12.refs_0_), channel_id=1, source_target_pairs={{2,4},{3,5},{4,2},{5,3},{10,12},{11,13},{12,10},{13,11},{18,20},{1... | collective-permute-start | bytes 1572872 | tf_op jit(solution)/shard_map/ppermute | solution.py:399
  30.6 24.7 %collective-permute-start.17 = (bf16[4,128,1024]{2,1,0:T(8,128)(2,1)S(1)}, bf16[4,128,1024]{2,1,0:T(8,128)(2,1)S(1)}, u32[]{:S(2)}, u32[]{:S(2)}) collective-permute-start(bf16[4,128,1024]{2,1,0:T(8,128)(2,1)S(1)} %get-tuple-element.11), channel_id=1, source_target_pairs={{0,1},{1,0},{2,3},{3,2},{4,5},{5,4},{6,7},{7,6},{8,9},{9,8},{10,11... | collective-permute-start | bytes 3145736 | tf_op jit(solution)/shard_map/ppermute | solution.py:399
  33.0 16.7 %collective-permute-start.23 = (bf16[2,128,1024]{2,1,0:T(8,128)(2,1)S(1)}, bf16[2,128,1024]{2,1,0:T(8,128)(2,1)S(1)}, u32[]{:S(2)}, u32[]{:S(2)}) collective-permute-start(bf16[2,128,1024]{2,1,0:T(8,128)(2,1)S(1)} %collective-permute-done.21.refs_1_.refs_2_.refs_9_.refs_10_), channel_id=1, source_target_pairs={{2,4},{3,5},{4,2},{5,3},{6,22},{7,23},{10,12},{11,13},{12,10},{13,... | collective-permute-start | bytes 1572872 | tf_op jit(solution)/shard_map/ppermute | solution.py:399
  34.3 16.7 %collective-permute-start.26 = (bf16[2,128,1024]{2,1,0:T(8,128)(2,1)S(1)}, bf16[2,128,1024]{2,1,0:T(8,128)(2,1)S(1)}, u32[]{:S(2)}, u32[]{:S(2)}) collective-permute-start(bf16[2,128,1024]{2,1,0:T(8,128)(2,1)S(1)} %collective-permute-done.22.refs_3_.refs_11_), channel_id=1, source_target_pairs={{2,0},{3,1},{10,8},{11,9},{20,22},{21,23},{28,30},{29,31}} | collective-permute-start | bytes 1572872 | tf_op jit(solution)/shard_map/ppermute | solution.py:399
  35.6 16.1 %collective-permute-start.24 = (bf16[2,128,1024]{2,1,0:T(8,128)(2,1)S(1)}, bf16[2,128,1024]{2,1,0:T(8,128)(2,1)S(1)}, u32[]{:S(2)}, u32[]{:S(2)}) collective-permute-start(bf16[2,128,1024]{2,1,0:T(8,128)(2,1)S(1)} %collective-permute-done.22.refs_3_.refs_11_), channel_id=1, source_target_pairs={{4,6},{5,7},{12,14},{13,15},{18,16},{19,17},{26,24},{27,25}} | collective-permute-start | bytes 1572872 | tf_op jit(solution)/shard_map/ppermute | solution.py:399
  36.3 22.3 %collective-permute-start.3 = (bf16[2,128,1024]{2,1,0:T(8,128)(2,1)S(1)}, bf16[2,128,1024]{2,1,0:T(8,128)(2,1)S(1)}, u32[]{:S(2)}, u32[]{:S(2)}) collective-permute-start(bf16[2,128,1024]{2,1,0:T(8,128)(2,1)S(1)} %collective-permute-done.2.refs_1_), channel_id=1, source_target_pairs={{2,4},{3,5},{4,2},{5,3},{6,22},{7,23},{10,12},{11,13},{12,10},{13,... | collective-permute-start | bytes 1572872 | tf_op jit(solution)/shard_map/ppermute | solution.py:399
  49.7 21.7 %collective-permute-start.6 = (bf16[2,128,1024]{2,1,0:T(8,128)(2,1)S(1)}, bf16[2,128,1024]{2,1,0:T(8,128)(2,1)S(1)}, u32[]{:S(2)}, u32[]{:S(2)}) collective-permute-start(bf16[2,128,1024]{2,1,0:T(8,128)(2,1)S(1)} %collective-permute-done.5.refs_4_), channel_id=1, source_target_pairs={{2,0},{3,1},{10,8},{11,9},{20,22},{21,23},{28,30},{29,31}} | collective-permute-start | bytes 1572872 | tf_op jit(solution)/shard_map/ppermute | solution.py:399
  51.0 22.0 %collective-permute-start.12 = (bf16[2,128,1024]{2,1,0:T(8,128)(2,1)S(1)}, bf16[2,128,1024]{2,1,0:T(8,128)(2,1)S(1)}, u32[]{:S(2)}, u32[]{:S(2)}) collective-permute-start(bf16[2,128,1024]{2,1,0:T(8,128)(2,1)S(1)} %collective-permute-done.5.refs_4_), channel_id=1, source_target_pairs={{4,6},{5,7},{12,14},{13,15},{18,16},{19,17},{26,24},{27,25}} | collective-permute-start | bytes 1572872 | tf_op jit(solution)/shard_map/ppermute | solution.py:399
  51.7 27.0 %collective-permute-start.28 = (bf16[2,128,1024]{2,1,0:T(8,128)(2,1)S(1)}, bf16[2,128,1024]{2,1,0:T(8,128)(2,1)S(1)}, u32[]{:S(2)}, u32[]{:S(2)}) collective-permute-start(bf16[2,128,1024]{2,1,0:T(8,128)(2,1)S(1)} %collective-permute-done.23.refs_4_.refs_9_.refs_12_.refs_17_), channel_id=1, source_target_pairs={{2,0},{3,1},{10,8},{11,9},{20,22},{21,23},{28,30},{29,31}} | collective-permute-start | bytes 1572872 | tf_op jit(solution)/shard_map/ppermute | solution.py:399
  55.3 25.1 %collective-permute-start.25 = (bf16[2,128,1024]{2,1,0:T(8,128)(2,1)S(1)}, bf16[2,128,1024]{2,1,0:T(8,128)(2,1)S(1)}, u32[]{:S(2)}, u32[]{:S(2)}) collective-permute-start(bf16[2,128,1024]{2,1,0:T(8,128)(2,1)S(1)} %collective-permute-done.23.refs_4_.refs_9_.refs_12_.refs_17_), channel_id=1, source_target_pairs={{2,18},{3,19},{4,6},{5,7},{10,26},{11,27},{12,14},{13,15},{18,16},... | collective-permute-start | bytes 1572872 | tf_op jit(solution)/shard_map/ppermute | solution.py:399
  58.6 21.8 %collective-permute-start.27 = (bf16[2,128,1024]{2,1,0:T(8,128)(2,1)S(1)}, bf16[2,128,1024]{2,1,0:T(8,128)(2,1)S(1)}, u32[]{:S(2)}, u32[]{:S(2)}) collective-permute-start(bf16[2,128,1024]{2,1,0:T(8,128)(2,1)S(1)} %collective-permute-done.26), channel_id=1, source_target_pairs={{0,16},{1,17},{8,24},{9,25},{22,6},{23,7},{30,14},{31,15}} | collective-permute-start | bytes 1572872 | tf_op jit(solution)/shard_map/ppermute | solution.py:399
  71.4 30.4 %collective-permute-start.1 = (bf16[4,128,1024]{2,1,0:T(8,128)(2,1)S(1)}, bf16[4,128,1024]{2,1,0:T(8,128)(2,1)S(1)}, u32[]{:S(2)}, u32[]{:S(2)}) collective-permute-start(bf16[4,128,1024]{2,1,0:T(8,128)(2,1)S(1)} %collective-permute-done.refs_8_.refs_2_.refs_7_.refs_15_.refs_0_), channel_id=1, source_target_pairs={{0,2},{1,3},{2,4},{3,5},{8,10},{9,11},{10,12},{11,13},{20,18},{21,... | collective-permute-start | bytes 3145736 | tf_op jit(solution)/shard_map/ppermute | solution.py:399
  72.9 15.3 %collective-permute-start.4 = (bf16[2,128,1024]{2,1,0:T(8,128)(2,1)S(1)}, bf16[2,128,1024]{2,1,0:T(8,128)(2,1)S(1)}, u32[]{:S(2)}, u32[]{:S(2)}) collective-permute-start(bf16[2,128,1024]{2,1,0:T(8,128)(2,1)S(1)} %collective-permute-done.3.refs_5_.refs_10_.refs_2_), channel_id=1, source_target_pairs={{2,18},{3,19},{4,6},{5,7},{10,26},{11,27},{12,14},{13,15},{18,16},... | collective-permute-start | bytes 1572872 | tf_op jit(solution)/shard_map/ppermute | solution.py:399
  78.6 32.8 %collective-permute-start.19 = (bf16[4,128,1024]{2,1,0:T(8,128)(2,1)S(1)}, bf16[4,128,1024]{2,1,0:T(8,128)(2,1)S(1)}, u32[]{:S(2)}, u32[]{:S(2)}) collective-permute-start(bf16[4,128,1024]{2,1,0:T(8,128)(2,1)S(1)} %collective-permute-done.refs_8_.refs_2_.refs_7_.refs_15_.refs_0_), channel_id=1, source_target_pairs={{0,1},{1,0},{2,3},{3,2},{4,5},{5,4},{6,7},{7,6},{8,9},{9,8},{10,11... | collective-permute-start | bytes 3145736 | tf_op jit(solution)/shard_map/ppermute | solution.py:399
  80.4 31.7 %collective-permute-start.15 = (bf16[4,128,1024]{2,1,0:T(8,128)(2,1)S(1)}, bf16[4,128,1024]{2,1,0:T(8,128)(2,1)S(1)}, u32[]{:S(2)}, u32[]{:S(2)}) collective-permute-start(bf16[4,128,1024]{2,1,0:T(8,128)(2,1)S(1)} %get-tuple-element.11), channel_id=1, source_target_pairs={{0,8},{1,9},{2,10},{3,11},{4,12},{5,13},{6,14},{7,15},{8,0},{9,1},... | collective-permute-start | bytes 3145736 | tf_op jit(solution)/shard_map/ppermute | solution.py:399
  80.4 20.1 %collective-permute-start.7 = (bf16[2,128,1024]{2,1,0:T(8,128)(2,1)S(1)}, bf16[2,128,1024]{2,1,0:T(8,128)(2,1)S(1)}, u32[]{:S(2)}, u32[]{:S(2)}) collective-permute-start(bf16[2,128,1024]{2,1,0:T(8,128)(2,1)S(1)} %collective-permute-done.6), channel_id=1, source_target_pairs={{0,16},{1,17},{8,24},{9,25},{22,6},{23,7},{30,14},{31,15}} | collective-permute-start | bytes 1572872 | tf_op jit(solution)/shard_map/ppermute | solution.py:399
  88.3 23.0 %collective-permute-start.29 = (bf16[2,128,1024]{2,1,0:T(8,128)(2,1)S(1)}, bf16[2,128,1024]{2,1,0:T(8,128)(2,1)S(1)}, u32[]{:S(2)}, u32[]{:S(2)}) collective-permute-start(bf16[2,128,1024]{2,1,0:T(8,128)(2,1)S(1)} %collective-permute-done.28), channel_id=1, source_target_pairs={{0,16},{1,17},{8,24},{9,25},{22,6},{23,7},{30,14},{31,15}} | collective-permute-start | bytes 1572872 | tf_op jit(solution)/shard_map/ppermute | solution.py:399
  100.5 14.9 %collective-permute-start.8 = (bf16[2,128,1024]{2,1,0:T(8,128)(2,1)S(1)}, bf16[2,128,1024]{2,1,0:T(8,128)(2,1)S(1)}, u32[]{:S(2)}, u32[]{:S(2)}) collective-permute-start(bf16[2,128,1024]{2,1,0:T(8,128)(2,1)S(1)} %collective-permute-done.3.refs_5_.refs_10_.refs_2_), channel_id=1, source_target_pairs={{2,0},{3,1},{10,8},{11,9},{20,22},{21,23},{28,30},{29,31}} | collective-permute-start | bytes 1572872 | tf_op jit(solution)/shard_map/ppermute | solution.py:399
  101.8 13.6 %collective-permute-start.16 = (bf16[4,128,1024]{2,1,0:T(8,128)(2,1)S(1)}, bf16[4,128,1024]{2,1,0:T(8,128)(2,1)S(1)}, u32[]{:S(2)}, u32[]{:S(2)}) collective-permute-start(bf16[4,128,1024]{2,1,0:T(8,128)(2,1)S(1)} %collective-permute-done.refs_8_.refs_2_.refs_7_.refs_15_.refs_0_), channel_id=1, source_target_pairs={{0,8},{1,9},{2,10},{3,11},{4,12},{5,13},{6,14},{7,15},{8,0},{9,1},... | collective-permute-start | bytes 3145736 | tf_op jit(solution)/shard_map/ppermute | solution.py:399
  111.3 5.5 %collective-permute-start.18 = (bf16[4,128,1024]{2,1,0:T(8,128)(2,1)S(1)}, bf16[4,128,1024]{2,1,0:T(8,128)(2,1)S(1)}, u32[]{:S(2)}, u32[]{:S(2)}) collective-permute-start(bf16[4,128,1024]{2,1,0:T(8,128)(2,1)S(1)} %collective-permute-done.17.refs_4_), channel_id=1, source_target_pairs={{0,8},{1,9},{2,10},{3,11},{4,12},{5,13},{6,14},{7,15},{8,0},{9,1},... | collective-permute-start | bytes 3145736 | tf_op jit(solution)/shard_map/ppermute | solution.py:399
  111.4 7.5 %collective-permute-start.20 = (bf16[4,128,1024]{2,1,0:T(8,128)(2,1)S(1)}, bf16[4,128,1024]{2,1,0:T(8,128)(2,1)S(1)}, u32[]{:S(2)}, u32[]{:S(2)}) collective-permute-start(bf16[4,128,1024]{2,1,0:T(8,128)(2,1)S(1)} %collective-permute-done.19.refs_6_), channel_id=1, source_target_pairs={{0,8},{1,9},{2,10},{3,11},{4,12},{5,13},{6,14},{7,15},{8,0},{9,1},... | collective-permute-start | bytes 3145736 | tf_op jit(solution)/shard_map/ppermute | solution.py:399
  112.1 8.6 %collective-permute-start.30 = (bf16[2,2,128,1024]{3,2,1,0:T(8,128)(2,1)S(1)}, bf16[2,2,128,1024]{3,2,1,0:T(8,128)(2,1)S(1)}, u32[]{:S(2)}, u32[]{:S(2)}) collective-permute-start(bf16[2,2,128,1024]{3,2,1,0:T(8,128)(2,1)S(1)} %shard_map.74), channel_id=1, source_target_pairs={{0,8},{1,9},{2,10},{3,11},{4,12},{5,13},{6,14},{7,15},{8,0},{9,1},... | collective-permute-start | bytes 3145736 | tf_op jit(solution)/shard_map/ppermute | solution.py:399
  115.4 9.0 %collective-permute-start.13 = (bf16[2,2,128,1024]{3,2,1,0:T(8,128)(2,1)S(1)}, bf16[2,2,128,1024]{3,2,1,0:T(8,128)(2,1)S(1)}, u32[]{:S(2)}, u32[]{:S(2)}) collective-permute-start(bf16[2,2,128,1024]{3,2,1,0:T(8,128)(2,1)S(1)} %shard_map.73), channel_id=1, source_target_pairs={{0,8},{1,9},{2,10},{3,11},{4,12},{5,13},{6,14},{7,15},{8,0},{9,1},... | collective-permute-start | bytes 3145736 | tf_op jit(solution)/shard_map/ppermute | solution.py:399
  115.4 12.9 %collective-permute-start.14 = (bf16[2,128,1024]{2,1,0:T(8,128)(2,1)S(1)}, bf16[2,128,1024]{2,1,0:T(8,128)(2,1)S(1)}, u32[]{:S(2)}, u32[]{:S(2)}) collective-permute-start(bf16[2,128,1024]{2,1,0:T(8,128)(2,1)S(1)} %collective-permute-done.8), channel_id=1, source_target_pairs={{0,24},{1,25},{30,6},{31,7}} | collective-permute-start | bytes 1572872 | tf_op jit(solution)/shard_map/ppermute | solution.py:399
  116.8 11.5 %collective-permute-start.9 = (bf16[2,128,1024]{2,1,0:T(8,128)(2,1)S(1)}, bf16[2,128,1024]{2,1,0:T(8,128)(2,1)S(1)}, u32[]{:S(2)}, u32[]{:S(2)}) collective-permute-start(bf16[2,128,1024]{2,1,0:T(8,128)(2,1)S(1)} %collective-permute-done.8), channel_id=1, source_target_pairs={{8,24},{9,25},{22,6},{23,7}} | collective-permute-start | bytes 1572872 | tf_op jit(solution)/shard_map/ppermute | solution.py:399

commit v2 on v1

--- a/solution.py
+++ b/solution.py
@@ -108,7 +108,7 @@
 HBM = pl.BlockSpec(memory_space=pltpu.HBM)
 VMEM = pl.BlockSpec(memory_space=pltpu.VMEM)
 SMEM = pl.BlockSpec(memory_space=pltpu.SMEM)
-LIMIT = pltpu.CompilerParams(vmem_limit_bytes=24 * 2**20)
+LIMIT = pltpu.CompilerParams(vmem_limit_bytes=16 * 2**20)
 AXES = ("kgrp", "row", "col")
 
 
@@ -117,7 +117,15 @@
     return lax.div(group, 2), lax.rem(group, 2), lax.axis_index("row"), lax.axis_index("col")
 
 
-def prep_kernel(levels_ref, rank_ref, times_ref, map_ref, kpoint_ref, weight_ref, pair_ref, slot_of):
+def prep_kernel(levels_in, rank_in, times_ref, map_ref, kpoint_ref, weight_ref, pair_ref, slot_of, levels_ref, rank_ref, sems):
+    copies = [
+        pltpu.make_async_copy(levels_in, levels_ref, sems.at[0]),
+        pltpu.make_async_copy(rank_in, rank_ref, sems.at[1]),
+    ]
+    for copy in copies:
+        copy.start()
+    for copy in copies:
+        copy.wait()
     bands = levels_ref.shape[2]
     times = weight_ref.shape[1]
     for kind in range(2):
@@ -233,7 +241,7 @@
     for k in groups:
         if k & 1:
             inside = recv.at[k >> 1]
-            if last is None:
+            if last is None or k == 1:
                 fetch(inside, k)
             else:
                 pl.when(keep == 6)(functools.partial(fetch, last, k))
@@ -281,19 +289,16 @@
 
 
 def occ_kernel(cases, *refs):
-    rows, direct, crossed = refs[:8], refs[8 : 8 + cases], refs[8 + cases : 8 + 2 * cases]
-    recv, weight_ref, out_ref, row_buf, col_buf, sems = refs[8 + 2 * cases :]
-    load_columns(0, range(4), direct, crossed, recv, None, col_buf, sems)
-    load_rows(0, range(4), rows, row_buf, sems)
+    direct, crossed = refs[:cases], refs[cases : 2 * cases]
+    recv, last, scaled_ref, out_ref, col_buf, sems = refs[2 * cases :]
+    load_columns(0, range(4), direct, crossed, recv, last, col_buf, sems)
     per_group = col_buf.shape[1]
     for k in range(4):
         wait_columns(k, col_buf, sems)
-        wait_rows(k, row_buf, sems)
         for i in range(per_group):
             stacked = stack_columns(col_buf[k, i])
             for half in range(2):
-                scaled = scale_rows(0, k, i, half, row_buf, weight_ref)
-                out_ref[k * per_group + i, half] = tile(stacked, scaled)
+                out_ref[k * per_group + i, half] = tile(stacked, scaled_ref[half, k, i])
 
 
 STRIP = 16
@@ -327,14 +332,14 @@
         lax.fori_loop(0, block // STRIP, strip, 0)
 
 
-def scale_kernel(*refs):
+def scale_kernel(kind, *refs):
     rows, weight_ref, scaled_ref, row_buf, sems = refs[:8], *refs[8:]
-    load_rows(1, range(4), rows, row_buf, sems)
+    load_rows(kind, range(4), rows, row_buf, sems)
     for k in range(4):
         wait_rows(k, row_buf, sems)
         for i in range(row_buf.shape[2]):
             for half in range(2):
-                scaled_ref[half, k, i] = scale_rows(1, k, i, half, row_buf, weight_ref)
+                scaled_ref[half, k, i] = scale_rows(kind, k, i, half, row_buf, weight_ref)
 
 
 def emp_direct_kernel(cases, *refs):
@@ -356,8 +361,9 @@
 
 
 def closing_kernel(factor, cases, *refs):
-    crossed = refs[:cases]
-    recv, last, scaled_ref, pair_ref, occ_ref, sum_ref, out_ref, col_buf, moved, sems = refs[cases:]
+    crossed = list(refs[: cases - 1]) + [refs[cases - 1 : cases + 1]]
+    recv, scaled_ref, pair_ref, occ_ref, sum_ref, out_ref, col_buf, moved, sems = refs[cases + 1 : cases + 2] + refs[cases + 4 :]
+    last = refs[cases + 2 : cases + 4]
     load_columns(1, (2, 3), None, crossed, recv, last, col_buf, sems)
     per_group, block = col_buf.shape[1:3]
     times = out_ref.shape[3]
@@ -435,6 +441,9 @@
             return None
         return (x, h, top - z, y) if inner(z) else (x, h, z ^ 1, y)
 
+    def inward_near(x, h, z, y):
+        return (x, h, z ^ 1, y) if near(x, z) and not inner(z) else None
+
     def to_far_or_outward(x, h, z, y):
         if not inner(z):
             return None
@@ -450,6 +459,17 @@
     def to_other_owner(x, h, z, y):
         owner = h != z // half
         return None if owner or inner(z) or not near(x, z) else (1 - x, 1 - h, z, y)
+
+    def outward_owner(x, h, z, y):
+        owner = h != z // half
+        return (x, h, z ^ 1, y) if inner(z) and not near(x, z) and owner else None
+
+    def outward_other(x, h, z, y):
+        owner = h != z // half
+        return None if owner or near(x, z) or not inner(z) else (x, 1 - h, z ^ 1, y)
+
+    def to_far_inner(x, h, z, y):
+        return (1 - x, h, z, y) if near(x, z) and inner(z) else None
 
     def flip_y(x, h, z, y):
         return x, h, z, 1 - y
@@ -483,9 +503,14 @@
             jax.ShapeDtypeStruct((2, times, kpoints, width), jnp.float32),
             jax.ShapeDtypeStruct((transfers, kpoints), jnp.int32),
         ],
-        in_specs=[VMEM, VMEM, SMEM, SMEM, SMEM],
+        in_specs=[HBM, HBM, SMEM, SMEM, SMEM],
         out_specs=[VMEM, SMEM],
-        scratch_shapes=[pltpu.SMEM((kpoints,), jnp.int32)],
+        scratch_shapes=[
+            pltpu.SMEM((kpoints,), jnp.int32),
+            pltpu.VMEM(energies.shape, energies.dtype),
+            pltpu.VMEM(band_order.shape, band_order.dtype),
+            pltpu.SemaphoreType.DMA((2,)),
+        ],
         compiler_params=LIMIT,
         name="prep",
     )
@@ -499,17 +524,21 @@
     sibling = send(both, flip_core)
     d = [send(s1[i], middle_or_to_near) for i in range(2)]
     en = [send(b[i], outward_near) for i in range(2)]
-    e = [send(b[i], outward_far) for i in range(2)]
-    bx = send(crossed, from_near)
+    e = [send(b[0], to_far_or_outward), send(b[1], outward_far)]
+    bx = [send(crossed[:slots], inward_near), send(crossed[slots:], from_near)]
     turned_crossed = send(crossed, flip_y)
     crossed_sibling = send(crossed, flip_core)
     turned_sibling = send(turned, flip_core)
     turned_crossed_sibling = send(turned_crossed, flip_core)
     ex = [send(en[i], to_far_outer) for i in range(2)]
-    fn = [send(d[i], outward_near) for i in range(2)]
-    f = [send(d[i], to_far_or_outward) for i in range(2)]
-    fx = [send(fn[0], to_far_outer), send(fn[1], to_owner)]
-    last = send(fn[1], to_other_owner)
+    head = slots // 2
+    fn = [send(d[0], outward_near), send(d[1][:head], outward_near)]
+    f = [send(d[0], to_far_or_outward), send(d[1], outward_far)]
+    dx = [f[0], send(d[1], to_far_inner)]
+    fx = [send(fn[0], to_owner), send(fn[1], to_owner)]
+    rest = dx[1][head:]
+    last = [[send(fn[0], to_other_owner)], [send(fn[1], to_other_owner), send(rest, outward_other)]]
+    outer_rest = send(rest, outward_owner)
     row_panels, direct, across, given = [], [], [], []
     for kind in range(2):
         row_panels.append([
@@ -518,8 +547,8 @@
         ])
         swapped = late if kind else s1[:1]
         direct.append([kinds[kind], s1[kind], *swapped, b[kind], d[kind], e[kind], f[kind]])
-        across.append([crossed, bx, d[kind], bx, f[kind], ex[kind], fx[kind]])
-        ready = across[kind][:-1] + [ex[1] if kind else fx[0]]
+        across.append([crossed, bx[kind], d[kind], bx[1] if kind else e[0], dx[kind], ex[kind], fx[kind]] + [outer_rest] * kind)
+        ready = across[kind][:6] + [ex[kind]]
         give = pack(kind, direct[kind], ready, (slots, block, width))
         given.append(send(give, flip_core))
 
@@ -528,27 +557,28 @@
         pltpu.VMEM((4, slots, block, width), jnp.bfloat16),
     ]
     cases = len(across[0])
+    scaled = []
+    for kind in range(2):
+        scale = pl.pallas_call(
+            functools.partial(scale_kernel, kind),
+            out_shape=jax.ShapeDtypeStruct((2, 4, slots, times * block, width), jnp.bfloat16),
+            in_specs=[HBM] * 8 + [VMEM],
+            out_specs=VMEM,
+            scratch_shapes=panel_scratch[:1] + [pltpu.SemaphoreType.DMA((4, 3))],
+            compiler_params=LIMIT,
+        )
+        scaled.append(scale(*row_panels[kind], weights))
     occ_tiles = pl.pallas_call(
         functools.partial(occ_kernel, cases),
         out_shape=jax.ShapeDtypeStruct((kpoints, 2, 2 * block, times * block), jnp.float32),
-        in_specs=[HBM] * (9 + 2 * cases) + [VMEM],
+        in_specs=[HBM] * (2 + 2 * cases) + [VMEM],
         out_specs=VMEM,
-        scratch_shapes=panel_scratch + [pltpu.SemaphoreType.DMA((4, 3))],
+        scratch_shapes=panel_scratch[1:] + [pltpu.SemaphoreType.DMA((4, 3))],
         compiler_params=LIMIT,
         name="occ_tiles",
     )
-    tiles = occ_tiles(*row_panels[0], *direct[0], *across[0], given[0], weights)
+    tiles = occ_tiles(*direct[0], *across[0], given[0], *last[0], scaled[0])
     half_tiles = (kpoints // 2, 2, 2 * block, times * block)
-    scale = pl.pallas_call(
-        scale_kernel,
-        out_shape=jax.ShapeDtypeStruct((2, 4, slots, times * block, width), jnp.bfloat16),
-        in_specs=[HBM] * 8 + [VMEM],
-        out_specs=VMEM,
-        scratch_shapes=panel_scratch[:1] + [pltpu.SemaphoreType.DMA((4, 3))],
-        compiler_params=LIMIT,
-        name="scale",
-    )
-    scaled = scale(*row_panels[1], weights)
     emp_direct = pl.pallas_call(
         functools.partial(emp_direct_kernel, cases),
         out_shape=jax.ShapeDtypeStruct((transfers, 2, 2, block, times * block), jnp.float32),
@@ -558,16 +588,16 @@
         compiler_params=LIMIT,
         name="emp_direct",
     )
-    sums = emp_direct(*direct[1], given[1], scaled, pairs, tiles)
+    sums = emp_direct(*direct[1], given[1], scaled[1], pairs, tiles)
     result = pl.pallas_call(
         functools.partial(closing_kernel, -1.0 / kpoints, cases),
         out_shape=jax.ShapeDtypeStruct((2, transfers, block, times, cols * block), jnp.float32),
-        in_specs=[HBM] * (2 + cases) + [VMEM, SMEM, VMEM, VMEM],
+        in_specs=[HBM] * (4 + cases) + [VMEM, SMEM, VMEM, VMEM],
         out_specs=VMEM,
         scratch_shapes=panel_scratch[1:] + [pltpu.VMEM(half_tiles, jnp.float32), pltpu.SemaphoreType.DMA((4, 3))],
         compiler_params=LIMIT,
         name="closing",
-    )(*across[1], given[1], last, scaled, pairs, tiles, sums)
+    )(*across[1], given[1], *last[1], scaled[1], pairs, tiles, sums)
     return result[:, :, None]
 
 

time: 134 us -> 147 us (1.097)
  waiting for transfers between devices: 61.2 us -> 75.8 us
  starting transfers between devices: 54.1 us -> 51.1 us
  Pallas kernels: 15 us -> 16.7 us
    ppermute x31 -> x36, waiting for transfers between devices: 61.2 us -> 75.8 us  [send(): return lax.ppermute(array, AXES, pairs)]
    ppermute x31 -> x36, starting transfers between devices: 54.1 us -> 51.1 us  [send(): return lax.ppermute(array, AXES, pairs)]
    pallas_call x3 -> x4, Pallas kernels: 8.55 us -> 10.1 us  [the longest x2 3.66 us: output_stationary(): scaled.append(scale(*row_panels[kind], weights))]
  transfers between devices with their start and end apart: 31 -> 36, of which waited for: 10 -> 11; matrix products, arithmetic and copies ran while one was open for 0% -> 0% of each run, Pallas kernels for 8% -> 8%
where the time goes in v2:
time: 147 us
  waiting for transfers between devices  75.8 us (52%)
  starting transfers between devices  51.1 us (35%)
  Pallas kernels  16.7 us (11%)
  local copies, waits for them, and re-layouts  2.24 us (2%)
    ppermute x36, waiting for transfers between devices, send(): return lax.ppermute(array, AXES, pairs)  75.8 us
    ppermute x36, starting transfers between devices, send(): return lax.ppermute(array, AXES, pairs)  51.1 us
    pallas_call x1, Pallas kernels, output_stationary(): pl.pallas_call(functools.partial(closing_kernel, -1.0 / kpoints, cases),...  4.55 us
    pallas_call x2, Pallas kernels, output_stationary(): scaled.append(scale(*row_panels[kind], weights))  3.66 us
    pallas_call x1, Pallas kernels, output_stationary(): tiles = occ_tiles(*direct[0], *across[0], given[0], *last[0], scaled[0])  3.31 us
    pallas_call x1, Pallas kernels, output_stationary(): sums = emp_direct(*direct[1], given[1], scaled[1], pairs, tiles)  3.15 us
  transfers between devices with their start and end apart: 36, of which 11 were waited for; matrix products, arithmetic and copies ran while one was open for 0% of the time, Pallas kernels for 8%

profile of v2, /device:TPU:0, one launch (start us, length us, event | category | flops | bytes accessed | tf_op | source)
XLA Modules:
  0.0 146.5 jit_solution(8043375151084488109)
XLA Ops:
  0.0 1.0 copy-done
  1.0 0.2 flatten_occ.1.occ_flat_ref.refs_0_
  1.2 3.1 %collective-permute-start.24 = (bf16[2,128,1024]{2,1,0:T(8,128)(2,1)S(1)}, bf16[2,128,1024]{2,1,0:T(8,128)(2,1)S(1)}, u32[]{:S(2)}, u32[]{:S(2)}) collective-permute-start(bf16[2,128,1024]{2,1,0:T(8,128)(2,1)S(1)} %flatten_occ.1.occ_flat_ref.refs_0_), channel_id=1, source_target_pairs={{0,2},{1,3},{2,0},{3,1},{4,6},{5,7},{6,4},{7,5},{8,10},{9,11},{10,... | collective-permute-start | bytes 1572872 | tf_op jit(solution)/shard_map/ppermute | solution.py:405
  4.3 1.0 copy-done.1
  5.4 0.2 flatten_emp.1
  5.5 1.3 collective-permute-start.11
  6.8 1.3 collective-permute-start.12
  8.1 0.7 collective-permute-start.25
  8.8 0.3 collective-permute-start
  9.2 13.5 %collective-permute-done.11.refs_2_ = bf16[1,128,1024]{2,1,0:T(8,128)(2,1)S(1)} collective-permute-done((bf16[1,128,1024]{2,1,0:T(8,128)(2,1)S(1)}, bf16[1,128,1024]{2,1,0:T(8,128)(2,1)S(1)}, u32[]{:S(2)}, u32[]{:S(2)}) %collective-permute-start.11) | collective-permute-done | bytes 262176 | tf_op jit(solution)/shard_map/ppermute | solution.py:405
  22.7 2.0 %collective-permute-start.20 = (bf16[4,128,1024]{2,1,0:T(8,128)(2,1)S(1)}, bf16[4,128,1024]{2,1,0:T(8,128)(2,1)S(1)}, u32[]{:S(2)}, u32[]{:S(2)}) collective-permute-start(bf16[4,128,1024]{2,1,0:T(8,128)(2,1)S(1)} %get-tuple-element.11), channel_id=1, source_target_pairs={{0,1},{1,0},{2,3},{3,2},{4,5},{5,4},{6,7},{7,6},{8,9},{9,8},{10,11... | collective-permute-start | bytes 3145736 | tf_op jit(solution)/shard_map/ppermute | solution.py:405
  24.7 2.8 %collective-permute-done.12.refs_3_ = bf16[1,128,1024]{2,1,0:T(8,128)(2,1)S(1)} collective-permute-done((bf16[1,128,1024]{2,1,0:T(8,128)(2,1)S(1)}, bf16[1,128,1024]{2,1,0:T(8,128)(2,1)S(1)}, u32[]{:S(2)}, u32[]{:S(2)}) %collective-permute-start.12) | collective-permute-done | bytes 262176 | tf_op jit(solution)/shard_map/ppermute | solution.py:405
  27.5 1.5 %collective-permute-start.2 = (bf16[2,128,1024]{2,1,0:T(8,128)(2,1)S(1)}, bf16[2,128,1024]{2,1,0:T(8,128)(2,1)S(1)}, u32[]{:S(2)}, u32[]{:S(2)}) collective-permute-start(bf16[2,128,1024]{2,1,0:T(8,128)(2,1)S(1)} %get-tuple-element.12.refs_0_), channel_id=1, source_target_pairs={{0,2},{1,3},{4,6},{5,7},{6,4},{7,5},{8,10},{9,11},{12,14},{13,15},... | collective-permute-start | bytes 1572872 | tf_op jit(solution)/shard_map/ppermute | solution.py:405
  29.0 0.7 collective-permute-start.5
  29.7 11.2 %collective-permute-done.2.refs_1_ = bf16[2,128,1024]{2,1,0:T(8,128)(2,1)S(1)} collective-permute-done((bf16[2,128,1024]{2,1,0:T(8,128)(2,1)S(1)}, bf16[2,128,1024]{2,1,0:T(8,128)(2,1)S(1)}, u32[]{:S(2)}, u32[]{:S(2)}) %collective-permute-start.2) | collective-permute-done | bytes 524320 | tf_op jit(solution)/shard_map/ppermute | solution.py:405
  40.9 1.3 collective-permute-start.26
  42.2 1.3 collective-permute-start.3
  43.5 0.0 collective-permute-done.refs_8_.refs_2_.refs_7_.refs_0_
  43.5 1.3 collective-permute-start.30
  44.8 1.4 collective-permute-done.20.refs_4_
  46.2 0.7 collective-permute-start.27
  46.9 1.3 collective-permute-start.6
  48.2 9.4 %collective-permute-done.26.refs_4_.refs_9_ = bf16[2,128,1024]{2,1,0:T(8,128)(2,1)S(1)} collective-permute-done((bf16[2,128,1024]{2,1,0:T(8,128)(2,1)S(1)}, bf16[2,128,1024]{2,1,0:T(8,128)(2,1)S(1)}, u32[]{:S(2)}, u32[]{:S(2)}) %collective-permute-start.26) | collective-permute-done | bytes 524320 | tf_op jit(solution)/shard_map/ppermute | solution.py:405
  57.6 0.7 collective-permute-start.13
  58.3 0.1 fusion
  58.4 9.2 %collective-permute-done.3.refs_5_.refs_10_.refs_2_ = bf16[2,128,1024]{2,1,0:T(8,128)(2,1)S(1)} collective-permute-done((bf16[2,128,1024]{2,1,0:T(8,128)(2,1)S(1)}, bf16[2,128,1024]{2,1,0:T(8,128)(2,1)S(1)}, u32[]{:S(2)}, u32[]{:S(2)}) %collective-permute-start.3) | collective-permute-done | bytes 524320 | tf_op jit(solution)/shard_map/ppermute | solution.py:405
  67.6 4.4 %collective-permute-start.29 = (bf16[2,128,1024]{2,1,0:T(8,128)(2,1)S(1)}, bf16[2,128,1024]{2,1,0:T(8,128)(2,1)S(1)}, u32[]{:S(2)}, u32[]{:S(2)}) collective-permute-start(bf16[2,128,1024]{2,1,0:T(8,128)(2,1)S(1)} %get-tuple-element.17), channel_id=1, source_target_pairs={{0,2},{1,3},{8,10},{9,11},{22,20},{23,21},{30,28},{31,29}} | collective-permute-start | bytes 1572872 | tf_op jit(solution)/shard_map/ppermute | solution.py:405
  72.0 0.0 collective-permute-done.30
  72.1 0.7 collective-permute-start.28
  72.8 0.0 collective-permute-done.27.refs_5_.refs_10_
  72.8 1.3 collective-permute-start.8
  74.1 0.0 collective-permute-done.6
  74.1 1.3 collective-permute-start.31
  75.4 0.0 collective-permute-done.13.refs_6_
  75.4 0.7 collective-permute-start.4
  76.1 5.9 %collective-permute-done.8 = bf16[1,128,1024]{2,1,0:T(8,128)(2,1)S(1)} collective-permute-done((bf16[1,128,1024]{2,1,0:T(8,128)(2,1)S(1)}, bf16[1,128,1024]{2,1,0:T(8,128)(2,1)S(1)}, u32[]{:S(2)}, u32[]{:S(2)}) %collective-permute-start.8) | collective-permute-done | bytes 262176 | tf_op jit(solution)/shard_map/ppermute | solution.py:405
  82.1 0.0 copy-start.6
  82.1 1.6 %collective-permute-start.1 = (bf16[2,128,1024]{2,1,0:T(8,128)(2,1)S(1)}, bf16[2,128,1024]{2,1,0:T(8,128)(2,1)S(1)}, u32[]{:S(2)}, u32[]{:S(2)}) collective-permute-start(bf16[2,128,1024]{2,1,0:T(8,128)(2,1)S(1)} %get-tuple-element.18), channel_id=1, source_target_pairs={{0,2},{1,3},{2,4},{3,5},{8,10},{9,11},{10,12},{11,13},{20,18},{21,... | collective-permute-start | bytes 1572872 | tf_op jit(solution)/shard_map/ppermute | solution.py:405
  83.7 0.0 collective-permute-done.29.refs_8_
  83.7 1.6 %collective-permute-start.22 = (bf16[4,128,1024]{2,1,0:T(8,128)(2,1)S(1)}, bf16[4,128,1024]{2,1,0:T(8,128)(2,1)S(1)}, u32[]{:S(2)}, u32[]{:S(2)}) collective-permute-start(bf16[4,128,1024]{2,1,0:T(8,128)(2,1)S(1)} %collective-permute-done.refs_8_.refs_2_.refs_7_.refs_0_), channel_id=1, source_target_pairs={{0,1},{1,0},{2,3},{3,2},{4,5},{5,4},{6,7},{7,6},{8,9},{9,8},{10,11... | collective-permute-start | bytes 3145736 | tf_op jit(solution)/shard_map/ppermute | solution.py:405
  85.3 0.7 collective-permute-start.14
  86.0 0.0 collective-permute-done.31.refs_12_.refs_13_
  86.0 0.1 collective-permute-start.19
  86.1 0.5 collective-permute-start.21
  86.6 6.9 %collective-permute-done.1.refs_9_.refs_11_.refs_1_.refs_3_ = bf16[2,128,1024]{2,1,0:T(8,128)(2,1)S(1)} collective-permute-done((bf16[2,128,1024]{2,1,0:T(8,128)(2,1)S(1)}, bf16[2,128,1024]{2,1,0:T(8,128)(2,1)S(1)}, u32[]{:S(2)}, u32[]{:S(2)}) %collective-permute-start.1) | collective-permute-done | bytes 524320 | tf_op jit(solution)/shard_map/ppermute | solution.py:405
  93.5 1.3 collective-permute-start.7
  94.8 1.3 collective-permute-start.32
  96.1 0.2 shard_map.75
  96.3 7.7 %collective-permute-done.7.refs_13_.refs_14_.refs_5_ = bf16[2,128,1024]{2,1,0:T(8,128)(2,1)S(1)} collective-permute-done((bf16[2,128,1024]{2,1,0:T(8,128)(2,1)S(1)}, bf16[2,128,1024]{2,1,0:T(8,128)(2,1)S(1)}, u32[]{:S(2)}, u32[]{:S(2)}) %collective-permute-start.7) | collective-permute-done | bytes 524320 | tf_op jit(solution)/shard_map/ppermute | solution.py:405
  104.0 3.0 %collective-permute-done.22.refs_6_ = bf16[4,128,1024]{2,1,0:T(8,128)(2,1)S(1)} collective-permute-done((bf16[4,128,1024]{2,1,0:T(8,128)(2,1)S(1)}, bf16[4,128,1024]{2,1,0:T(8,128)(2,1)S(1)}, u32[]{:S(2)}, u32[]{:S(2)}) %collective-permute-start.22) | collective-permute-done | bytes 1048608 | tf_op jit(solution)/shard_map/ppermute | solution.py:405
  107.0 0.1 shard_map.73
  107.1 4.6 %collective-permute-done.32 = bf16[2,128,1024]{2,1,0:T(8,128)(2,1)S(1)} collective-permute-done((bf16[2,128,1024]{2,1,0:T(8,128)(2,1)S(1)}, bf16[2,128,1024]{2,1,0:T(8,128)(2,1)S(1)}, u32[]{:S(2)}, u32[]{:S(2)}) %collective-permute-start.32) | collective-permute-done | bytes 524320 | tf_op jit(solution)/shard_map/ppermute | solution.py:405
  111.7 0.7 collective-permute-start.33
  112.4 1.3 collective-permute-start.35
  113.8 14.2 %collective-permute-start.16 = (bf16[1,128,1024]{2,1,0:T(8,128)(2,1)S(1)}, bf16[1,128,1024]{2,1,0:T(8,128)(2,1)S(1)}, u32[]{:S(2)}, u32[]{:S(2)}) collective-permute-start(bf16[1,128,1024]{2,1,0:T(8,128)(2,1)S(1)} %collective-permute-done.8), channel_id=1, source_target_pairs={{0,24},{1,25},{30,6},{31,7}} | collective-permute-start | bytes 786440 | tf_op jit(solution)/shard_map/ppermute | solution.py:405
  128.0 0.7 collective-permute-start.9
  128.7 0.7 collective-permute-start.10
  129.4 0.7 collective-permute-start.17
  130.2 1.4 prep.1
  131.6 1.8 %shard_map.76.refs_16_ = bf16[2,4,2,256,1024]{4,3,2,1,0:T(8,128)(2,1)S(1)} custom-call(bf16[2,128,1024]{2,1,0:T(8,128)(2,1)S(1)} %flatten_occ.1.occ_flat_ref.refs_0_, bf16[4,128,1024]{2,1,0:T(8,128)(2,1)S(1)} %collective-permute-done.18.refs_1_, bf16[4,128,1024]{2,1,0:T(8,128)(2,1)S(1)} %collective-permute-done.refs_8_.refs_2_.refs_7_.refs_0_, ...), custom_call_target="tpu_custom_call" | custom-call | tf_op jit(solution)/shard_map/pallas_call | solution.py:570
  133.4 1.8 %shard_map.74.refs_9_.refs_11_ = bf16[2,4,2,256,1024]{4,3,2,1,0:T(8,128)(2,1)S(1)} custom-call(bf16[2,128,1024]{2,1,0:T(8,128)(2,1)S(1)} %get-tuple-element.12.refs_0_, bf16[4,128,1024]{2,1,0:T(8,128)(2,1)S(1)} %collective-permute-done.18.refs_1_, bf16[4,128,1024]{2,1,0:T(8,128)(2,1)S(1)} %collective-permute-done.refs_8_.refs_2_.refs_7_.refs_0_, ...), custom_call_target="tpu_custom_call" | custom-call | tf_op jit(solution)/shard_map/pallas_call | solution.py:570
  135.3 3.3 %occ_tiles.1.refs_11_.refs_13_ = f32[8,2,256,256]{3,2,1,0:T(8,128)S(1)} custom-call(bf16[2,128,1024]{2,1,0:T(8,128)(2,1)S(1)} %flatten_occ.1.occ_flat_ref.refs_0_, bf16[2,128,1024]{2,1,0:T(8,128)(2,1)S(1)} %collective-permute-done.24.refs_1_.refs_2_, bf16[2,128,1024]{2,1,0:T(8,128)(2,1)S(1)} %collective-permute-done.24.refs_1_.refs_2_, ...), custom_call_target="tpu_custom_call" | custom-call | tf_op jit(solution)/shard_map/occ_tiles/pallas_call | solution.py:580
  138.6 3.2 %emp_direct.1.refs_14_ = f32[2,2,2,128,256]{4,3,2,1,0:T(8,128)S(1)} custom-call(bf16[2,128,1024]{2,1,0:T(8,128)(2,1)S(1)} %get-tuple-element.12.refs_0_, bf16[2,128,1024]{2,1,0:T(8,128)(2,1)S(1)} %collective-permute-done.2.refs_1_, bf16[1,128,1024]{2,1,0:T(8,128)(2,1)S(1)} %collective-permute-done.11.refs_2_, ...), custom_call_target="tpu_custom_call" | custom-call | tf_op jit(solution)/shard_map/emp_direct/pallas_call | solution.py:591
  141.8 4.6 %closing.1 = f32[2,2,128,2,256]{4,3,2,1,0:T(2,128)} custom-call(bf16[4,128,1024]{2,1,0:T(8,128)(2,1)S(1)} %collective-permute-done.refs_8_.refs_2_.refs_7_.refs_0_, bf16[2,128,1024]{2,1,0:T(8,128)(2,1)S(1)} %collective-permute-done.1.refs_9_.refs_11_.refs_1_.refs_3_, bf16[2,128,1024]{2,1,0:T(8,128)(2,1)S(1)} %collective-permute-done.3.refs_5_.refs_10_.refs_2_, ...), custom_call_target="tpu_custom_call" | custom-call | tf_op jit(solution)/shard_map/closing/pallas_call | solution.py:592
  (35 shorter events, 0.1 us)
Async XLA Ops:
  0.0 1.0 copy-start
  1.2 26.3 %collective-permute-start.24 = (bf16[2,128,1024]{2,1,0:T(8,128)(2,1)S(1)}, bf16[2,128,1024]{2,1,0:T(8,128)(2,1)S(1)}, u32[]{:S(2)}, u32[]{:S(2)}) collective-permute-start(bf16[2,128,1024]{2,1,0:T(8,128)(2,1)S(1)} %flatten_occ.1.occ_flat_ref.refs_0_), channel_id=1, source_target_pairs={{0,2},{1,3},{2,0},{3,1},{4,6},{5,7},{6,4},{7,5},{8,10},{9,11},{10,... | collective-permute-start | bytes 1572872 | tf_op jit(solution)/shard_map/ppermute | solution.py:405
  4.3 1.0 copy-start.1
  5.5 17.2 %collective-permute-start.11 = (bf16[1,128,1024]{2,1,0:T(8,128)(2,1)S(1)}, bf16[1,128,1024]{2,1,0:T(8,128)(2,1)S(1)}, u32[]{:S(2)}, u32[]{:S(2)}) collective-permute-start(bf16[1,128,1024]{2,1,0:T(8,128)(2,1)S(1)} %get-tuple-element.13), channel_id=1, source_target_pairs={{2,0},{3,1},{10,8},{11,9},{20,22},{21,23},{28,30},{29,31}} | collective-permute-start | bytes 786440 | tf_op jit(solution)/shard_map/ppermute | solution.py:405
  6.8 20.6 %collective-permute-start.12 = (bf16[1,128,1024]{2,1,0:T(8,128)(2,1)S(1)}, bf16[1,128,1024]{2,1,0:T(8,128)(2,1)S(1)}, u32[]{:S(2)}, u32[]{:S(2)}) collective-permute-start(bf16[1,128,1024]{2,1,0:T(8,128)(2,1)S(1)} %get-tuple-element.14), channel_id=1, source_target_pairs={{2,0},{3,1},{10,8},{11,9},{20,22},{21,23},{28,30},{29,31}} | collective-permute-start | bytes 786440 | tf_op jit(solution)/shard_map/ppermute | solution.py:405
  8.1 20.8 %collective-permute-start.25 = (bf16[2,128,1024]{2,1,0:T(8,128)(2,1)S(1)}, bf16[2,128,1024]{2,1,0:T(8,128)(2,1)S(1)}, u32[]{:S(2)}, u32[]{:S(2)}) collective-permute-start(bf16[2,128,1024]{2,1,0:T(8,128)(2,1)S(1)} %flatten_occ.1.occ_flat_ref.refs_0_), channel_id=1, source_target_pairs={{2,4},{3,5},{4,2},{5,3},{10,12},{11,13},{12,10},{13,11},{18,20},{1... | collective-permute-start | bytes 1572872 | tf_op jit(solution)/shard_map/ppermute | solution.py:405
  8.8 34.7 %collective-permute-start = (bf16[4,128,1024]{2,1,0:T(8,128)(2,1)S(1)}, bf16[4,128,1024]{2,1,0:T(8,128)(2,1)S(1)}, u32[]{:S(2)}, u32[]{:S(2)}) collective-permute-start(bf16[4,128,1024]{2,1,0:T(8,128)(2,1)S(1)} %get-tuple-element.11), channel_id=1, source_target_pairs={{0,16},{1,17},{2,18},{3,19},{4,20},{5,21},{6,22},{7,23},{8,24},{9,... | collective-permute-start | bytes 3145736 | tf_op jit(solution)/shard_map/ppermute | solution.py:405
  22.7 23.5 %collective-permute-start.20 = (bf16[4,128,1024]{2,1,0:T(8,128)(2,1)S(1)}, bf16[4,128,1024]{2,1,0:T(8,128)(2,1)S(1)}, u32[]{:S(2)}, u32[]{:S(2)}) collective-permute-start(bf16[4,128,1024]{2,1,0:T(8,128)(2,1)S(1)} %get-tuple-element.11), channel_id=1, source_target_pairs={{0,1},{1,0},{2,3},{3,2},{4,5},{5,4},{6,7},{7,6},{8,9},{9,8},{10,11... | collective-permute-start | bytes 3145736 | tf_op jit(solution)/shard_map/ppermute | solution.py:405
  27.5 19.4 %collective-permute-start.18 = (bf16[4,128,1024]{2,1,0:T(8,128)(2,1)S(1)}, bf16[4,128,1024]{2,1,0:T(8,128)(2,1)S(1)}, u32[]{:S(2)}, u32[]{:S(2)}) collective-permute-start(bf16[4,128,1024]{2,1,0:T(8,128)(2,1)S(1)} %get-tuple-element.11), channel_id=1, source_target_pairs={{0,8},{1,9},{2,10},{3,11},{4,12},{5,13},{6,14},{7,15},{8,0},{9,1},... | collective-permute-start | bytes 3145736 | tf_op jit(solution)/shard_map/ppermute | solution.py:405
  27.5 13.4 %collective-permute-start.2 = (bf16[2,128,1024]{2,1,0:T(8,128)(2,1)S(1)}, bf16[2,128,1024]{2,1,0:T(8,128)(2,1)S(1)}, u32[]{:S(2)}, u32[]{:S(2)}) collective-permute-start(bf16[2,128,1024]{2,1,0:T(8,128)(2,1)S(1)} %get-tuple-element.12.refs_0_), channel_id=1, source_target_pairs={{0,2},{1,3},{4,6},{5,7},{6,4},{7,5},{8,10},{9,11},{12,14},{13,15},... | collective-permute-start | bytes 1572872 | tf_op jit(solution)/shard_map/ppermute | solution.py:405
  29.0 13.2 %collective-permute-start.5 = (bf16[2,128,1024]{2,1,0:T(8,128)(2,1)S(1)}, bf16[2,128,1024]{2,1,0:T(8,128)(2,1)S(1)}, u32[]{:S(2)}, u32[]{:S(2)}) collective-permute-start(bf16[2,128,1024]{2,1,0:T(8,128)(2,1)S(1)} %get-tuple-element.12.refs_0_), channel_id=1, source_target_pairs={{2,4},{3,5},{4,2},{5,3},{10,12},{11,13},{12,10},{13,11},{18,20},{1... | collective-permute-start | bytes 1572872 | tf_op jit(solution)/shard_map/ppermute | solution.py:405
  40.9 16.7 %collective-permute-start.26 = (bf16[2,128,1024]{2,1,0:T(8,128)(2,1)S(1)}, bf16[2,128,1024]{2,1,0:T(8,128)(2,1)S(1)}, u32[]{:S(2)}, u32[]{:S(2)}) collective-permute-start(bf16[2,128,1024]{2,1,0:T(8,128)(2,1)S(1)} %collective-permute-done.24.refs_1_.refs_2_), channel_id=1, source_target_pairs={{2,4},{3,5},{4,2},{5,3},{6,22},{7,23},{10,12},{11,13},{12,10},{13,... | collective-permute-start | bytes 1572872 | tf_op jit(solution)/shard_map/ppermute | solution.py:405
  42.2 25.4 %collective-permute-start.3 = (bf16[2,128,1024]{2,1,0:T(8,128)(2,1)S(1)}, bf16[2,128,1024]{2,1,0:T(8,128)(2,1)S(1)}, u32[]{:S(2)}, u32[]{:S(2)}) collective-permute-start(bf16[2,128,1024]{2,1,0:T(8,128)(2,1)S(1)} %collective-permute-done.2.refs_1_), channel_id=1, source_target_pairs={{2,4},{3,5},{4,2},{5,3},{6,22},{7,23},{10,12},{11,13},{12,10},{13,... | collective-permute-start | bytes 1572872 | tf_op jit(solution)/shard_map/ppermute | solution.py:405
  43.5 28.6 %collective-permute-start.30 = (bf16[2,128,1024]{2,1,0:T(8,128)(2,1)S(1)}, bf16[2,128,1024]{2,1,0:T(8,128)(2,1)S(1)}, u32[]{:S(2)}, u32[]{:S(2)}) collective-permute-start(bf16[2,128,1024]{2,1,0:T(8,128)(2,1)S(1)} %collective-permute-done.25.refs_3_), channel_id=1, source_target_pairs={{2,0},{3,1},{10,8},{11,9},{20,22},{21,23},{28,30},{29,31}} | collective-permute-start | bytes 1572872 | tf_op jit(solution)/shard_map/ppermute | solution.py:405
  46.2 26.6 %collective-permute-start.27 = (bf16[2,128,1024]{2,1,0:T(8,128)(2,1)S(1)}, bf16[2,128,1024]{2,1,0:T(8,128)(2,1)S(1)}, u32[]{:S(2)}, u32[]{:S(2)}) collective-permute-start(bf16[2,128,1024]{2,1,0:T(8,128)(2,1)S(1)} %collective-permute-done.25.refs_3_), channel_id=1, source_target_pairs={{2,18},{3,19},{4,6},{5,7},{10,26},{11,27},{12,14},{13,15},{18,16},... | collective-permute-start | bytes 1572872 | tf_op jit(solution)/shard_map/ppermute | solution.py:405
  46.9 27.2 %collective-permute-start.6 = (bf16[2,128,1024]{2,1,0:T(8,128)(2,1)S(1)}, bf16[2,128,1024]{2,1,0:T(8,128)(2,1)S(1)}, u32[]{:S(2)}, u32[]{:S(2)}) collective-permute-start(bf16[2,128,1024]{2,1,0:T(8,128)(2,1)S(1)} %collective-permute-done.5.refs_4_), channel_id=1, source_target_pairs={{2,0},{3,1},{10,8},{11,9},{20,22},{21,23},{28,30},{29,31}} | collective-permute-start | bytes 1572872 | tf_op jit(solution)/shard_map/ppermute | solution.py:405
  57.6 17.8 %collective-permute-start.13 = (bf16[2,128,1024]{2,1,0:T(8,128)(2,1)S(1)}, bf16[2,128,1024]{2,1,0:T(8,128)(2,1)S(1)}, u32[]{:S(2)}, u32[]{:S(2)}) collective-permute-start(bf16[2,128,1024]{2,1,0:T(8,128)(2,1)S(1)} %collective-permute-done.5.refs_4_), channel_id=1, source_target_pairs={{4,6},{5,7},{12,14},{13,15},{18,16},{19,17},{26,24},{27,25}} | collective-permute-start | bytes 1572872 | tf_op jit(solution)/shard_map/ppermute | solution.py:405
  67.6 16.1 %collective-permute-start.29 = (bf16[2,128,1024]{2,1,0:T(8,128)(2,1)S(1)}, bf16[2,128,1024]{2,1,0:T(8,128)(2,1)S(1)}, u32[]{:S(2)}, u32[]{:S(2)}) collective-permute-start(bf16[2,128,1024]{2,1,0:T(8,128)(2,1)S(1)} %get-tuple-element.17), channel_id=1, source_target_pairs={{0,2},{1,3},{8,10},{9,11},{22,20},{23,21},{30,28},{31,29}} | collective-permute-start | bytes 1572872 | tf_op jit(solution)/shard_map/ppermute | solution.py:405
  72.1 13.2 %collective-permute-start.28 = (bf16[2,128,1024]{2,1,0:T(8,128)(2,1)S(1)}, bf16[2,128,1024]{2,1,0:T(8,128)(2,1)S(1)}, u32[]{:S(2)}, u32[]{:S(2)}) collective-permute-start(bf16[2,128,1024]{2,1,0:T(8,128)(2,1)S(1)} %collective-permute-done.26.refs_4_.refs_9_), channel_id=1, source_target_pairs={{2,18},{3,19},{4,6},{5,7},{10,26},{11,27},{12,14},{13,15},{18,16},... | collective-permute-start | bytes 1572872 | tf_op jit(solution)/shard_map/ppermute | solution.py:405
  72.8 9.3 %collective-permute-start.8 = (bf16[1,128,1024]{2,1,0:T(8,128)(2,1)S(1)}, bf16[1,128,1024]{2,1,0:T(8,128)(2,1)S(1)}, u32[]{:S(2)}, u32[]{:S(2)}) collective-permute-start(bf16[1,128,1024]{2,1,0:T(8,128)(2,1)S(1)} %slice.17), channel_id=1, source_target_pairs={{2,0},{3,1},{10,8},{11,9},{20,22},{21,23},{28,30},{29,31}} | collective-permute-start | bytes 786440 | tf_op jit(solution)/shard_map/ppermute | solution.py:405
  74.1 11.9 %collective-permute-start.31 = (bf16[2,128,1024]{2,1,0:T(8,128)(2,1)S(1)}, bf16[2,128,1024]{2,1,0:T(8,128)(2,1)S(1)}, u32[]{:S(2)}, u32[]{:S(2)}) collective-permute-start(bf16[2,128,1024]{2,1,0:T(8,128)(2,1)S(1)} %collective-permute-done.30), channel_id=1, source_target_pairs={{0,16},{1,17},{8,24},{9,25},{22,6},{23,7},{30,14},{31,15}} | collective-permute-start | bytes 1572872 | tf_op jit(solution)/shard_map/ppermute | solution.py:405
  75.4 10.7 %collective-permute-start.4 = (bf16[2,128,1024]{2,1,0:T(8,128)(2,1)S(1)}, bf16[2,128,1024]{2,1,0:T(8,128)(2,1)S(1)}, u32[]{:S(2)}, u32[]{:S(2)}) collective-permute-start(bf16[2,128,1024]{2,1,0:T(8,128)(2,1)S(1)} %collective-permute-done.3.refs_5_.refs_10_.refs_2_), channel_id=1, source_target_pairs={{2,18},{3,19},{10,26},{11,27},{20,4},{21,5},{28,12},{29,13}} | collective-permute-start | bytes 1572872 | tf_op jit(solution)/shard_map/ppermute | solution.py:405
  82.1 48.1 %copy-start.2 = (f32[2,8,512]{2,1,0:T(8,128)S(1)}, f32[2,8,512]{2,1,0:T(8,128)}, u32[]{:S(2)}) copy-start(f32[2,8,512]{2,1,0:T(8,128)} %levels_in.1) | copy-start | bytes 98308
  82.1 48.1 %copy-start.3 = (s32[2,8,512]{2,1,0:T(8,128)S(1)}, s32[2,8,512]{2,1,0:T(8,128)}, u32[]{:S(2)}) copy-start(s32[2,8,512]{2,1,0:T(8,128)} %rank_in.1) | copy-start | bytes 98308
  82.1 48.1 %copy-start.4 = (s32[2,8]{1,0:T(2,128)S(1)}, s32[2,8]{1,0:T(2,128)}, u32[]{:S(2)}) copy-start(s32[2,8]{1,0:T(2,128)} %map_ref.1) | copy-start | bytes 196
  82.1 48.1 %copy-start.5 = (f32[2]{0:T(128)S(1)}, f32[2]{0:T(128)}, u32[]{:S(2)}) copy-start(f32[2]{0:T(128)} %times_ref.1) | copy-start | bytes 28
  82.1 48.1 %copy-start.6 = (s32[8]{0:T(128)S(1)}, s32[8]{0:T(128)}, u32[]{:S(2)}) copy-start(s32[8]{0:T(128)} %kpoint_ref.1) | copy-start | bytes 100
  82.1 11.4 %collective-permute-start.1 = (bf16[2,128,1024]{2,1,0:T(8,128)(2,1)S(1)}, bf16[2,128,1024]{2,1,0:T(8,128)(2,1)S(1)}, u32[]{:S(2)}, u32[]{:S(2)}) collective-permute-start(bf16[2,128,1024]{2,1,0:T(8,128)(2,1)S(1)} %get-tuple-element.18), channel_id=1, source_target_pairs={{0,2},{1,3},{2,4},{3,5},{8,10},{9,11},{10,12},{11,13},{20,18},{21,... | collective-permute-start | bytes 1572872 | tf_op jit(solution)/shard_map/ppermute | solution.py:405
  83.7 23.3 %collective-permute-start.22 = (bf16[4,128,1024]{2,1,0:T(8,128)(2,1)S(1)}, bf16[4,128,1024]{2,1,0:T(8,128)(2,1)S(1)}, u32[]{:S(2)}, u32[]{:S(2)}) collective-permute-start(bf16[4,128,1024]{2,1,0:T(8,128)(2,1)S(1)} %collective-permute-done.refs_8_.refs_2_.refs_7_.refs_0_), channel_id=1, source_target_pairs={{0,1},{1,0},{2,3},{3,2},{4,5},{5,4},{6,7},{7,6},{8,9},{9,8},{10,11... | collective-permute-start | bytes 3145736 | tf_op jit(solution)/shard_map/ppermute | solution.py:405
  85.3 9.5 %collective-permute-start.14 = (bf16[2,128,1024]{2,1,0:T(8,128)(2,1)S(1)}, bf16[2,128,1024]{2,1,0:T(8,128)(2,1)S(1)}, u32[]{:S(2)}, u32[]{:S(2)}) collective-permute-start(bf16[2,128,1024]{2,1,0:T(8,128)(2,1)S(1)} %collective-permute-done.3.refs_5_.refs_10_.refs_2_), channel_id=1, source_target_pairs={{4,6},{5,7},{12,14},{13,15},{18,16},{19,17},{26,24},{27,25}} | collective-permute-start | bytes 1572872 | tf_op jit(solution)/shard_map/ppermute | solution.py:405
  86.0 25.7 %collective-permute-start.19 = (bf16[4,128,1024]{2,1,0:T(8,128)(2,1)S(1)}, bf16[4,128,1024]{2,1,0:T(8,128)(2,1)S(1)}, u32[]{:S(2)}, u32[]{:S(2)}) collective-permute-start(bf16[4,128,1024]{2,1,0:T(8,128)(2,1)S(1)} %collective-permute-done.refs_8_.refs_2_.refs_7_.refs_0_), channel_id=1, source_target_pairs={{0,8},{1,9},{2,10},{3,11},{4,12},{5,13},{6,14},{7,15},{8,0},{9,1},... | collective-permute-start | bytes 3145736 | tf_op jit(solution)/shard_map/ppermute | solution.py:405
  86.1 26.3 %collective-permute-start.21 = (bf16[4,128,1024]{2,1,0:T(8,128)(2,1)S(1)}, bf16[4,128,1024]{2,1,0:T(8,128)(2,1)S(1)}, u32[]{:S(2)}, u32[]{:S(2)}) collective-permute-start(bf16[4,128,1024]{2,1,0:T(8,128)(2,1)S(1)} %collective-permute-done.20.refs_4_), channel_id=1, source_target_pairs={{0,8},{1,9},{2,10},{3,11},{4,12},{5,13},{6,14},{7,15},{8,0},{9,1},... | collective-permute-start | bytes 3145736 | tf_op jit(solution)/shard_map/ppermute | solution.py:405
  93.5 10.5 %collective-permute-start.7 = (bf16[2,128,1024]{2,1,0:T(8,128)(2,1)S(1)}, bf16[2,128,1024]{2,1,0:T(8,128)(2,1)S(1)}, u32[]{:S(2)}, u32[]{:S(2)}) collective-permute-start(bf16[2,128,1024]{2,1,0:T(8,128)(2,1)S(1)} %collective-permute-done.6), channel_id=1, source_target_pairs={{0,16},{1,17},{8,24},{9,25},{22,6},{23,7},{30,14},{31,15}} | collective-permute-start | bytes 1572872 | tf_op jit(solution)/shard_map/ppermute | solution.py:405
  94.8 16.9 %collective-permute-start.32 = (bf16[2,128,1024]{2,1,0:T(8,128)(2,1)S(1)}, bf16[2,128,1024]{2,1,0:T(8,128)(2,1)S(1)}, u32[]{:S(2)}, u32[]{:S(2)}) collective-permute-start(bf16[2,128,1024]{2,1,0:T(8,128)(2,1)S(1)} %collective-permute-done.26.refs_4_.refs_9_), channel_id=1, source_target_pairs={{2,0},{3,1},{10,8},{11,9},{20,22},{21,23},{28,30},{29,31}} | collective-permute-start | bytes 1572872 | tf_op jit(solution)/shard_map/ppermute | solution.py:405
  104.0 24.7 %collective-permute-start.34 = (bf16[2,2,128,1024]{3,2,1,0:T(8,128)(2,1)S(1)}, bf16[2,2,128,1024]{3,2,1,0:T(8,128)(2,1)S(1)}, u32[]{:S(2)}, u32[]{:S(2)}) collective-permute-start(bf16[2,2,128,1024]{3,2,1,0:T(8,128)(2,1)S(1)} %shard_map.75), channel_id=1, source_target_pairs={{0,8},{1,9},{2,10},{3,11},{4,12},{5,13},{6,14},{7,15},{8,0},{9,1},... | collective-permute-start | bytes 3145736 | tf_op jit(solution)/shard_map/ppermute | solution.py:405
  107.0 22.4 %collective-permute-start.23 = (bf16[4,128,1024]{2,1,0:T(8,128)(2,1)S(1)}, bf16[4,128,1024]{2,1,0:T(8,128)(2,1)S(1)}, u32[]{:S(2)}, u32[]{:S(2)}) collective-permute-start(bf16[4,128,1024]{2,1,0:T(8,128)(2,1)S(1)} %collective-permute-done.22.refs_6_), channel_id=1, source_target_pairs={{0,8},{1,9},{2,10},{3,11},{4,12},{5,13},{6,14},{7,15},{8,0},{9,1},... | collective-permute-start | bytes 3145736 | tf_op jit(solution)/shard_map/ppermute | solution.py:405
  111.7 26.9 %collective-permute-start.15 = (bf16[2,2,128,1024]{3,2,1,0:T(8,128)(2,1)S(1)}, bf16[2,2,128,1024]{3,2,1,0:T(8,128)(2,1)S(1)}, u32[]{:S(2)}, u32[]{:S(2)}) collective-permute-start(bf16[2,2,128,1024]{3,2,1,0:T(8,128)(2,1)S(1)} %shard_map.73), channel_id=1, source_target_pairs={{0,8},{1,9},{2,10},{3,11},{4,12},{5,13},{6,14},{7,15},{8,0},{9,1},... | collective-permute-start | bytes 3145736 | tf_op jit(solution)/shard_map/ppermute | solution.py:405
  111.7 2.1 %collective-permute-start.33 = (bf16[2,128,1024]{2,1,0:T(8,128)(2,1)S(1)}, bf16[2,128,1024]{2,1,0:T(8,128)(2,1)S(1)}, u32[]{:S(2)}, u32[]{:S(2)}) collective-permute-start(bf16[2,128,1024]{2,1,0:T(8,128)(2,1)S(1)} %collective-permute-done.32), channel_id=1, source_target_pairs={{8,24},{9,25},{22,6},{23,7}} | collective-permute-start | bytes 1572872 | tf_op jit(solution)/shard_map/ppermute | solution.py:405
  112.4 15.6 %collective-permute-start.35 = (bf16[2,128,1024]{2,1,0:T(8,128)(2,1)S(1)}, bf16[2,128,1024]{2,1,0:T(8,128)(2,1)S(1)}, u32[]{:S(2)}, u32[]{:S(2)}) collective-permute-start(bf16[2,128,1024]{2,1,0:T(8,128)(2,1)S(1)} %collective-permute-done.32), channel_id=1, source_target_pairs={{0,24},{1,25},{30,6},{31,7}} | collective-permute-start | bytes 1572872 | tf_op jit(solution)/shard_map/ppermute | solution.py:405
  113.8 28.0 %collective-permute-start.16 = (bf16[1,128,1024]{2,1,0:T(8,128)(2,1)S(1)}, bf16[1,128,1024]{2,1,0:T(8,128)(2,1)S(1)}, u32[]{:S(2)}, u32[]{:S(2)}) collective-permute-start(bf16[1,128,1024]{2,1,0:T(8,128)(2,1)S(1)} %collective-permute-done.8), channel_id=1, source_target_pairs={{0,24},{1,25},{30,6},{31,7}} | collective-permute-start | bytes 786440 | tf_op jit(solution)/shard_map/ppermute | solution.py:405
  128.0 13.7 %collective-permute-start.9 = (bf16[1,128,1024]{2,1,0:T(8,128)(2,1)S(1)}, bf16[1,128,1024]{2,1,0:T(8,128)(2,1)S(1)}, u32[]{:S(2)}, u32[]{:S(2)}) collective-permute-start(bf16[1,128,1024]{2,1,0:T(8,128)(2,1)S(1)} %collective-permute-done.8), channel_id=1, source_target_pairs={{8,24},{9,25},{22,6},{23,7}} | collective-permute-start | bytes 786440 | tf_op jit(solution)/shard_map/ppermute | solution.py:405
  128.7 13.1 %collective-permute-start.10 = (bf16[1,128,1024]{2,1,0:T(8,128)(2,1)S(1)}, bf16[1,128,1024]{2,1,0:T(8,128)(2,1)S(1)}, u32[]{:S(2)}, u32[]{:S(2)}) collective-permute-start(bf16[1,128,1024]{2,1,0:T(8,128)(2,1)S(1)} %slice.18), channel_id=1, source_target_pairs={{4,6},{5,7},{26,24},{27,25}} | collective-permute-start | bytes 786440 | tf_op jit(solution)/shard_map/ppermute | solution.py:405
  129.4 12.4 %collective-permute-start.17 = (bf16[1,128,1024]{2,1,0:T(8,128)(2,1)S(1)}, bf16[1,128,1024]{2,1,0:T(8,128)(2,1)S(1)}, u32[]{:S(2)}, u32[]{:S(2)}) collective-permute-start(bf16[1,128,1024]{2,1,0:T(8,128)(2,1)S(1)} %slice.18), channel_id=1, source_target_pairs={{12,6},{13,7},{18,24},{19,25}} | collective-permute-start | bytes 786440 | tf_op jit(solution)/shard_map/ppermute | solution.py:405

commit v3 on v2

--- a/solution.py
+++ b/solution.py
@@ -251,31 +251,8 @@
                 pl.when(keep == case)(functools.partial(fetch, source, k))
 
 
-def load_rows(kind, groups, rows, row_buf, sems):
-    slots = row_buf.shape[2]
-    for k in groups:
-        for half in range(2):
-            panel = part(rows[half * 4 + k], kind, slots)
-            pltpu.make_async_copy(panel, row_buf.at[half, k], sems.at[k, 1 + half]).start()
-
-
 def wait_columns(k, col_buf, sems):
     pltpu.make_async_copy(col_buf.at[k], col_buf.at[k], sems.at[k, 0]).wait()
-
-
-def wait_rows(k, row_buf, sems):
-    for half in range(2):
-        pltpu.make_async_copy(row_buf.at[half, k], row_buf.at[half, k], sems.at[k, 1 + half]).wait()
-
-
-def scale_rows(kind, k, i, half, row_buf, weight_ref):
-    slot = (lax.axis_index("kgrp") ^ k) * row_buf.shape[2] + i
-    panel = row_buf[half, k, i].astype(jnp.float32)
-    scaled = [
-        (panel * weight_ref[kind, t, pl.ds(slot, 1), :]).astype(jnp.bfloat16)
-        for t in range(weight_ref.shape[1])
-    ]
-    return jnp.concatenate(scaled, axis=0)
 
 
 def tile(stacked, scaled):
@@ -305,8 +282,9 @@
 
 
 def pair_sums(moved, occ_ref, pair_ref, first, before, store):
-    count, halves = moved.shape[:2]
-    block = moved.shape[2] // 2
+    per_part, halves = moved[0].shape[:2]
+    count = per_part * len(moved)
+    block = moved[0].shape[2] // 2
     transfers = pair_ref.shape[0]
     held = [[pair_ref[q, first + a] for a in range(count)] for q in range(transfers)]
     for half in range(halves):
@@ -318,7 +296,9 @@
             if before is not None:
                 sums = [[before[q, half, comp, real_rows, :] for comp in range(2)] for q in range(transfers)]
             for a in range(count):
-                re, im = moved[a, half, real_rows, :], moved[a, half, imag_rows, :]
+                held_part = moved[a // per_part]
+                re = held_part[a % per_part, half, real_rows, :]
+                im = held_part[a % per_part, half, imag_rows, :]
                 for q in range(transfers):
                     ro = occ_ref[held[q][a], half, real_rows, :]
                     io = occ_ref[held[q][a], half, imag_rows, :]
@@ -333,31 +313,40 @@
 
 
 def scale_kernel(kind, *refs):
-    rows, weight_ref, scaled_ref, row_buf, sems = refs[:8], *refs[8:]
-    load_rows(kind, range(4), rows, row_buf, sems)
-    for k in range(4):
-        wait_rows(k, row_buf, sems)
-        for i in range(row_buf.shape[2]):
-            for half in range(2):
-                scaled_ref[half, k, i] = scale_rows(kind, k, i, half, row_buf, weight_ref)
-
-
-def emp_direct_kernel(cases, *refs):
-    direct = grouped(refs[:-8], cases)
-    recv, scaled_ref, pair_ref, occ_ref, sum_ref, col_buf, moved, sems = refs[-8:]
-    load_columns(1, (0, 1), direct, None, recv, None, col_buf, sems)
-    per_group = col_buf.shape[1]
-    for k in (0, 1):
-        wait_columns(k, col_buf, sems)
-        for i in range(per_group):
-            stacked = stack_columns(col_buf[k, i])
-            for half in range(2):
-                moved[k * per_group + i, half] = tile(stacked, scaled_ref[half, k, i])
-
+    rows, weight_ref, scaled_ref = refs[:8], *refs[8:]
+    groups, slots = scaled_ref.shape[1:3]
+    group = lax.axis_index("kgrp")
+    for k in range(groups):
+        for half in range(2):
+            panels = rows[half * groups + k]
+            skip = panels.shape[0] - slots
+            for i in range(slots):
+                panel = panels[kind * skip + i].astype(jnp.float32)
+                parts = []
+                for t in range(weight_ref.shape[1]):
+                    weight = weight_ref[kind, t, pl.ds((group ^ k) * slots + i, 1), :]
+                    parts.append((panel * weight).astype(jnp.bfloat16))
+                scaled_ref[half, k, i] = jnp.concatenate(parts, axis=0)
+
+
+def emp_tiles_kernel(k, cases, *refs):
+    scaled_ref, moved, col_buf, sems = refs[-4:]
+    if k:
+        load_columns(1, (k,), None, None, refs[0], None, col_buf, sems)
+    else:
+        load_columns(1, (k,), grouped(refs[:-4], cases), None, None, None, col_buf, sems)
+    wait_columns(k, col_buf, sems)
+    for i in range(col_buf.shape[1]):
+        stacked = stack_columns(col_buf[k, i])
+        for half in range(2):
+            moved[i, half] = tile(stacked, scaled_ref[half, k, i])
+
+
+def sums_kernel(own, given, pair_ref, occ_ref, sum_ref):
     def store(half, rows_at, q, comp, value):
         sum_ref[q, half, comp, rows_at, :] = value
 
-    pair_sums(moved, occ_ref, pair_ref, 0, None, store)
+    pair_sums((own, given), occ_ref, pair_ref, 0, None, store)
 
 
 def closing_kernel(factor, cases, *refs):
@@ -381,7 +370,7 @@
         for t in range(times):
             out_ref[comp, q, rows_at, t, pl.ds(start, block)] = value[:, t * block : (t + 1) * block]
 
-    pair_sums(moved, occ_ref, pair_ref, 2 * per_group, sum_ref, store)
+    pair_sums((moved,), occ_ref, pair_ref, 2 * per_group, sum_ref, store)
 
 
 def output_stationary(occ_orbitals, emp_orbitals, energies, band_order, imag_times, kq_map, slot_kpoint):
@@ -552,20 +541,16 @@
         give = pack(kind, direct[kind], ready, (slots, block, width))
         given.append(send(give, flip_core))
 
-    panel_scratch = [
-        pltpu.VMEM((2, 4, slots, block, width), jnp.bfloat16),
-        pltpu.VMEM((4, slots, block, width), jnp.bfloat16),
-    ]
+    column_scratch = pltpu.VMEM((4, slots, block, width), jnp.bfloat16)
     cases = len(across[0])
     scaled = []
     for kind in range(2):
         scale = pl.pallas_call(
             functools.partial(scale_kernel, kind),
             out_shape=jax.ShapeDtypeStruct((2, 4, slots, times * block, width), jnp.bfloat16),
-            in_specs=[HBM] * 8 + [VMEM],
+            in_specs=[VMEM] * 9,
             out_specs=VMEM,
-            scratch_shapes=panel_scratch[:1] + [pltpu.SemaphoreType.DMA((4, 3))],
-            compiler_params=LIMIT,
+            compiler_params=pltpu.CompilerParams(vmem_limit_bytes=20 * 2**20),
         )
         scaled.append(scale(*row_panels[kind], weights))
     occ_tiles = pl.pallas_call(
@@ -573,28 +558,38 @@
         out_shape=jax.ShapeDtypeStruct((kpoints, 2, 2 * block, times * block), jnp.float32),
         in_specs=[HBM] * (2 + 2 * cases) + [VMEM],
         out_specs=VMEM,
-        scratch_shapes=panel_scratch[1:] + [pltpu.SemaphoreType.DMA((4, 3))],
+        scratch_shapes=[column_scratch, pltpu.SemaphoreType.DMA((4, 1))],
         compiler_params=LIMIT,
         name="occ_tiles",
     )
     tiles = occ_tiles(*direct[0], *across[0], given[0], *last[0], scaled[0])
     half_tiles = (kpoints // 2, 2, 2 * block, times * block)
-    emp_direct = pl.pallas_call(
-        functools.partial(emp_direct_kernel, cases),
+    moved = []
+    for k, panels in enumerate((direct[1], given[1:])):
+        emp_tiles = pl.pallas_call(
+            functools.partial(emp_tiles_kernel, k, cases),
+            out_shape=jax.ShapeDtypeStruct((slots,) + half_tiles[1:], jnp.float32),
+            in_specs=[HBM] * len(panels) + [VMEM],
+            out_specs=VMEM,
+            scratch_shapes=[column_scratch, pltpu.SemaphoreType.DMA((4, 1))],
+            compiler_params=LIMIT,
+        )
+        moved.append(emp_tiles(*panels, scaled[1]))
+    direct_sums = pl.pallas_call(
+        sums_kernel,
         out_shape=jax.ShapeDtypeStruct((transfers, 2, 2, block, times * block), jnp.float32),
-        in_specs=[HBM] * (1 + len(direct[1])) + [VMEM, SMEM, VMEM],
+        in_specs=[VMEM, VMEM, SMEM, VMEM],
         out_specs=VMEM,
-        scratch_shapes=panel_scratch[1:] + [pltpu.VMEM(half_tiles, jnp.float32), pltpu.SemaphoreType.DMA((4, 3))],
         compiler_params=LIMIT,
-        name="emp_direct",
-    )
-    sums = emp_direct(*direct[1], given[1], scaled[1], pairs, tiles)
+        name="direct_sums",
+    )
+    sums = direct_sums(*moved, pairs, tiles)
     result = pl.pallas_call(
         functools.partial(closing_kernel, -1.0 / kpoints, cases),
         out_shape=jax.ShapeDtypeStruct((2, transfers, block, times, cols * block), jnp.float32),
         in_specs=[HBM] * (4 + cases) + [VMEM, SMEM, VMEM, VMEM],
         out_specs=VMEM,
-        scratch_shapes=panel_scratch[1:] + [pltpu.VMEM(half_tiles, jnp.float32), pltpu.SemaphoreType.DMA((4, 3))],
+        scratch_shapes=[column_scratch, pltpu.VMEM(half_tiles, jnp.float32), pltpu.SemaphoreType.DMA((4, 1))],
         compiler_params=LIMIT,
         name="closing",
     )(*across[1], given[1], *last[1], scaled[1], pairs, tiles, sums)

time: 147 us -> 145 us (0.986)
  waiting for transfers between devices: 75.8 us -> 68.7 us
  starting transfers between devices: 51.1 us -> 56.3 us
    ppermute x36, waiting for transfers between devices: 75.8 us -> 68.7 us  [send(): return lax.ppermute(array, AXES, pairs)]
    ppermute x36, starting transfers between devices: 51.1 us -> 56.3 us  [send(): return lax.ppermute(array, AXES, pairs)]
    pallas_call x1 -> x3, Pallas kernels: 3.15 us -> 2.95 us  [the longest x2 1.69 us: output_stationary(): moved.append(emp_tiles(*panels, scaled[1]))]
where the time goes in v3:
time: 145 us; the launch traced here: 144 us
  waiting for transfers between devices  68.7 us (47%)
  starting transfers between devices  56.3 us (39%)
  Pallas kernels  15.7 us (11%)
  local copies, waits for them, and re-layouts  2.21 us (2%)
    ppermute x36, waiting for transfers between devices, send(): return lax.ppermute(array, AXES, pairs)  68.7 us
    ppermute x36, starting transfers between devices, send(): return lax.ppermute(array, AXES, pairs)  56.3 us
    pallas_call x1, Pallas kernels, output_stationary(): pl.pallas_call(functools.partial(closing_kernel, -1.0 / kpoints, cases),...  4.49 us
    pallas_call x1, Pallas kernels, output_stationary(): tiles = occ_tiles(*direct[0], *across[0], given[0], *last[0], scaled[0])  3.41 us
  transfers between devices with their start and end apart: 36, of which 11 were waited for; matrix products, arithmetic and copies ran while one was open for 0% of the time, Pallas kernels for 8%

profile of v3, /device:TPU:0, one launch (start us, length us, event | category | flops | bytes accessed | tf_op | source)
XLA Modules:
  0.0 143.7 jit_solution(4385610707435997588)
XLA Ops:
  0.0 1.0 copy-done
  1.0 0.2 flatten_occ.1.occ_flat_ref.refs_0_
  1.2 0.0 copy-start.1
  1.2 1.0 copy-done.1
  2.2 0.2 flatten_emp.1
  2.4 5.0 %collective-permute-start.2 = (bf16[2,128,1024]{2,1,0:T(8,128)(2,1)S(1)}, bf16[2,128,1024]{2,1,0:T(8,128)(2,1)S(1)}, u32[]{:S(2)}, u32[]{:S(2)}) collective-permute-start(bf16[2,128,1024]{2,1,0:T(8,128)(2,1)S(1)} %get-tuple-element.12.refs_0_), channel_id=1, source_target_pairs={{0,2},{1,3},{4,6},{5,7},{6,4},{7,5},{8,10},{9,11},{12,14},{13,15},... | collective-permute-start | bytes 1572872 | tf_op jit(solution)/shard_map/ppermute | solution.py:394
  7.4 0.7 collective-permute-start.5
  8.1 1.3 collective-permute-start.11
  9.4 1.3 collective-permute-start.12
  10.7 0.3 collective-permute-start
  11.0 9.9 %collective-permute-done.11.refs_2_ = bf16[1,128,1024]{2,1,0:T(8,128)(2,1)S(1)} collective-permute-done((bf16[1,128,1024]{2,1,0:T(8,128)(2,1)S(1)}, bf16[1,128,1024]{2,1,0:T(8,128)(2,1)S(1)}, u32[]{:S(2)}, u32[]{:S(2)}) %collective-permute-start.11) | collective-permute-done | bytes 262176 | tf_op jit(solution)/shard_map/ppermute | solution.py:394
  20.9 1.5 %collective-permute-start.20 = (bf16[4,128,1024]{2,1,0:T(8,128)(2,1)S(1)}, bf16[4,128,1024]{2,1,0:T(8,128)(2,1)S(1)}, u32[]{:S(2)}, u32[]{:S(2)}) collective-permute-start(bf16[4,128,1024]{2,1,0:T(8,128)(2,1)S(1)} %get-tuple-element.11), channel_id=1, source_target_pairs={{0,1},{1,0},{2,3},{3,2},{4,5},{5,4},{6,7},{7,6},{8,9},{9,8},{10,11... | collective-permute-start | bytes 3145736 | tf_op jit(solution)/shard_map/ppermute | solution.py:394
  22.4 2.7 %collective-permute-done.12.refs_3_ = bf16[1,128,1024]{2,1,0:T(8,128)(2,1)S(1)} collective-permute-done((bf16[1,128,1024]{2,1,0:T(8,128)(2,1)S(1)}, bf16[1,128,1024]{2,1,0:T(8,128)(2,1)S(1)}, u32[]{:S(2)}, u32[]{:S(2)}) %collective-permute-start.12) | collective-permute-done | bytes 262176 | tf_op jit(solution)/shard_map/ppermute | solution.py:394
  25.1 0.0 collective-permute-start.18
  25.1 0.0 collective-permute-done.2.refs_1_
  25.1 0.0 collective-permute-start.24
  25.1 0.7 collective-permute-start.25
  25.8 13.6 %collective-permute-done.24.refs_1_.refs_2_ = bf16[2,128,1024]{2,1,0:T(8,128)(2,1)S(1)} collective-permute-done((bf16[2,128,1024]{2,1,0:T(8,128)(2,1)S(1)}, bf16[2,128,1024]{2,1,0:T(8,128)(2,1)S(1)}, u32[]{:S(2)}, u32[]{:S(2)}) %collective-permute-start.24) | collective-permute-done | bytes 524320 | tf_op jit(solution)/shard_map/ppermute | solution.py:394
  39.4 1.3 collective-permute-start.3
  40.7 0.0 collective-permute-done.25.refs_3_
  40.7 0.7 collective-permute-start.13
  41.5 1.3 collective-permute-start.26
  42.8 0.5 collective-permute-done.20.refs_4_
  43.2 1.3 collective-permute-start.30
  44.5 0.7 collective-permute-start.27
  45.2 10.9 %collective-permute-done.3.refs_5_.refs_10_.refs_2_ = bf16[2,128,1024]{2,1,0:T(8,128)(2,1)S(1)} collective-permute-done((bf16[2,128,1024]{2,1,0:T(8,128)(2,1)S(1)}, bf16[2,128,1024]{2,1,0:T(8,128)(2,1)S(1)}, u32[]{:S(2)}, u32[]{:S(2)}) %collective-permute-start.3) | collective-permute-done | bytes 524320 | tf_op jit(solution)/shard_map/ppermute | solution.py:394
  56.1 1.3 collective-permute-start.6
  57.4 0.7 collective-permute-start.14
  58.1 0.1 fusion
  58.2 7.8 %collective-permute-done.26.refs_4_.refs_9_ = bf16[2,128,1024]{2,1,0:T(8,128)(2,1)S(1)} collective-permute-done((bf16[2,128,1024]{2,1,0:T(8,128)(2,1)S(1)}, bf16[2,128,1024]{2,1,0:T(8,128)(2,1)S(1)}, u32[]{:S(2)}, u32[]{:S(2)}) %collective-permute-start.26) | collective-permute-done | bytes 524320 | tf_op jit(solution)/shard_map/ppermute | solution.py:394
  66.0 2.5 %collective-permute-start.29 = (bf16[2,128,1024]{2,1,0:T(8,128)(2,1)S(1)}, bf16[2,128,1024]{2,1,0:T(8,128)(2,1)S(1)}, u32[]{:S(2)}, u32[]{:S(2)}) collective-permute-start(bf16[2,128,1024]{2,1,0:T(8,128)(2,1)S(1)} %get-tuple-element.17), channel_id=1, source_target_pairs={{0,2},{1,3},{8,10},{9,11},{22,20},{23,21},{30,28},{31,29}} | collective-permute-start | bytes 1572872 | tf_op jit(solution)/shard_map/ppermute | solution.py:394
  68.6 1.3 collective-permute-start.8
  69.9 0.7 collective-permute-start.28
  70.6 1.7 %collective-permute-done.6 = bf16[2,128,1024]{2,1,0:T(8,128)(2,1)S(1)} collective-permute-done((bf16[2,128,1024]{2,1,0:T(8,128)(2,1)S(1)}, bf16[2,128,1024]{2,1,0:T(8,128)(2,1)S(1)}, u32[]{:S(2)}, u32[]{:S(2)}) %collective-permute-start.6) | collective-permute-done | bytes 524320 | tf_op jit(solution)/shard_map/ppermute | solution.py:394
  72.3 0.7 collective-permute-start.4
  73.0 4.7 %collective-permute-done.8 = bf16[1,128,1024]{2,1,0:T(8,128)(2,1)S(1)} collective-permute-done((bf16[1,128,1024]{2,1,0:T(8,128)(2,1)S(1)}, bf16[1,128,1024]{2,1,0:T(8,128)(2,1)S(1)}, u32[]{:S(2)}, u32[]{:S(2)}) %collective-permute-start.8) | collective-permute-done | bytes 262176 | tf_op jit(solution)/shard_map/ppermute | solution.py:394
  77.7 0.0 copy-start.6
  77.7 1.6 %collective-permute-start.1 = (bf16[2,128,1024]{2,1,0:T(8,128)(2,1)S(1)}, bf16[2,128,1024]{2,1,0:T(8,128)(2,1)S(1)}, u32[]{:S(2)}, u32[]{:S(2)}) collective-permute-start(bf16[2,128,1024]{2,1,0:T(8,128)(2,1)S(1)} %get-tuple-element.18), channel_id=1, source_target_pairs={{0,2},{1,3},{2,4},{3,5},{8,10},{9,11},{10,12},{11,13},{20,18},{21,... | collective-permute-start | bytes 1572872 | tf_op jit(solution)/shard_map/ppermute | solution.py:394
  79.4 1.6 %collective-permute-start.22 = (bf16[4,128,1024]{2,1,0:T(8,128)(2,1)S(1)}, bf16[4,128,1024]{2,1,0:T(8,128)(2,1)S(1)}, u32[]{:S(2)}, u32[]{:S(2)}) collective-permute-start(bf16[4,128,1024]{2,1,0:T(8,128)(2,1)S(1)} %collective-permute-done.refs_8_.refs_2_.refs_7_.refs_0_), channel_id=1, source_target_pairs={{0,1},{1,0},{2,3},{3,2},{4,5},{5,4},{6,7},{7,6},{8,9},{9,8},{10,11... | collective-permute-start | bytes 3145736 | tf_op jit(solution)/shard_map/ppermute | solution.py:394
  81.0 5.1 %collective-permute-start.7 = (bf16[2,128,1024]{2,1,0:T(8,128)(2,1)S(1)}, bf16[2,128,1024]{2,1,0:T(8,128)(2,1)S(1)}, u32[]{:S(2)}, u32[]{:S(2)}) collective-permute-start(bf16[2,128,1024]{2,1,0:T(8,128)(2,1)S(1)} %collective-permute-done.6), channel_id=1, source_target_pairs={{0,16},{1,17},{8,24},{9,25},{22,6},{23,7},{30,14},{31,15}} | collective-permute-start | bytes 1572872 | tf_op jit(solution)/shard_map/ppermute | solution.py:394
  86.0 0.1 collective-permute-start.19
  86.1 0.5 collective-permute-start.21
  86.6 3.5 %collective-permute-done.1.refs_9_.refs_11_.refs_1_.refs_3_ = bf16[2,128,1024]{2,1,0:T(8,128)(2,1)S(1)} collective-permute-done((bf16[2,128,1024]{2,1,0:T(8,128)(2,1)S(1)}, bf16[2,128,1024]{2,1,0:T(8,128)(2,1)S(1)}, u32[]{:S(2)}, u32[]{:S(2)}) %collective-permute-start.1) | collective-permute-done | bytes 524320 | tf_op jit(solution)/shard_map/ppermute | solution.py:394
  90.1 4.5 %collective-permute-start.31 = (bf16[2,128,1024]{2,1,0:T(8,128)(2,1)S(1)}, bf16[2,128,1024]{2,1,0:T(8,128)(2,1)S(1)}, u32[]{:S(2)}, u32[]{:S(2)}) collective-permute-start(bf16[2,128,1024]{2,1,0:T(8,128)(2,1)S(1)} %collective-permute-done.30), channel_id=1, source_target_pairs={{0,16},{1,17},{8,24},{9,25},{22,6},{23,7},{30,14},{31,15}} | collective-permute-start | bytes 1572872 | tf_op jit(solution)/shard_map/ppermute | solution.py:394
  94.7 1.3 collective-permute-start.32
  96.0 0.2 shard_map.73
  96.1 9.8 %collective-permute-done.31.refs_12_.refs_13_ = bf16[2,128,1024]{2,1,0:T(8,128)(2,1)S(1)} collective-permute-done((bf16[2,128,1024]{2,1,0:T(8,128)(2,1)S(1)}, bf16[2,128,1024]{2,1,0:T(8,128)(2,1)S(1)}, u32[]{:S(2)}, u32[]{:S(2)}) %collective-permute-start.31) | collective-permute-done | bytes 524320 | tf_op jit(solution)/shard_map/ppermute | solution.py:394
  106.0 0.5 collective-permute-start.23
  106.5 0.1 shard_map.75
  106.6 3.5 %collective-permute-done.32 = bf16[2,128,1024]{2,1,0:T(8,128)(2,1)S(1)} collective-permute-done((bf16[2,128,1024]{2,1,0:T(8,128)(2,1)S(1)}, bf16[2,128,1024]{2,1,0:T(8,128)(2,1)S(1)}, u32[]{:S(2)}, u32[]{:S(2)}) %collective-permute-start.32) | collective-permute-done | bytes 524320 | tf_op jit(solution)/shard_map/ppermute | solution.py:394
  110.1 0.7 collective-permute-start.33
  110.8 1.7 %collective-permute-start.35 = (bf16[2,128,1024]{2,1,0:T(8,128)(2,1)S(1)}, bf16[2,128,1024]{2,1,0:T(8,128)(2,1)S(1)}, u32[]{:S(2)}, u32[]{:S(2)}) collective-permute-start(bf16[2,128,1024]{2,1,0:T(8,128)(2,1)S(1)} %collective-permute-done.32), channel_id=1, source_target_pairs={{0,24},{1,25},{30,6},{31,7}} | collective-permute-start | bytes 1572872 | tf_op jit(solution)/shard_map/ppermute | solution.py:394
  112.5 13.6 %collective-permute-start.16 = (bf16[1,128,1024]{2,1,0:T(8,128)(2,1)S(1)}, bf16[1,128,1024]{2,1,0:T(8,128)(2,1)S(1)}, u32[]{:S(2)}, u32[]{:S(2)}) collective-permute-start(bf16[1,128,1024]{2,1,0:T(8,128)(2,1)S(1)} %collective-permute-done.8), channel_id=1, source_target_pairs={{0,24},{1,25},{30,6},{31,7}} | collective-permute-start | bytes 786440 | tf_op jit(solution)/shard_map/ppermute | solution.py:394
  126.1 0.7 collective-permute-start.9
  126.8 0.7 collective-permute-start.10
  127.5 0.7 collective-permute-start.17
  128.3 1.4 prep.1
  129.7 1.4 shard_map.74.refs_8_.refs_1_.refs_11_
  131.1 1.4 shard_map.76.refs_16_
  132.6 0.9 shard_map.77.own
  133.5 0.8 shard_map.78.given
  134.3 3.4 %occ_tiles.1.occ_ref.refs_13_ = f32[8,2,256,256]{3,2,1,0:T(8,128)S(1)} custom-call(bf16[2,128,1024]{2,1,0:T(8,128)(2,1)S(1)} %flatten_occ.1.occ_flat_ref.refs_0_, bf16[2,128,1024]{2,1,0:T(8,128)(2,1)S(1)} %collective-permute-done.24.refs_1_.refs_2_, bf16[2,128,1024]{2,1,0:T(8,128)(2,1)S(1)} %collective-permute-done.24.refs_1_.refs_2_, ...), custom_call_target="tpu_custom_call" | custom-call | tf_op jit(solution)/shard_map/occ_tiles/pallas_call | solution.py:565
  137.7 1.3 direct_sums.1.refs_14_
  139.0 4.5 %closing.1 = f32[2,2,128,2,256]{4,3,2,1,0:T(2,128)} custom-call(bf16[4,128,1024]{2,1,0:T(8,128)(2,1)S(1)} %collective-permute-done.refs_8_.refs_2_.refs_7_.refs_0_, bf16[2,128,1024]{2,1,0:T(8,128)(2,1)S(1)} %collective-permute-done.1.refs_9_.refs_11_.refs_1_.refs_3_, bf16[2,128,1024]{2,1,0:T(8,128)(2,1)S(1)} %collective-permute-done.3.refs_5_.refs_10_.refs_2_, ...), custom_call_target="tpu_custom_call" | custom-call | tf_op jit(solution)/shard_map/closing/pallas_call | solution.py:587
  (37 shorter events, 0.1 us)
Async XLA Ops:
  0.0 1.0 copy-start
  1.2 1.0 copy-start.1
  2.4 22.7 %collective-permute-start.2 = (bf16[2,128,1024]{2,1,0:T(8,128)(2,1)S(1)}, bf16[2,128,1024]{2,1,0:T(8,128)(2,1)S(1)}, u32[]{:S(2)}, u32[]{:S(2)}) collective-permute-start(bf16[2,128,1024]{2,1,0:T(8,128)(2,1)S(1)} %get-tuple-element.12.refs_0_), channel_id=1, source_target_pairs={{0,2},{1,3},{4,6},{5,7},{6,4},{7,5},{8,10},{9,11},{12,14},{13,15},... | collective-permute-start | bytes 1572872 | tf_op jit(solution)/shard_map/ppermute | solution.py:394
  7.4 17.7 %collective-permute-start.5 = (bf16[2,128,1024]{2,1,0:T(8,128)(2,1)S(1)}, bf16[2,128,1024]{2,1,0:T(8,128)(2,1)S(1)}, u32[]{:S(2)}, u32[]{:S(2)}) collective-permute-start(bf16[2,128,1024]{2,1,0:T(8,128)(2,1)S(1)} %get-tuple-element.12.refs_0_), channel_id=1, source_target_pairs={{2,4},{3,5},{4,2},{5,3},{10,12},{11,13},{12,10},{13,11},{18,20},{1... | collective-permute-start | bytes 1572872 | tf_op jit(solution)/shard_map/ppermute | solution.py:394
  8.1 12.8 %collective-permute-start.11 = (bf16[1,128,1024]{2,1,0:T(8,128)(2,1)S(1)}, bf16[1,128,1024]{2,1,0:T(8,128)(2,1)S(1)}, u32[]{:S(2)}, u32[]{:S(2)}) collective-permute-start(bf16[1,128,1024]{2,1,0:T(8,128)(2,1)S(1)} %get-tuple-element.13), channel_id=1, source_target_pairs={{2,0},{3,1},{10,8},{11,9},{20,22},{21,23},{28,30},{29,31}} | collective-permute-start | bytes 786440 | tf_op jit(solution)/shard_map/ppermute | solution.py:394
  9.4 15.7 %collective-permute-start.12 = (bf16[1,128,1024]{2,1,0:T(8,128)(2,1)S(1)}, bf16[1,128,1024]{2,1,0:T(8,128)(2,1)S(1)}, u32[]{:S(2)}, u32[]{:S(2)}) collective-permute-start(bf16[1,128,1024]{2,1,0:T(8,128)(2,1)S(1)} %get-tuple-element.14), channel_id=1, source_target_pairs={{2,0},{3,1},{10,8},{11,9},{20,22},{21,23},{28,30},{29,31}} | collective-permute-start | bytes 786440 | tf_op jit(solution)/shard_map/ppermute | solution.py:394
  10.7 30.7 %collective-permute-start = (bf16[4,128,1024]{2,1,0:T(8,128)(2,1)S(1)}, bf16[4,128,1024]{2,1,0:T(8,128)(2,1)S(1)}, u32[]{:S(2)}, u32[]{:S(2)}) collective-permute-start(bf16[4,128,1024]{2,1,0:T(8,128)(2,1)S(1)} %get-tuple-element.11), channel_id=1, source_target_pairs={{0,16},{1,17},{2,18},{3,19},{4,20},{5,21},{6,22},{7,23},{8,24},{9,... | collective-permute-start | bytes 3145736 | tf_op jit(solution)/shard_map/ppermute | solution.py:394
  20.9 22.4 %collective-permute-start.20 = (bf16[4,128,1024]{2,1,0:T(8,128)(2,1)S(1)}, bf16[4,128,1024]{2,1,0:T(8,128)(2,1)S(1)}, u32[]{:S(2)}, u32[]{:S(2)}) collective-permute-start(bf16[4,128,1024]{2,1,0:T(8,128)(2,1)S(1)} %get-tuple-element.11), channel_id=1, source_target_pairs={{0,1},{1,0},{2,3},{3,2},{4,5},{5,4},{6,7},{7,6},{8,9},{9,8},{10,11... | collective-permute-start | bytes 3145736 | tf_op jit(solution)/shard_map/ppermute | solution.py:394
  25.1 19.4 %collective-permute-start.18 = (bf16[4,128,1024]{2,1,0:T(8,128)(2,1)S(1)}, bf16[4,128,1024]{2,1,0:T(8,128)(2,1)S(1)}, u32[]{:S(2)}, u32[]{:S(2)}) collective-permute-start(bf16[4,128,1024]{2,1,0:T(8,128)(2,1)S(1)} %get-tuple-element.11), channel_id=1, source_target_pairs={{0,8},{1,9},{2,10},{3,11},{4,12},{5,13},{6,14},{7,15},{8,0},{9,1},... | collective-permute-start | bytes 3145736 | tf_op jit(solution)/shard_map/ppermute | solution.py:394
  25.1 14.3 %collective-permute-start.24 = (bf16[2,128,1024]{2,1,0:T(8,128)(2,1)S(1)}, bf16[2,128,1024]{2,1,0:T(8,128)(2,1)S(1)}, u32[]{:S(2)}, u32[]{:S(2)}) collective-permute-start(bf16[2,128,1024]{2,1,0:T(8,128)(2,1)S(1)} %flatten_occ.1.occ_flat_ref.refs_0_), channel_id=1, source_target_pairs={{0,2},{1,3},{2,0},{3,1},{4,6},{5,7},{6,4},{7,5},{8,10},{9,11},{10,... | collective-permute-start | bytes 1572872 | tf_op jit(solution)/shard_map/ppermute | solution.py:394
  25.1 15.6 %collective-permute-start.25 = (bf16[2,128,1024]{2,1,0:T(8,128)(2,1)S(1)}, bf16[2,128,1024]{2,1,0:T(8,128)(2,1)S(1)}, u32[]{:S(2)}, u32[]{:S(2)}) collective-permute-start(bf16[2,128,1024]{2,1,0:T(8,128)(2,1)S(1)} %flatten_occ.1.occ_flat_ref.refs_0_), channel_id=1, source_target_pairs={{2,4},{3,5},{4,2},{5,3},{10,12},{11,13},{12,10},{13,11},{18,20},{1... | collective-permute-start | bytes 1572872 | tf_op jit(solution)/shard_map/ppermute | solution.py:394
  39.4 16.7 %collective-permute-start.3 = (bf16[2,128,1024]{2,1,0:T(8,128)(2,1)S(1)}, bf16[2,128,1024]{2,1,0:T(8,128)(2,1)S(1)}, u32[]{:S(2)}, u32[]{:S(2)}) collective-permute-start(bf16[2,128,1024]{2,1,0:T(8,128)(2,1)S(1)} %collective-permute-done.2.refs_1_), channel_id=1, source_target_pairs={{2,4},{3,5},{4,2},{5,3},{6,22},{7,23},{10,12},{11,13},{12,10},{13,... | collective-permute-start | bytes 1572872 | tf_op jit(solution)/shard_map/ppermute | solution.py:394
  40.7 16.7 %collective-permute-start.13 = (bf16[2,128,1024]{2,1,0:T(8,128)(2,1)S(1)}, bf16[2,128,1024]{2,1,0:T(8,128)(2,1)S(1)}, u32[]{:S(2)}, u32[]{:S(2)}) collective-permute-start(bf16[2,128,1024]{2,1,0:T(8,128)(2,1)S(1)} %collective-permute-done.5.refs_4_), channel_id=1, source_target_pairs={{4,6},{5,7},{12,14},{13,15},{18,16},{19,17},{26,24},{27,25}} | collective-permute-start | bytes 1572872 | tf_op jit(solution)/shard_map/ppermute | solution.py:394
  41.5 24.6 %collective-permute-start.26 = (bf16[2,128,1024]{2,1,0:T(8,128)(2,1)S(1)}, bf16[2,128,1024]{2,1,0:T(8,128)(2,1)S(1)}, u32[]{:S(2)}, u32[]{:S(2)}) collective-permute-start(bf16[2,128,1024]{2,1,0:T(8,128)(2,1)S(1)} %collective-permute-done.24.refs_1_.refs_2_), channel_id=1, source_target_pairs={{2,4},{3,5},{4,2},{5,3},{6,22},{7,23},{10,12},{11,13},{12,10},{13,... | collective-permute-start | bytes 1572872 | tf_op jit(solution)/shard_map/ppermute | solution.py:394
  43.2 25.3 %collective-permute-start.30 = (bf16[2,128,1024]{2,1,0:T(8,128)(2,1)S(1)}, bf16[2,128,1024]{2,1,0:T(8,128)(2,1)S(1)}, u32[]{:S(2)}, u32[]{:S(2)}) collective-permute-start(bf16[2,128,1024]{2,1,0:T(8,128)(2,1)S(1)} %collective-permute-done.25.refs_3_), channel_id=1, source_target_pairs={{2,0},{3,1},{10,8},{11,9},{20,22},{21,23},{28,30},{29,31}} | collective-permute-start | bytes 1572872 | tf_op jit(solution)/shard_map/ppermute | solution.py:394
  44.5 25.3 %collective-permute-start.27 = (bf16[2,128,1024]{2,1,0:T(8,128)(2,1)S(1)}, bf16[2,128,1024]{2,1,0:T(8,128)(2,1)S(1)}, u32[]{:S(2)}, u32[]{:S(2)}) collective-permute-start(bf16[2,128,1024]{2,1,0:T(8,128)(2,1)S(1)} %collective-permute-done.25.refs_3_), channel_id=1, source_target_pairs={{2,18},{3,19},{4,6},{5,7},{10,26},{11,27},{12,14},{13,15},{18,16},... | collective-permute-start | bytes 1572872 | tf_op jit(solution)/shard_map/ppermute | solution.py:394
  56.1 16.2 %collective-permute-start.6 = (bf16[2,128,1024]{2,1,0:T(8,128)(2,1)S(1)}, bf16[2,128,1024]{2,1,0:T(8,128)(2,1)S(1)}, u32[]{:S(2)}, u32[]{:S(2)}) collective-permute-start(bf16[2,128,1024]{2,1,0:T(8,128)(2,1)S(1)} %collective-permute-done.5.refs_4_), channel_id=1, source_target_pairs={{2,0},{3,1},{10,8},{11,9},{20,22},{21,23},{28,30},{29,31}} | collective-permute-start | bytes 1572872 | tf_op jit(solution)/shard_map/ppermute | solution.py:394
  57.4 22.0 %collective-permute-start.14 = (bf16[2,128,1024]{2,1,0:T(8,128)(2,1)S(1)}, bf16[2,128,1024]{2,1,0:T(8,128)(2,1)S(1)}, u32[]{:S(2)}, u32[]{:S(2)}) collective-permute-start(bf16[2,128,1024]{2,1,0:T(8,128)(2,1)S(1)} %collective-permute-done.3.refs_5_.refs_10_.refs_2_), channel_id=1, source_target_pairs={{4,6},{5,7},{12,14},{13,15},{18,16},{19,17},{26,24},{27,25}} | collective-permute-start | bytes 1572872 | tf_op jit(solution)/shard_map/ppermute | solution.py:394
  66.0 14.9 %collective-permute-start.29 = (bf16[2,128,1024]{2,1,0:T(8,128)(2,1)S(1)}, bf16[2,128,1024]{2,1,0:T(8,128)(2,1)S(1)}, u32[]{:S(2)}, u32[]{:S(2)}) collective-permute-start(bf16[2,128,1024]{2,1,0:T(8,128)(2,1)S(1)} %get-tuple-element.17), channel_id=1, source_target_pairs={{0,2},{1,3},{8,10},{9,11},{22,20},{23,21},{30,28},{31,29}} | collective-permute-start | bytes 1572872 | tf_op jit(solution)/shard_map/ppermute | solution.py:394
  68.6 9.1 %collective-permute-start.8 = (bf16[1,128,1024]{2,1,0:T(8,128)(2,1)S(1)}, bf16[1,128,1024]{2,1,0:T(8,128)(2,1)S(1)}, u32[]{:S(2)}, u32[]{:S(2)}) collective-permute-start(bf16[1,128,1024]{2,1,0:T(8,128)(2,1)S(1)} %slice.17), channel_id=1, source_target_pairs={{2,0},{3,1},{10,8},{11,9},{20,22},{21,23},{28,30},{29,31}} | collective-permute-start | bytes 786440 | tf_op jit(solution)/shard_map/ppermute | solution.py:394
  69.9 16.1 %collective-permute-start.28 = (bf16[2,128,1024]{2,1,0:T(8,128)(2,1)S(1)}, bf16[2,128,1024]{2,1,0:T(8,128)(2,1)S(1)}, u32[]{:S(2)}, u32[]{:S(2)}) collective-permute-start(bf16[2,128,1024]{2,1,0:T(8,128)(2,1)S(1)} %collective-permute-done.26.refs_4_.refs_9_), channel_id=1, source_target_pairs={{2,18},{3,19},{4,6},{5,7},{10,26},{11,27},{12,14},{13,15},{18,16},... | collective-permute-start | bytes 1572872 | tf_op jit(solution)/shard_map/ppermute | solution.py:394
  72.3 13.8 %collective-permute-start.4 = (bf16[2,128,1024]{2,1,0:T(8,128)(2,1)S(1)}, bf16[2,128,1024]{2,1,0:T(8,128)(2,1)S(1)}, u32[]{:S(2)}, u32[]{:S(2)}) collective-permute-start(bf16[2,128,1024]{2,1,0:T(8,128)(2,1)S(1)} %collective-permute-done.3.refs_5_.refs_10_.refs_2_), channel_id=1, source_target_pairs={{2,18},{3,19},{10,26},{11,27},{20,4},{21,5},{28,12},{29,13}} | collective-permute-start | bytes 1572872 | tf_op jit(solution)/shard_map/ppermute | solution.py:394
  77.7 50.5 %copy-start.2 = (f32[2,8,512]{2,1,0:T(8,128)S(1)}, f32[2,8,512]{2,1,0:T(8,128)}, u32[]{:S(2)}) copy-start(f32[2,8,512]{2,1,0:T(8,128)} %levels_in.1) | copy-start | bytes 98308
  77.7 50.5 %copy-start.3 = (s32[2,8,512]{2,1,0:T(8,128)S(1)}, s32[2,8,512]{2,1,0:T(8,128)}, u32[]{:S(2)}) copy-start(s32[2,8,512]{2,1,0:T(8,128)} %rank_in.1) | copy-start | bytes 98308
  77.7 50.5 %copy-start.4 = (s32[2,8]{1,0:T(2,128)S(1)}, s32[2,8]{1,0:T(2,128)}, u32[]{:S(2)}) copy-start(s32[2,8]{1,0:T(2,128)} %map_ref.1) | copy-start | bytes 196
  77.7 50.6 %copy-start.5 = (f32[2]{0:T(128)S(1)}, f32[2]{0:T(128)}, u32[]{:S(2)}) copy-start(f32[2]{0:T(128)} %times_ref.1) | copy-start | bytes 28
  77.7 50.6 %copy-start.6 = (s32[8]{0:T(128)S(1)}, s32[8]{0:T(128)}, u32[]{:S(2)}) copy-start(s32[8]{0:T(128)} %kpoint_ref.1) | copy-start | bytes 100
  77.7 12.4 %collective-permute-start.1 = (bf16[2,128,1024]{2,1,0:T(8,128)(2,1)S(1)}, bf16[2,128,1024]{2,1,0:T(8,128)(2,1)S(1)}, u32[]{:S(2)}, u32[]{:S(2)}) collective-permute-start(bf16[2,128,1024]{2,1,0:T(8,128)(2,1)S(1)} %get-tuple-element.18), channel_id=1, source_target_pairs={{0,2},{1,3},{2,4},{3,5},{8,10},{9,11},{10,12},{11,13},{20,18},{21,... | collective-permute-start | bytes 1572872 | tf_op jit(solution)/shard_map/ppermute | solution.py:394
  79.4 26.6 %collective-permute-start.22 = (bf16[4,128,1024]{2,1,0:T(8,128)(2,1)S(1)}, bf16[4,128,1024]{2,1,0:T(8,128)(2,1)S(1)}, u32[]{:S(2)}, u32[]{:S(2)}) collective-permute-start(bf16[4,128,1024]{2,1,0:T(8,128)(2,1)S(1)} %collective-permute-done.refs_8_.refs_2_.refs_7_.refs_0_), channel_id=1, source_target_pairs={{0,1},{1,0},{2,3},{3,2},{4,5},{5,4},{6,7},{7,6},{8,9},{9,8},{10,11... | collective-permute-start | bytes 3145736 | tf_op jit(solution)/shard_map/ppermute | solution.py:394
  81.0 13.7 %collective-permute-start.7 = (bf16[2,128,1024]{2,1,0:T(8,128)(2,1)S(1)}, bf16[2,128,1024]{2,1,0:T(8,128)(2,1)S(1)}, u32[]{:S(2)}, u32[]{:S(2)}) collective-permute-start(bf16[2,128,1024]{2,1,0:T(8,128)(2,1)S(1)} %collective-permute-done.6), channel_id=1, source_target_pairs={{0,16},{1,17},{8,24},{9,25},{22,6},{23,7},{30,14},{31,15}} | collective-permute-start | bytes 1572872 | tf_op jit(solution)/shard_map/ppermute | solution.py:394
  86.0 24.1 %collective-permute-start.19 = (bf16[4,128,1024]{2,1,0:T(8,128)(2,1)S(1)}, bf16[4,128,1024]{2,1,0:T(8,128)(2,1)S(1)}, u32[]{:S(2)}, u32[]{:S(2)}) collective-permute-start(bf16[4,128,1024]{2,1,0:T(8,128)(2,1)S(1)} %collective-permute-done.refs_8_.refs_2_.refs_7_.refs_0_), channel_id=1, source_target_pairs={{0,8},{1,9},{2,10},{3,11},{4,12},{5,13},{6,14},{7,15},{8,0},{9,1},... | collective-permute-start | bytes 3145736 | tf_op jit(solution)/shard_map/ppermute | solution.py:394
  86.1 24.7 %collective-permute-start.21 = (bf16[4,128,1024]{2,1,0:T(8,128)(2,1)S(1)}, bf16[4,128,1024]{2,1,0:T(8,128)(2,1)S(1)}, u32[]{:S(2)}, u32[]{:S(2)}) collective-permute-start(bf16[4,128,1024]{2,1,0:T(8,128)(2,1)S(1)} %collective-permute-done.20.refs_4_), channel_id=1, source_target_pairs={{0,8},{1,9},{2,10},{3,11},{4,12},{5,13},{6,14},{7,15},{8,0},{9,1},... | collective-permute-start | bytes 3145736 | tf_op jit(solution)/shard_map/ppermute | solution.py:394
  90.1 15.8 %collective-permute-start.31 = (bf16[2,128,1024]{2,1,0:T(8,128)(2,1)S(1)}, bf16[2,128,1024]{2,1,0:T(8,128)(2,1)S(1)}, u32[]{:S(2)}, u32[]{:S(2)}) collective-permute-start(bf16[2,128,1024]{2,1,0:T(8,128)(2,1)S(1)} %collective-permute-done.30), channel_id=1, source_target_pairs={{0,16},{1,17},{8,24},{9,25},{22,6},{23,7},{30,14},{31,15}} | collective-permute-start | bytes 1572872 | tf_op jit(solution)/shard_map/ppermute | solution.py:394
  94.7 15.5 %collective-permute-start.32 = (bf16[2,128,1024]{2,1,0:T(8,128)(2,1)S(1)}, bf16[2,128,1024]{2,1,0:T(8,128)(2,1)S(1)}, u32[]{:S(2)}, u32[]{:S(2)}) collective-permute-start(bf16[2,128,1024]{2,1,0:T(8,128)(2,1)S(1)} %collective-permute-done.26.refs_4_.refs_9_), channel_id=1, source_target_pairs={{2,0},{3,1},{10,8},{11,9},{20,22},{21,23},{28,30},{29,31}} | collective-permute-start | bytes 1572872 | tf_op jit(solution)/shard_map/ppermute | solution.py:394
  106.0 20.9 %collective-permute-start.15 = (bf16[2,2,128,1024]{3,2,1,0:T(8,128)(2,1)S(1)}, bf16[2,2,128,1024]{3,2,1,0:T(8,128)(2,1)S(1)}, u32[]{:S(2)}, u32[]{:S(2)}) collective-permute-start(bf16[2,2,128,1024]{3,2,1,0:T(8,128)(2,1)S(1)} %shard_map.73), channel_id=1, source_target_pairs={{0,8},{1,9},{2,10},{3,11},{4,12},{5,13},{6,14},{7,15},{8,0},{9,1},... | collective-permute-start | bytes 3145736 | tf_op jit(solution)/shard_map/ppermute | solution.py:394
  106.0 21.5 %collective-permute-start.23 = (bf16[4,128,1024]{2,1,0:T(8,128)(2,1)S(1)}, bf16[4,128,1024]{2,1,0:T(8,128)(2,1)S(1)}, u32[]{:S(2)}, u32[]{:S(2)}) collective-permute-start(bf16[4,128,1024]{2,1,0:T(8,128)(2,1)S(1)} %collective-permute-done.22.refs_6_), channel_id=1, source_target_pairs={{0,8},{1,9},{2,10},{3,11},{4,12},{5,13},{6,14},{7,15},{8,0},{9,1},... | collective-permute-start | bytes 3145736 | tf_op jit(solution)/shard_map/ppermute | solution.py:394
  110.1 24.2 %collective-permute-start.34 = (bf16[2,2,128,1024]{3,2,1,0:T(8,128)(2,1)S(1)}, bf16[2,2,128,1024]{3,2,1,0:T(8,128)(2,1)S(1)}, u32[]{:S(2)}, u32[]{:S(2)}) collective-permute-start(bf16[2,2,128,1024]{3,2,1,0:T(8,128)(2,1)S(1)} %shard_map.75), channel_id=1, source_target_pairs={{0,8},{1,9},{2,10},{3,11},{4,12},{5,13},{6,14},{7,15},{8,0},{9,1},... | collective-permute-start | bytes 3145736 | tf_op jit(solution)/shard_map/ppermute | solution.py:394
  110.1 2.4 %collective-permute-start.33 = (bf16[2,128,1024]{2,1,0:T(8,128)(2,1)S(1)}, bf16[2,128,1024]{2,1,0:T(8,128)(2,1)S(1)}, u32[]{:S(2)}, u32[]{:S(2)}) collective-permute-start(bf16[2,128,1024]{2,1,0:T(8,128)(2,1)S(1)} %collective-permute-done.32), channel_id=1, source_target_pairs={{8,24},{9,25},{22,6},{23,7}} | collective-permute-start | bytes 1572872 | tf_op jit(solution)/shard_map/ppermute | solution.py:394
  110.8 15.3 %collective-permute-start.35 = (bf16[2,128,1024]{2,1,0:T(8,128)(2,1)S(1)}, bf16[2,128,1024]{2,1,0:T(8,128)(2,1)S(1)}, u32[]{:S(2)}, u32[]{:S(2)}) collective-permute-start(bf16[2,128,1024]{2,1,0:T(8,128)(2,1)S(1)} %collective-permute-done.32), channel_id=1, source_target_pairs={{0,24},{1,25},{30,6},{31,7}} | collective-permute-start | bytes 1572872 | tf_op jit(solution)/shard_map/ppermute | solution.py:394
  112.5 26.4 %collective-permute-start.16 = (bf16[1,128,1024]{2,1,0:T(8,128)(2,1)S(1)}, bf16[1,128,1024]{2,1,0:T(8,128)(2,1)S(1)}, u32[]{:S(2)}, u32[]{:S(2)}) collective-permute-start(bf16[1,128,1024]{2,1,0:T(8,128)(2,1)S(1)} %collective-permute-done.8), channel_id=1, source_target_pairs={{0,24},{1,25},{30,6},{31,7}} | collective-permute-start | bytes 786440 | tf_op jit(solution)/shard_map/ppermute | solution.py:394
  126.1 12.9 %collective-permute-start.9 = (bf16[1,128,1024]{2,1,0:T(8,128)(2,1)S(1)}, bf16[1,128,1024]{2,1,0:T(8,128)(2,1)S(1)}, u32[]{:S(2)}, u32[]{:S(2)}) collective-permute-start(bf16[1,128,1024]{2,1,0:T(8,128)(2,1)S(1)} %collective-permute-done.8), channel_id=1, source_target_pairs={{8,24},{9,25},{22,6},{23,7}} | collective-permute-start | bytes 786440 | tf_op jit(solution)/shard_map/ppermute | solution.py:394
  126.8 12.2 %collective-permute-start.10 = (bf16[1,128,1024]{2,1,0:T(8,128)(2,1)S(1)}, bf16[1,128,1024]{2,1,0:T(8,128)(2,1)S(1)}, u32[]{:S(2)}, u32[]{:S(2)}) collective-permute-start(bf16[1,128,1024]{2,1,0:T(8,128)(2,1)S(1)} %slice.18), channel_id=1, source_target_pairs={{4,6},{5,7},{26,24},{27,25}} | collective-permute-start | bytes 786440 | tf_op jit(solution)/shard_map/ppermute | solution.py:394
  127.5 11.5 %collective-permute-start.17 = (bf16[1,128,1024]{2,1,0:T(8,128)(2,1)S(1)}, bf16[1,128,1024]{2,1,0:T(8,128)(2,1)S(1)}, u32[]{:S(2)}, u32[]{:S(2)}) collective-permute-start(bf16[1,128,1024]{2,1,0:T(8,128)(2,1)S(1)} %slice.18), channel_id=1, source_target_pairs={{12,6},{13,7},{18,24},{19,25}} | collective-permute-start | bytes 786440 | tf_op jit(solution)/shard_map/ppermute | solution.py:394
